TPU v7x, 32 devices: a whole 2x2x4 slice. The times are simulated.
32 devices in a mesh: dp: 16 (over z, x, core), mp: 2 (over y).
Axes of the slice: x: 2, y: 2, z: 4, core: 2. Of those that a mesh axis runs over, the one named last changes fastest.
Arguments:
- tokens: bfloat16 [2, 16384, 768], P(None, ('dp', 'mp')), may hold values from -6 to 6
- lengths: int32 [16, 4], P('dp'), may hold values from 1 to 682, 1024 in all within a row
- block_size: int32 [1], replicated, may hold values from 4 to 16
- cotangent: bfloat16 [2, 16384, 768], P(None, ('dp', 'mp')), may hold values from -6 to 6
- ln1_gain: float32 [768], replicated, may hold values from 0.5 to 1.5
- ln1_bias: float32 [768], replicated, may hold values from -1.5 to 1.5
- w_qkv: bfloat16 [768, 3, 768], P(None, None, 'mp'), may hold values from -0.21875 to 0.21875
- w_out: bfloat16 [768, 768], P('mp'), may hold values from -0.875 to 0.875
- ln2_gain: float32 [768], replicated, may hold values from 0.5 to 1.5
- ln2_bias: float32 [768], replicated, may hold values from -1.5 to 1.5
- w_up: bfloat16 [768, 3072], P(None, 'mp'), may hold values from -0.21875 to 0.21875
- b_up: bfloat16 [3072], P('mp'), may hold values from -1.5 to 1.5
- w_down: bfloat16 [3072, 768], P('mp'), may hold values from -0.109375 to 0.109375
- b_down: float32 [768], replicated, may hold values from -1.5 to 1.5
Outputs:
- out: bfloat16 [2, 16384, 768], P(None, ('dp', 'mp'))
- grad_tokens: float32 [2, 16384, 768], P(None, ('dp', 'mp'))
- grad_ln1_gain: float32 [768], replicated
- grad_ln1_bias: float32 [768], replicated
- grad_w_qkv: float32 [768, 3, 768], P(None, None, 'mp')
- grad_w_out: float32 [768, 768], P('mp')
- grad_ln2_gain: float32 [768], replicated
- grad_ln2_bias: float32 [768], replicated
- grad_w_up: float32 [768, 3072], P(None, 'mp')
- grad_b_up: float32 [3072], P('mp')
- grad_w_down: float32 [3072, 768], P('mp')
- grad_b_down: float32 [768], replicated
Inputs may be any that keep to these rules, and one draw needn't show every extreme that they name: Each row lists the lengths of the 4 sequences packed in order into one pack of 1024 tokens; they sum to 1024 and the longest of each row is exactly 682.
All inputs are finite; a program needn't handle non-finite values.
Results may differ from a plain program's by a relative error of at most 0.011.
Values may be sent and summed in bfloat16 or wider, within the bound.
A program may use at most 256 MiB of HBM per device.

v0:
```python
import math

import jax
import jax.numpy as jnp
from jax import lax
from jax.sharding import PartitionSpec as P

HD = 64
TOK_DEV = 1024


epsilon = 1e-05
neg_large = -1e30


def layer_norm(values, norm_gain, norm_bias):
    average = jnp.mean(values, axis=-1, keepdims=True)
    centred = values - average
    variance = jnp.mean(centred * centred, axis=-1, keepdims=True)
    return centred * lax.rsqrt(variance + epsilon) * norm_gain + norm_bias


def gelu_tanh(values):
    inner = 0.7978845608028654 * (values + 0.044715 * values * values * values)
    return 0.5 * values * (1.0 + jnp.tanh(inner))


def pack_layout(seq_lengths, block_len, tokens_count):
    token_index = jnp.arange(tokens_count, dtype=jnp.int32)
    seq_ends = jnp.cumsum(seq_lengths)
    passed = token_index[:, None] >= seq_ends[None, :]
    doc_ids = jnp.sum(passed.astype(jnp.int32), axis=1)
    starts = jnp.sum(jnp.where(passed, seq_lengths[None, :], 0), axis=1)
    positions = token_index - starts
    blocks = positions // block_len
    return (doc_ids, positions, blocks)


def rotary_tables(positions, head_dim):
    half_dim = head_dim // 2
    frequency = jnp.exp(jnp.arange(half_dim, dtype=jnp.float32) * (-math.log(10000.0) / half_dim))
    angles = positions.astype(jnp.float32)[:, None] * frequency[None, :]
    return (jnp.cos(angles), jnp.sin(angles))


def rotate(field, cosine, sine):
    half_dim = field.shape[-1] // 2
    first = field[..., :half_dim]
    second = field[..., half_dim:]
    cos_rows = cosine[:, None, :]
    sin_rows = sine[:, None, :]
    return jnp.concatenate(
        [first * cos_rows - second * sin_rows, second * cos_rows + first * sin_rows], axis=-1
    )


def allowed_keys(query_noisy, query_doc, query_block, key_noisy, key_doc, key_block):
    same_doc = query_doc[:, None] == key_doc[None, :]
    key_flag = key_noisy[None, :]
    noisy_rule = jnp.where(
        key_flag,
        key_block[None, :] == query_block[:, None],
        key_block[None, :] < query_block[:, None],
    )
    clean_rule = jnp.logical_and(
        jnp.logical_not(key_flag), key_block[None, :] <= query_block[:, None]
    )
    return jnp.logical_and(same_doc, jnp.where(query_noisy[:, None], noisy_rule, clean_rule))


def block_forward(query_blk, key_set, value_set, mask):
    scores = (
        jnp.einsum("qhe,khe->hqk", query_blk, key_set, preferred_element_type=jnp.float32) * 0.125
    )
    masked = jnp.where(mask[None], scores, neg_large)
    row_top = jnp.max(masked, axis=-1, keepdims=True)
    expo = jnp.exp(masked - row_top)
    row_total = jnp.sum(expo, axis=-1, keepdims=True)
    probs = expo / row_total
    attended = jnp.einsum(
        "hqk,khe->qhe", probs.astype(jnp.bfloat16), value_set, preferred_element_type=jnp.float32
    )
    return (attended, row_top + jnp.log(row_total))


def block_backward(query_blk, key_set, value_set, mask, log_total, d_out):
    scores = (
        jnp.einsum("qhe,khe->hqk", query_blk, key_set, preferred_element_type=jnp.float32) * 0.125
    )
    masked = jnp.where(mask[None], scores, neg_large)
    probs = jnp.exp(masked - log_total)
    d_probs = jnp.einsum("qhe,khe->hqk", d_out, value_set, preferred_element_type=jnp.float32)
    inner = jnp.sum(probs * d_probs, axis=-1, keepdims=True)
    d_scores = (probs * (d_probs - inner) * 0.125).astype(jnp.bfloat16)
    d_query = jnp.einsum("hqk,khe->qhe", d_scores, key_set, preferred_element_type=jnp.float32)
    d_keys = jnp.einsum("hqk,qhe->khe", d_scores, query_blk, preferred_element_type=jnp.float32)
    d_values = jnp.einsum(
        "hqk,qhe->khe", probs.astype(jnp.bfloat16), d_out, preferred_element_type=jnp.float32
    )
    return (d_query, d_keys, d_values)


def attend_forward(
    query_rows,
    noisy_query,
    query_doc,
    query_block,
    key_set,
    value_set,
    key_noisy,
    key_doc,
    key_block,
    block_rows,
):
    count = query_rows.shape[0] // block_rows

    def one_block(item):
        query_blk, doc_blk, block_blk = item
        flags = jnp.full(doc_blk.shape, noisy_query)
        mask = allowed_keys(flags, doc_blk, block_blk, key_noisy, key_doc, key_block)
        return block_forward(query_blk, key_set, value_set, mask)

    items = (
        query_rows.reshape((count, block_rows) + query_rows.shape[1:]),
        query_doc.reshape(count, block_rows),
        query_block.reshape(count, block_rows),
    )
    return lax.map(one_block, items)


def attend_backward(
    query_rows,
    noisy_query,
    query_doc,
    query_block,
    key_set,
    value_set,
    key_noisy,
    key_doc,
    key_block,
    log_totals,
    d_out_rows,
    block_rows,
):
    count = query_rows.shape[0] // block_rows

    def one_block(carry, item):
        query_blk, doc_blk, block_blk, log_total, d_out = item
        flags = jnp.full(doc_blk.shape, noisy_query)
        mask = allowed_keys(flags, doc_blk, block_blk, key_noisy, key_doc, key_block)
        d_query, d_keys, d_values = block_backward(
            query_blk, key_set, value_set, mask, log_total, d_out
        )
        return ((carry[0] + d_keys, carry[1] + d_values), d_query)

    items = (
        query_rows.reshape((count, block_rows) + query_rows.shape[1:]),
        query_doc.reshape(count, block_rows),
        query_block.reshape(count, block_rows),
        log_totals,
        d_out_rows.reshape((count, block_rows) + d_out_rows.shape[1:]),
    )
    zeros = jnp.zeros(key_set.shape, jnp.float32)
    (d_keys, d_values), d_query = lax.scan(one_block, (zeros, zeros), items)
    return (d_query.reshape(query_rows.shape), d_keys, d_values)


def local(
    tokens,
    lengths,
    block_size,
    cotangent,
    ln1_gain,
    ln1_bias,
    w_qkv,
    w_out,
    ln2_gain,
    ln2_bias,
    w_up,
    b_up,
    w_down,
    b_down,
):
    local_rows = tokens.shape[1]
    width = tokens.shape[2]
    row_count = 2 * TOK_DEV
    heads_here = w_out.shape[0] // HD
    block_rows = min(512, TOK_DEV)
    doc_ids, positions, blocks = pack_layout(lengths[0], block_size[0], TOK_DEV)
    cosine, sine = rotary_tables(positions, HD)
    row_doc = jnp.concatenate([doc_ids, doc_ids])
    row_block = jnp.concatenate([blocks, blocks])
    row_noisy = jnp.arange(row_count, dtype=jnp.int32) < TOK_DEV
    row_cos = jnp.concatenate([cosine, cosine])
    row_sin = jnp.concatenate([sine, sine])
    x_rows = tokens.astype(jnp.float32).reshape(2 * local_rows, width)
    normed1, norm1_back = jax.vjp(layer_norm, x_rows, ln1_gain, ln1_bias)
    normed1_low = normed1.astype(jnp.bfloat16).reshape(2, local_rows, width)
    gathered1 = lax.all_gather(normed1_low, "mp", axis=1, tiled=True).reshape(row_count, width)
    qkv = jnp.einsum("rd,dcf->rcf", gathered1, w_qkv, preferred_element_type=jnp.float32)
    query = rotate(qkv[:, 0].reshape(row_count, heads_here, HD), row_cos, row_sin).astype(
        jnp.bfloat16
    )
    keys = rotate(qkv[:, 1].reshape(row_count, heads_here, HD), row_cos, row_sin).astype(
        jnp.bfloat16
    )
    values = qkv[:, 2].reshape(row_count, heads_here, HD).astype(jnp.bfloat16)
    noisy_out, noisy_lse = attend_forward(
        query[:TOK_DEV],
        True,
        doc_ids,
        blocks,
        keys,
        values,
        row_noisy,
        row_doc,
        row_block,
        block_rows,
    )
    clean_flags = jnp.zeros((TOK_DEV,), jnp.bool_)
    clean_out, clean_lse = attend_forward(
        query[TOK_DEV:],
        False,
        doc_ids,
        blocks,
        keys[TOK_DEV:],
        values[TOK_DEV:],
        clean_flags,
        doc_ids,
        blocks,
        block_rows,
    )
    attended = jnp.concatenate(
        [noisy_out.reshape(TOK_DEV, heads_here * HD), clean_out.reshape(TOK_DEV, heads_here * HD)],
        axis=0,
    ).astype(jnp.bfloat16)
    branch = jnp.dot(attended, w_out, preferred_element_type=jnp.float32).reshape(2, TOK_DEV, width)
    branch_mine = lax.psum_scatter(branch, "mp", scatter_dimension=1, tiled=True).reshape(
        2 * local_rows, width
    )
    mid = x_rows + branch_mine
    normed2, norm2_back = jax.vjp(layer_norm, mid, ln2_gain, ln2_bias)
    normed2_low = normed2.astype(jnp.bfloat16)
    up_full, up_bias_full, down_full = (w_up, b_up, w_down)
    mlp_rows = lax.all_gather(
        normed2_low.reshape(2, local_rows, width), "mp", axis=1, tiled=True
    ).reshape(row_count, width)
    pre = jnp.dot(mlp_rows, up_full, preferred_element_type=jnp.float32) + up_bias_full.astype(
        jnp.float32
    )
    act_low = gelu_tanh(pre).astype(jnp.bfloat16)
    down = jnp.dot(act_low, down_full, preferred_element_type=jnp.float32)
    down_mine = (
        lax.psum_scatter(
            down.reshape(2, TOK_DEV, width).astype(jnp.bfloat16),
            "mp",
            scatter_dimension=1,
            tiled=True,
        )
        .astype(jnp.float32)
        .reshape(2 * local_rows, width)
    )
    out_rows = mid + down_mine + b_down
    out = out_rows.astype(jnp.bfloat16).reshape(2, local_rows, width)
    d_out_rows = cotangent.astype(jnp.float32).reshape(2 * local_rows, width)
    grad_b_down = jnp.sum(d_out_rows, axis=0)
    d_down_rows = lax.all_gather(cotangent, "mp", axis=1, tiled=True).reshape(row_count, width)
    grad_down = jnp.einsum("rf,rd->fd", act_low, d_down_rows, preferred_element_type=jnp.float32)
    d_act = jnp.einsum("rd,fd->rf", d_down_rows, down_full, preferred_element_type=jnp.float32)
    d_pre = jax.vjp(gelu_tanh, pre)[1](d_act)[0].astype(jnp.bfloat16)
    grad_up_bias = jnp.sum(d_pre.astype(jnp.float32), axis=0)
    grad_up = jnp.einsum("rd,rf->df", mlp_rows, d_pre, preferred_element_type=jnp.float32)
    d_normed2 = jnp.einsum("rf,df->rd", d_pre, up_full, preferred_element_type=jnp.float32)
    d_normed2_mine = lax.psum_scatter(
        d_normed2.reshape(2, TOK_DEV, width), "mp", scatter_dimension=1, tiled=True
    ).reshape(2 * local_rows, width)
    d_mid_norm, grad_ln2_gain, grad_ln2_bias = norm2_back(d_normed2_mine)
    d_mid = d_out_rows + d_mid_norm
    d_branch_low = d_mid.astype(jnp.bfloat16).reshape(2, local_rows, width)
    d_branch_rows = lax.all_gather(d_branch_low, "mp", axis=1, tiled=True).reshape(row_count, width)
    grad_out = jnp.einsum("rf,rd->fd", attended, d_branch_rows, preferred_element_type=jnp.float32)
    d_attended = (
        jnp.einsum("rd,fd->rf", d_branch_rows, w_out, preferred_element_type=jnp.float32)
        .astype(jnp.bfloat16)
        .reshape(row_count, heads_here, HD)
    )
    d_query_noisy, d_keys_all, d_values_all = attend_backward(
        query[:TOK_DEV],
        True,
        doc_ids,
        blocks,
        keys,
        values,
        row_noisy,
        row_doc,
        row_block,
        noisy_lse,
        d_attended[:TOK_DEV],
        block_rows,
    )
    d_query_clean, d_keys_clean, d_values_clean = attend_backward(
        query[TOK_DEV:],
        False,
        doc_ids,
        blocks,
        keys[TOK_DEV:],
        values[TOK_DEV:],
        clean_flags,
        doc_ids,
        blocks,
        clean_lse,
        d_attended[TOK_DEV:],
        block_rows,
    )
    d_query = jnp.concatenate([d_query_noisy, d_query_clean], axis=0)
    d_keys = jnp.concatenate([d_keys_all[:TOK_DEV], d_keys_all[TOK_DEV:] + d_keys_clean], axis=0)
    d_values = jnp.concatenate(
        [d_values_all[:TOK_DEV], d_values_all[TOK_DEV:] + d_values_clean], axis=0
    )
    d_query_raw = rotate(d_query, row_cos, -row_sin).reshape(row_count, heads_here * HD)
    d_keys_raw = rotate(d_keys, row_cos, -row_sin).reshape(row_count, heads_here * HD)
    d_qkv = jnp.stack(
        [d_query_raw, d_keys_raw, d_values.reshape(row_count, heads_here * HD)], axis=1
    ).astype(jnp.bfloat16)
    grad_qkv = jnp.einsum("rd,rcf->dcf", gathered1, d_qkv, preferred_element_type=jnp.float32)
    d_normed1 = jnp.einsum("rcf,dcf->rd", d_qkv, w_qkv, preferred_element_type=jnp.float32).reshape(
        2, TOK_DEV, width
    )
    d_normed1_mine = lax.psum_scatter(d_normed1, "mp", scatter_dimension=1, tiled=True).reshape(
        2 * local_rows, width
    )
    d_x_norm, grad_ln1_gain, grad_ln1_bias = norm1_back(d_normed1_mine)
    grad_tokens = (d_mid + d_x_norm).reshape(2, local_rows, width)
    grad_qkv, grad_out, grad_up, grad_up_bias, grad_down = lax.psum(
        (grad_qkv, grad_out, grad_up, grad_up_bias, grad_down), "dp"
    )
    grad_ln1_gain, grad_ln1_bias, grad_ln2_gain, grad_ln2_bias, grad_b_down = lax.psum(
        (grad_ln1_gain, grad_ln1_bias, grad_ln2_gain, grad_ln2_bias, grad_b_down), ("dp", "mp")
    )
    return (
        out,
        grad_tokens,
        grad_ln1_gain,
        grad_ln1_bias,
        grad_qkv,
        grad_out,
        grad_ln2_gain,
        grad_ln2_bias,
        grad_up,
        grad_up_bias,
        grad_down,
        grad_b_down,
    )


def solution(mesh):
    in_specs = (
        P(None, ("dp", "mp"), None),
        P("dp", None),
        P(),
        P(None, ("dp", "mp"), None),
        P(),
        P(),
        P(None, None, "mp"),
        P("mp", None),
        P(),
        P(),
        P(None, "mp"),
        P("mp"),
        P("mp", None),
        P(),
    )
    out_specs = (
        P(None, ("dp", "mp"), None),
        P(None, ("dp", "mp"), None),
        P(),
        P(),
        P(None, None, "mp"),
        P("mp", None),
        P(),
        P(),
        P(None, "mp"),
        P("mp"),
        P("mp", None),
        P(),
    )
    return jax.shard_map(local, mesh=mesh, in_specs=in_specs, out_specs=out_specs, check_vma=False)
```

profile of v0, /device:TPU:0, one launch (start us, length us, event | category | flops | bytes accessed | tf_op | source)
XLA Modules:
  0.0 1462.9 jit_solution(6704899134425501747)
XLA Ops:
  16.9 45.1 %all-gather.5.cloned.1.call-done = bf16[2,1024,768]{2,1,0:T(8,128)(2,1)} async-done(((bf16[2,512,768]{2,1,0:T(8,128)(2,1)}), bf16[2,1024,768]{2,1,0:T(8,128)(2,1)}) %all-gather.5.cloned.1.call-update) | async-done | bytes 3145744 | tf_op jit(solution)/shard_map/all_gather | solution.py:199
  62.0 6.5 fusion.191
  77.0 36.8 %while.55 = (s32[]{:T(128)}, bf16[2,512,6,64]{1,3,2,0:T(8,128)(2,1)}, f32[2,6,512,1]{2,1,3,0:T(8,128)S(1)}, s32[2,512]{1,0:T(2,128)S(1)}, s32[1024]{0:T(1024)S(1...) while((s32[]{:T(128)}, ...), condition=%wide.region_12.13_spmd, body=%wide.region_9.12_spmd.sunk | while | flops 844624896 | bytes 52175064 | solution.py:128
  91.9 3.6 fusion.268
  95.6 4.4 fusion.269
  101.4 3.4 fusion.267
  104.8 3.6 fusion.268
  108.5 4.4 fusion.269
  114.9 81.3 %while.56 = (s32[]{:T(128)}, bf16[2,512,6,64]{1,3,2,0:T(8,128)(2,1)}, f32[2,6,512,1]{2,1,3,0:T(8,128)S(1)}, s32[2,512]{1,0:T(2,128)S(1)}, s32[2048]{0:T(1024)S(1...) while((s32[]{:T(128)}, ...), condition=%wide.region_8.9_spmd.clone, body=%wide.region_5.8_spmd.clone.sunk | while | flops 1691352064 | bytes 96751840 | solution.py:128
  116.5 14.3 fusion.272
  130.7 12.1 fusion.273
  142.9 11.6 fusion.274
  156.9 14.3 fusion.272
  171.2 12.1 fusion.273
  183.3 11.6 fusion.274
  199.5 4.5 fusion.192
  204.1 77.2 %reduce-scatter.5.cloned.1.call-done = f32[2,512,768]{2,1,0:T(8,128)} async-done(((f32[2,1024,768]{2,1,0:T(8,128)}), f32[2,512,768]{2,1,0:T(8,128)}) %reduce-scatter.5.cloned.1.call-update) | async-done | bytes 3145744 | tf_op jit(solution)/shard_map/reduce_scatter | solution.py:238
  288.1 44.4 %all-gather.7.cloned.1.call-done = bf16[2,1024,768]{2,1,0:T(8,128)(2,1)} async-done(((bf16[2,512,768]{2,1,0:T(8,128)(2,1)}), bf16[2,1024,768]{2,1,0:T(8,128)(2,1)}) %all-gather.7.cloned.1.call-update) | async-done | bytes 3145744 | tf_op jit(solution)/shard_map/all_gather | solution.py:245
  332.5 13.4 fusion.159
  345.9 33.1 %all-gather.9.cloned.1.call-done = bf16[2,1024,768]{2,1,0:T(8,128)(2,1)} async-done(((bf16[2,512,768]{2,1,0:T(8,128)(2,1)}), bf16[2,1024,768]{2,1,0:T(8,128)(2,1)}) %all-gather.9.cloned.1.call-update) | async-done | bytes 3145744 | tf_op jit(solution)/shard_map/all_gather | solution.py:267
  378.9 19.4 %convert_reduce_fusion = (f32[1536]{0:T(1024)}, bf16[2048,1536]{1,0:T(8,128)(2,1)S(1)}) fusion(f32[2048,1536]{1,0:T(8,128)} %get-tuple-element.680, f32[1536]{0:T(1024)S(1)} %convert_element_type.88, bf16[2048,768]{1,0:T(8,128)(2,1)} %bitcast.277, bf16[1536,768]{1,0:T(8,128)(2,1)} %param.34), kind=kOutput, calls=%fused_computation.144 | convolution fusion | flops 4916771328 | bytes 24391680 | tf_op jit(solution)/shard_map/rd,fd->rf/dot_general | solution.py:269
  398.4 7.0 fusion.193
  407.0 9.2 convolution_convert_fusion
  416.3 66.3 %reduce-scatter.9.cloned.1.call-done = f32[2,512,768]{2,1,0:T(8,128)} async-done(((f32[2,1024,768]{2,1,0:T(8,128)}), f32[2,512,768]{2,1,0:T(8,128)}) %reduce-scatter.9.cloned.1.call-update) | async-done | bytes 3145744 | tf_op jit(solution)/shard_map/reduce_scatter | solution.py:274
  482.6 4.2 multiply_reduce_fusion.2
  486.8 41.8 %reduce-scatter.7.cloned.1.call-done = bf16[2,512,768]{2,1,0:T(8,128)(2,1)} async-done(((bf16[2,1024,768]{2,1,0:T(8,128)(2,1)}), bf16[2,512,768]{2,1,0:T(8,128)(2,1)}) %reduce-scatter.7.cloned.1.call-update) | async-done | bytes 1572880 | tf_op jit(solution)/shard_map/reduce_scatter | solution.py:254
  528.6 4.9 fusion.186
  536.9 45.0 %all-gather.11.cloned.1.call-done = bf16[2,1024,768]{2,1,0:T(8,128)(2,1)} async-done(((bf16[2,512,768]{2,1,0:T(8,128)(2,1)}), bf16[2,1024,768]{2,1,0:T(8,128)(2,1)}) %all-gather.11.cloned.1.call-update) | async-done | bytes 3145744 | tf_op jit(solution)/shard_map/all_gather | solution.py:280
  581.9 3.7 convolution_convert_fusion.1
  593.7 292.0 %while.57 = (s32[]{:T(128)}, f32[2048,6,64]{0,2,1:T(8,128)}, f32[2048,6,64]{0,2,1:T(8,128)}, f32[2,512,6,64]{1,0,3,2:T(2,128)}, bf16[2,512,6,64]{1,3,2,0:T(8,128...) while((s32[]{:T(128)}, f32[2048,6,64]{0,2,1:T(8,128)}, ...), condition=%wide.region_22.23_spmd.clone, body=%wide.region_20.22_spmd.clone.sunk | while | flops 4198510592 | bytes 290308384 | solution.py:164
  595.6 10.1 fusion.286
  605.7 11.9 bitcast_add_fusion.9
  619.3 11.1 fusion.285
  630.4 45.5 %fusion.287 = f32[1,512,6,64]{1,3,2,0:T(8,128)} fusion(bf16[2048,6,64]{0,2,1:T(8,128)(2,1)S(1)} %get-tuple-element.1140, f32[6,512,2048]{2,1,0:T(8,128)} %fusion.285, f32[6,512,2048]{2,1,0:T(8,128)} %fusion.286, f32[6,512]{1,0:T(8,128)S(1)} %dynamic-slice_bitcast_fusion.4, pred[512,2048]{1,0:T(8,128)(4,1)} %copy-done.18), kind=kOutput, calls=%fused_computation.60.clone.1 | convolution fusion | flops 874517504 | bytes 53751808 | tf_op jit(solution)/shard_map/while/body/eval_jaxpr/hqk,khe->qhe/dot_general | solution.py:95
  675.9 47.0 %bitcast_add_fusion.8 = f32[2048,6,64]{0,2,1:T(8,128)} fusion(f32[2048,6,64]{0,2,1:T(8,128)} %get-tuple-element.1117, f32[6,512,2048]{2,1,0:T(8,128)} %fusion.285, f32[6,512,2048]{2,1,0:T(8,128)} %fusion.286, f32[6,512]{1,0:T(8,128)S(1)} %dynamic-slice_bitcast_fusion.4, pred[512,2048]{1,0:T(8,128)(4,1)} %copy-done.18, pred[]{:T(512)S(6)} %compare.6, ...), kind=kOutput, calls=%fused_computation.59.clone.1 | convolution fusion | flops 876090368 | bytes 109477896 | tf_op jit(solution)/shard_map/while/body/eval_jaxpr/hqk,qhe->khe/dot_general | solution.py:96
  724.9 14.9 %dynamic_update_slice.38 = f32[2,512,6,64]{1,0,3,2:T(2,128)} dynamic-update-slice(f32[2,512,6,64]{1,0,3,2:T(2,128)} %get-tuple-element.1119, f32[1,512,6,64]{1,0,3,2:T(1,128)S(1)} %copy.103, s32[]{:T(128)S(6)} %copy.146, s32[]{:T(128)} %constant.113.clone.1..sunk, s32[]{:T(128)} %constant.113.clone.1..sunk, s32[]{:T(128)} %constant.113.clone.1..sunk) | dynamic-update-slice | bytes 1572868 | tf_op jit(solution)/shard_map/while/body/jit(dynamic_update_index_in_dim)/dynamic_update_slice | solution.py:128
  741.4 10.1 fusion.286
  751.5 11.9 bitcast_add_fusion.9
  765.0 11.1 fusion.285
  776.1 45.5 %fusion.287 = f32[1,512,6,64]{1,3,2,0:T(8,128)} fusion(bf16[2048,6,64]{0,2,1:T(8,128)(2,1)S(1)} %get-tuple-element.1140, f32[6,512,2048]{2,1,0:T(8,128)} %fusion.285, f32[6,512,2048]{2,1,0:T(8,128)} %fusion.286, f32[6,512]{1,0:T(8,128)S(1)} %dynamic-slice_bitcast_fusion.4, pred[512,2048]{1,0:T(8,128)(4,1)} %copy-done.18), kind=kOutput, calls=%fused_computation.60.clone.1 | convolution fusion | flops 874517504 | bytes 53751808 | tf_op jit(solution)/shard_map/while/body/eval_jaxpr/hqk,khe->qhe/dot_general | solution.py:95
  821.6 47.0 %bitcast_add_fusion.8 = f32[2048,6,64]{0,2,1:T(8,128)} fusion(f32[2048,6,64]{0,2,1:T(8,128)} %get-tuple-element.1117, f32[6,512,2048]{2,1,0:T(8,128)} %fusion.285, f32[6,512,2048]{2,1,0:T(8,128)} %fusion.286, f32[6,512]{1,0:T(8,128)S(1)} %dynamic-slice_bitcast_fusion.4, pred[512,2048]{1,0:T(8,128)(4,1)} %copy-done.18, pred[]{:T(512)S(6)} %compare.6, ...), kind=kOutput, calls=%fused_computation.59.clone.1 | convolution fusion | flops 876090368 | bytes 109477896 | tf_op jit(solution)/shard_map/while/body/eval_jaxpr/hqk,qhe->khe/dot_general | solution.py:96
  870.6 14.9 %dynamic_update_slice.38 = f32[2,512,6,64]{1,0,3,2:T(2,128)} dynamic-update-slice(f32[2,512,6,64]{1,0,3,2:T(2,128)} %get-tuple-element.1119, f32[1,512,6,64]{1,0,3,2:T(1,128)S(1)} %copy.103, s32[]{:T(128)S(6)} %copy.146, s32[]{:T(128)} %constant.113.clone.1..sunk, s32[]{:T(128)} %constant.113.clone.1..sunk, s32[]{:T(128)} %constant.113.clone.1..sunk) | dynamic-update-slice | bytes 1572868 | tf_op jit(solution)/shard_map/while/body/jit(dynamic_update_index_in_dim)/dynamic_update_slice | solution.py:128
  885.7 3.4 reshape.931
  898.3 175.3 %while.58 = (s32[]{:T(128)}, f32[1024,6,64]{0,2,1:T(8,128)}, f32[1024,6,64]{0,2,1:T(8,128)}, f32[2,512,6,64]{1,0,3,2:T(2,128)}, bf16[2,512,6,64]{1,3,2,0:T(8,128...) while((s32[]{:T(128)}, f32[1024,6,64]{0,2,1:T(8,128)}, ...), condition=%wide.region_25.26_spmd.clone, body=%wide.region_23.25_spmd.clone.sunk | while | flops 2098208768 | bytes 183607536 | solution.py:164
  900.7 5.0 bitcast_add_fusion.11
  905.7 6.4 fusion.298
  912.1 26.6 %fusion.300 = f32[1,512,6,64]{1,3,2,0:T(8,128)} fusion(bf16[1024,6,64]{0,2,1:T(8,128)(2,1)S(1)} %get-tuple-element.1095, f32[6,512,1024]{2,1,0:T(8,128)} %fusion.298, f32[6,512,1024]{2,1,0:T(8,128)} %copy-done.3, f32[6,512]{1,0:T(8,128)S(1)} %dynamic-slice_bitcast_fusion.5, pred[512,1024]{1,0:T(8,128)(4,1)S(1)} %compare_and_fusion.5), kind=kOutput, calls=%fused_computation.108.clone.1 | convolution fusion | flops 437260288 | bytes 27275264 | tf_op jit(solution)/shard_map/while/body/eval_jaxpr/hqk,khe->qhe/dot_general | solution.py:95
  938.7 29.2 %bitcast_add_fusion.10 = f32[1024,6,64]{0,2,1:T(8,128)} fusion(f32[1024,6,64]{0,2,1:T(8,128)} %get-tuple-element.1072, f32[6,512,1024]{2,1,0:T(8,128)} %fusion.298, f32[6,512,1024]{2,1,0:T(8,128)} %copy-done.3, f32[6,512]{1,0:T(8,128)S(1)} %dynamic-slice_bitcast_fusion.5, pred[512,1024]{1,0:T(8,128)(4,1)S(1)} %compare_and_fusion.5, ...), kind=kOutput, calls=%fused_computation.107.clone.1 | convolution fusion | flops 438046720 | bytes 54951940 | tf_op jit(solution)/shard_map/while/body/eval_jaxpr/hqk,qhe->khe/dot_general | solution.py:96
  969.9 15.0 %dynamic_update_slice.39 = f32[2,512,6,64]{1,0,3,2:T(2,128)} dynamic-update-slice(f32[2,512,6,64]{1,0,3,2:T(2,128)} %get-tuple-element.1074, f32[1,512,6,64]{1,0,3,2:T(1,128)S(1)} %copy.104, s32[]{:T(128)S(6)} %copy.134, s32[]{:T(128)} %constant.113.clone.1..sunk.1, s32[]{:T(128)} %constant.113.clone.1..sunk.1, s32[]{:T(128)} %constant.113.clone.1..sunk.1) | dynamic-update-slice | bytes 1572868 | tf_op jit(solution)/shard_map/while/body/jit(dynamic_update_index_in_dim)/dynamic_update_slice | solution.py:128
  987.2 6.6 bitcast_add_fusion.11
  993.8 6.4 fusion.298
  1000.2 26.6 %fusion.300 = f32[1,512,6,64]{1,3,2,0:T(8,128)} fusion(bf16[1024,6,64]{0,2,1:T(8,128)(2,1)S(1)} %get-tuple-element.1095, f32[6,512,1024]{2,1,0:T(8,128)} %fusion.298, f32[6,512,1024]{2,1,0:T(8,128)} %copy-done.3, f32[6,512]{1,0:T(8,128)S(1)} %dynamic-slice_bitcast_fusion.5, pred[512,1024]{1,0:T(8,128)(4,1)S(1)} %compare_and_fusion.5), kind=kOutput, calls=%fused_computation.108.clone.1 | convolution fusion | flops 437260288 | bytes 27275264 | tf_op jit(solution)/shard_map/while/body/eval_jaxpr/hqk,khe->qhe/dot_general | solution.py:95
  1026.8 29.4 %bitcast_add_fusion.10 = f32[1024,6,64]{0,2,1:T(8,128)} fusion(f32[1024,6,64]{0,2,1:T(8,128)} %get-tuple-element.1072, f32[6,512,1024]{2,1,0:T(8,128)} %fusion.298, f32[6,512,1024]{2,1,0:T(8,128)} %copy-done.3, f32[6,512]{1,0:T(8,128)S(1)} %dynamic-slice_bitcast_fusion.5, pred[512,1024]{1,0:T(8,128)(4,1)S(1)} %compare_and_fusion.5, ...), kind=kOutput, calls=%fused_computation.107.clone.1 | convolution fusion | flops 438046720 | bytes 54951940 | tf_op jit(solution)/shard_map/while/body/eval_jaxpr/hqk,qhe->khe/dot_general | solution.py:96
  1058.2 15.0 %dynamic_update_slice.39 = f32[2,512,6,64]{1,0,3,2:T(2,128)} dynamic-update-slice(f32[2,512,6,64]{1,0,3,2:T(2,128)} %get-tuple-element.1074, f32[1,512,6,64]{1,0,3,2:T(1,128)S(1)} %copy.104, s32[]{:T(128)S(6)} %copy.134, s32[]{:T(128)} %constant.113.clone.1..sunk.1, s32[]{:T(128)} %constant.113.clone.1..sunk.1, s32[]{:T(128)} %constant.113.clone.1..sunk.1) | dynamic-update-slice | bytes 1572868 | tf_op jit(solution)/shard_map/while/body/jit(dynamic_update_index_in_dim)/dynamic_update_slice | solution.py:128
  1079.8 3.4 reshape.933
  1092.7 9.9 fusion.173
  1102.7 9.9 fusion.195
  1112.6 8.9 fusion.196
  1125.3 6.1 fusion.172
  1132.1 34.4 %psum.77 = f32[1536]{0:T(1024)} all-reduce(f32[1536]{0:T(1024)S(1)} %copy-done.62), channel_id=1, replica_groups=mesh['dp'=16,'mp'=2] {'dp'}, use_global_device_ids=true, to_apply=%region_41.42 | all-reduce | flops 1536 | bytes 12288 | tf_op jit(solution)/shard_map/psum | solution.py:334
  1166.5 13.4 reduce-scatter.11.cloned.1.call-done
  1187.8 41.7 %all-reduce = (f32[768]{0:T(1024)}, f32[768]{0:T(1024)}, f32[768]{0:T(1024)}, f32[768]{0:T(1024)}, f32[768]{0:T(1024)}) all-reduce(f32[768]{0:T(1024)S(1)} %get-tuple-element.524, f32[768]{0:T(1024)S(1)} %get-tuple-element.527, f32[768]{0:T(1024)S(1)} %copy-done.60, ...), channel_id=1, replica_groups=mesh['dp'=16,'mp'=2] {'dp','mp'}, use_global_device_ids=true, to_apply=%region_30.31 | all-reduce | flops 3840 | bytes 30720 | tf_op jit(solution)/shard_map/psum | solution.py:337
  1229.5 215.8 %all-reduce.4.cloned.1.call-done = (f32[768,3,384]{2,0,1:T(8,128)}, f32[384,768]{1,0:T(8,128)}, f32[768,1536]{1,0:T(8,128)}, f32[1536,768]{1,0:T(8,128)}) async-done(((f32[768,3,384]{2,0,1:T(8,128)}, f32[384,768]{1,0:T(8,128)}, f32[768,1536]{1,0:T(8,128)}, f32[1536,768]{1,0:T(8,128)}), (f32[768,3,384]{2,0,1:T(8,128)}, f32[384,768]{1,0:T(8,128)}, f32[768,1536]{1,0:T(8,128)}, ...) | async-done | bytes 14155792 | tf_op jit(solution)/shard_map/psum | solution.py:334
  1445.3 4.2 copy.160
  (310 shorter events, 115.1 us)
Async XLA Ops:
  7.2 325.3 %copy-start = (bf16[768,1536]{1,0:T(8,128)(2,1)S(1)}, bf16[768,1536]{1,0:T(8,128)(2,1)}, u32[]{:S(2)}) copy-start(bf16[768,1536]{1,0:T(8,128)(2,1)} %param.32) | copy-start | bytes 7077892
  7.2 5.2 copy-start.51
  7.2 5.2 copy-start.63
  7.2 54.8 %all-gather.5.cloned.1.call-start = ((), (), s32[]{:S(2)}) async-start(), calls=%async_computation.4 | async-start | bytes 4718592 | tf_op jit(solution)/shard_map/all_gather | solution.py:199
  7.3 5.1 copy-start.9
  9.1 2.6 copy-start.49
  9.1 5.7 copy-start.67
  14.2 267.1 %reduce-scatter.5.cloned.1.call-start = ((), (), s32[]{:S(2)}) async-start(), calls=%async_computation.5 | async-start | bytes 9437184 | tf_op jit(solution)/shard_map/reduce_scatter | solution.py:238
  16.9 52.4 %copy-start.33 = (f32[2048,32]{0,1:T(8,128)}, f32[2048,32]{0,1:T(8,128)S(1)}, u32[]{:S(2)}) copy-start(f32[2048,32]{0,1:T(8,128)S(1)} %get-tuple-element.683) | copy-start | bytes 786436
  91.9 3.7 copy-start.16
  91.9 3.7 copy-start.26
  104.8 3.7 copy-start.16
  104.8 3.7 copy-start.26
  130.7 12.1 copy-start.6
  130.7 12.1 copy-start.29
  171.2 12.1 copy-start.6
  171.2 12.1 copy-start.29
  199.5 4.5 copy-start.24
  204.1 128.4 %all-gather.7.cloned.1.call-start = ((), (), s32[]{:S(2)}) async-start(), calls=%async_computation.6 | async-start | bytes 4718592 | tf_op jit(solution)/shard_map/all_gather | solution.py:245
  287.4 91.5 %all-gather.9.cloned.1.call-start = ((), (), s32[]{:S(2)}) async-start(), calls=%async_computation.8 | async-start | bytes 4718592 | tf_op jit(solution)/shard_map/all_gather | solution.py:267
  288.0 194.6 %reduce-scatter.9.cloned.1.call-start = ((), (), s32[]{:S(2)}) async-start(), calls=%async_computation.9 | async-start | bytes 9437184 | tf_op jit(solution)/shard_map/reduce_scatter | solution.py:274
  398.4 7.0 copy-start.72
  405.4 123.3 %reduce-scatter.7.cloned.1.call-start = ((), (), s32[]{:S(2)}) async-start(), calls=%async_computation.7 | async-start | bytes 4718592 | tf_op jit(solution)/shard_map/reduce_scatter | solution.py:254
  416.2 112.4 %copy-start.65 = (f32[768]{0:T(1024)S(1)}, f32[768]{0:T(1024)}, u32[]{:S(2)}) copy-start(f32[768]{0:T(1024)} %param.35) | copy-start | bytes 9220
  416.2 165.7 %all-gather.11.cloned.1.call-start = ((), (), s32[]{:S(2)}) async-start(), calls=%async_computation.10 | async-start | bytes 4718592 | tf_op jit(solution)/shard_map/all_gather | solution.py:280
  486.8 48.4 %copy-start.19 = (bf16[2,512,768]{2,1,0:T(8,128)(2,1)S(1)}, bf16[2,512,768]{2,1,0:T(8,128)(2,1)}, u32[]{:S(2)}) copy-start(bf16[2,512,768]{2,1,0:T(8,128)(2,1)} %param.25) | copy-start | bytes 4718596
  533.5 3.3 copy-start.55
  536.8 643.0 %reduce-scatter.11.cloned.1.call-start = ((), (), s32[]{:S(2)}) async-start(), calls=%async_computation.11 | async-start | bytes 9437184 | tf_op jit(solution)/shard_map/reduce_scatter | solution.py:329
  586.9 6.7 copy-start.2
  586.9 6.7 copy-start.11
  595.6 10.1 copy-start.18
  595.6 10.1 copy-start.35
  605.7 13.5 copy-start.7
  741.3 10.1 copy-start.18
  741.4 10.1 copy-start.35
  751.5 13.6 copy-start.7
  891.5 6.7 copy-start.5
  891.5 6.7 copy-start.12
  891.5 6.7 copy-start.17
  891.5 6.7 copy-start.43
  891.5 6.7 copy-start.45
  891.6 6.7 copy-start.48
  900.7 5.0 copy-start.3
  987.2 6.6 copy-start.3
  1077.1 6.2 copy-start.22
  1102.6 342.7 %all-reduce.4.cloned.1.call-start = ((), (), s32[]{:S(2)}) async-start(), calls=%async_computation.12 | async-start | bytes 28311552 | tf_op jit(solution)/shard_map/psum | solution.py:334
  1102.7 9.9 copy-start.69
  1112.6 8.9 copy-start.25
  1112.6 8.9 copy-start.70
  1121.5 3.8 copy-start.68
  1131.4 48.5 %copy-start.10 = (bf16[2,512,768]{2,1,0:T(8,128)(2,1)S(1)}, bf16[2,512,768]{2,1,0:T(8,128)(2,1)}, u32[]{:S(2)}) copy-start(bf16[2,512,768]{2,1,0:T(8,128)(2,1)} %param.22) | copy-start | bytes 4718596
  1131.4 48.5 %copy-start.50 = (f32[2,512]{1,0:T(2,128)S(1)}, f32[2,512]{1,0:T(2,128)}, u32[]{:S(2)}) copy-start(f32[2,512]{1,0:T(2,128)} %copy-done.49) | copy-start | bytes 12292
  1131.4 48.5 %copy-start.52 = (f32[768]{0:T(1024)S(1)}, f32[768]{0:T(1024)}, u32[]{:S(2)}) copy-start(f32[768]{0:T(1024)} %param.26) | copy-start | bytes 9220
  1131.4 51.4 %copy-start.59 = (f32[2,512]{1,0:T(2,128)S(1)}, f32[2,512]{1,0:T(2,128)}, u32[]{:S(2)}) copy-start(f32[2,512]{1,0:T(2,128)} %copy-done.58) | copy-start | bytes 12292
  1131.4 51.4 %copy-start.54 = (f32[2,512]{1,0:T(2,128)S(1)}, f32[2,512]{1,0:T(2,128)}, u32[]{:S(2)}) copy-start(f32[2,512]{1,0:T(2,128)} %copy-done.53) | copy-start | bytes 12292
  1179.8 3.0 copy-start.13
  1185.1 2.7 copy-start.60
  1185.1 2.7 copy-start.61
  1445.3 5.2 slice-start.2
  1445.3 4.2 copy-start.40
  1445.3 5.2 slice-start.3
  1449.5 4.1 slice-start
  1450.5 3.4 slice-start.1
  1450.5 5.6 copy-start.1
  (34 other events, 53.1 us)
Sparse Core Ops, SparseCore 0:
  14.3 47.6 all-gather.4
  204.2 77.0 reduce-scatter.4
  287.5 44.9 all-gather.6
  334.0 44.9 all-gather.8
  405.5 77.0 reduce-scatter.8
  485.3 43.3 reduce-scatter.6
  536.9 44.9 all-gather.10
  1102.7 77.0 reduce-scatter.10
  1185.5 259.7 all-reduce.3
where the time goes:
time: 1470 us; the launch traced here: 1460 us
  waiting for transfers between devices  583 us (40%)
  matrix products  559 us (38%)
  local copies, waits for them, and re-layouts  137 us (9%)
  other arithmetic  79.3 us (5%)
  blocking collectives  76.1 us (5%)
  between operations  15.5 us (1%)
    psum x1, waiting for transfers between devices, local(): lax.psum((grad_qkv, grad_out, grad_up, grad_up_bias, grad_down), 'dp')  216 us
    dot_general x4, matrix products, block_backward(): jnp.einsum('hqk,qhe->khe', d_scores, query_blk, preferred_element_type=jn...  153 us
    dot_general x4, matrix products, block_backward(): jnp.einsum('hqk,khe->qhe', d_scores, key_set, preferred_element_type=jnp....  144 us
    reduce_scatter x1, waiting for transfers between devices, local(): lax.psum_scatter(branch, 'mp', scatter_dimension=1, tiled=True)  77.2 us
    dynamic_update_slice x8, local copies, waits for them, and re-layouts, attend_forward(): return lax.map(one_block, items)  67.6 us
    reduce_scatter x1, waiting for transfers between devices, local(): lax.psum_scatter(d_normed2.reshape(2, TOK_DEV, width), 'mp', scatter_dime...  66.3 us
    all_gather x1, waiting for transfers between devices, local(): lax.all_gather(normed1_low, 'mp', axis=1, tiled=True)  45.1 us
    all_gather x1, waiting for transfers between devices, local(): lax.all_gather(d_branch_low, 'mp', axis=1, tiled=True)  45 us
  transfers between devices with their start and end apart: 9, of which 9 were waited for; matrix products, arithmetic and copies ran while one was open for 4% of the time, Pallas kernels for 0%

commit v1 on v0

v1 whole, which is shorter than its diff:
```python
import functools
import math

import jax
import jax.numpy as jnp
from jax import lax
from jax.experimental import pallas as pl
from jax.experimental.pallas import tpu as pltpu
from jax.sharding import PartitionSpec as P

HD = 64
TOK_DEV = 1024
HALF = TOK_DEV // 2
EDGE = 16
CLEAN_OWN = HALF
NOISY_BASE = 2 * HALF + EDGE
NOISY_OWN = NOISY_BASE + EDGE
KEY_ROWS = NOISY_OWN + HALF + EDGE
TILE = 128
TILES = HALF // TILE
WINDOW = TILE + 2 * EDGE
KEY_TILE = 256
LANES = 128

epsilon = 1e-05
neg_large = -1e30
to_base2 = 0.125 * math.log2(math.e)
f32 = jnp.float32
bf16 = jnp.bfloat16

NN = (((1,), (0,)), ((), ()))
NT = (((1,), (1,)), ((), ()))


def dot(left, right, dims=NN):
    return lax.dot_general(left, right, dims, preferred_element_type=f32)


def layer_norm(values, norm_gain, norm_bias):
    average = jnp.mean(values, axis=-1, keepdims=True)
    centred = values - average
    variance = jnp.mean(centred * centred, axis=-1, keepdims=True)
    return centred * lax.rsqrt(variance + epsilon) * norm_gain + norm_bias


def gelu_tanh(values):
    inner = 0.7978845608028654 * (values + 0.044715 * values * values * values)
    return 0.5 * values * (1.0 + jnp.tanh(inner))


def low_lanes(shape):
    return lax.broadcasted_iota(jnp.int32, shape, 1) < HD


def turn(values, cosine, sine):
    lane = lax.broadcasted_iota(jnp.int32, values.shape, 1)
    first_half = (lane & (HD - 1)) < HD // 2
    swapped = jnp.where(
        first_half,
        pltpu.roll(values, LANES - HD // 2, 1),
        pltpu.roll(values, HD // 2, 1),
    )
    return values * cosine + swapped * sine


def project_kernel(rows_ref, w_ref, cos_ref, sin_ref, q_ref, k_ref, v_ref):
    rows = rows_ref[...]
    cosine, sine = cos_ref[...], sin_ref[...]
    for part, out_ref in ((0, q_ref), (1, k_ref)):
        field = dot(rows, w_ref[part])
        for pair in range(field.shape[1] // LANES):
            cols = slice(pair * LANES, (pair + 1) * LANES)
            out_ref[:, cols] = turn(field[:, cols], cosine, sine).astype(bf16)
    v_ref[...] = dot(rows, w_ref[2]).astype(bf16)


def project(rows, weights, cosine, sine):
    count, width = rows.shape
    cols = weights.shape[2]
    step = count // 9
    row_spec = pl.BlockSpec((step, width), lambda i: (i, 0))
    table_spec = pl.BlockSpec((step, LANES), lambda i: (i, 0))
    out_spec = pl.BlockSpec((step, cols), lambda i: (i, 0))
    shape = jax.ShapeDtypeStruct((count, cols), bf16)
    return pl.pallas_call(
        project_kernel,
        grid=(9,),
        in_specs=[
            row_spec,
            pl.BlockSpec(weights.shape, lambda i: (0, 0, 0)),
            table_spec,
            table_spec,
        ],
        out_specs=[out_spec] * 3,
        out_shape=[shape] * 3,
        name="project",
        cost_estimate=pl.CostEstimate(
            flops=2 * count * width * 3 * cols,
            bytes_accessed=2 * (count * (width + 3 * cols) + 3 * width * cols),
            transcendentals=0,
        ),
    )(rows, weights, cosine, sine)


def split_heads(rows):
    low = low_lanes(rows.shape)
    zero = jnp.zeros_like(rows)
    return jnp.where(low, rows, zero), jnp.where(low, zero, rows)


def between(shape, offset, low, high):
    index = lax.broadcasted_iota(jnp.int32, shape, 0) + offset
    return jnp.logical_and(index >= low, index < high)


def forward_kernel(
    span_ref, clean_ref, noisy_ref, q_ref, k_ref, v_ref, out_ref, lse_ref
):
    def one_tile(t, _):
        clean_at = pl.multiple_of(CLEAN_OWN + t * TILE, TILE)
        noisy_at = pl.multiple_of(NOISY_OWN + t * TILE, EDGE)
        window_at = pl.multiple_of(NOISY_BASE + t * TILE, EDGE)
        query = jnp.concatenate(
            [q_ref[pl.ds(noisy_at, TILE), :], q_ref[pl.ds(clean_at, TILE), :]], axis=0
        )
        queries = split_heads(query)
        key_low, key_high = clean_ref[t, 0:1, :], clean_ref[t, 1:2, :]
        own_low, own_high = noisy_ref[t, 0:1, :], noisy_ref[t, 1:2, :]
        keys = k_ref[pl.ds(window_at, WINDOW), :]
        values_t = v_ref[pl.ds(window_at, WINDOW), :].T
        allowed = between((WINDOW, TILE), 0, own_low, own_high)
        state = []
        for head in range(2):
            scores = dot(keys, queries[head][:TILE], NT) * to_base2
            scores = jnp.where(allowed, scores, neg_large)
            top = jnp.max(scores, axis=0, keepdims=True)
            expo = jnp.exp2(scores - top)
            total = jnp.sum(expo, axis=0, keepdims=True)
            mixed = dot(values_t[head * HD : (head + 1) * HD], expo.astype(bf16))
            blank = jnp.zeros((1, TILE), f32)
            state += [
                jnp.concatenate([top, blank + neg_large], axis=1),
                jnp.concatenate([total, blank], axis=1),
                jnp.concatenate([mixed, jnp.zeros((HD, TILE), f32)], axis=1),
            ]
        first_key, trips = span_ref[t, 0], span_ref[t, 1]

        def one_step(j, state):
            at = pl.multiple_of(first_key + j * KEY_TILE, EDGE)
            keys = k_ref[pl.ds(at, KEY_TILE), :]
            values_t = v_ref[pl.ds(at, KEY_TILE), :].T
            allowed = between((KEY_TILE, 2 * TILE), at, key_low, key_high)
            after = []
            for head in range(2):
                top, total, mixed = state[3 * head : 3 * head + 3]
                scores = dot(keys, queries[head], NT) * to_base2
                scores = jnp.where(allowed, scores, neg_large)
                new_top = jnp.maximum(top, jnp.max(scores, axis=0, keepdims=True))
                keep = jnp.exp2(top - new_top)
                expo = jnp.exp2(scores - new_top)
                after += [
                    new_top,
                    total * keep + jnp.sum(expo, axis=0, keepdims=True),
                    mixed * keep
                    + dot(values_t[head * HD : (head + 1) * HD], expo.astype(bf16)),
                ]
            return tuple(after)

        state = lax.fori_loop(0, trips, one_step, tuple(state))
        pair = jnp.concatenate(
            [state[2] / state[1], state[5] / state[4]], axis=0
        ).T.astype(bf16)
        out_at = pl.multiple_of(t * TILE, TILE)
        out_ref[pl.ds(out_at, TILE), :] = pair[:TILE]
        out_ref[pl.ds(pl.multiple_of(HALF + t * TILE, TILE), TILE), :] = pair[TILE:]
        lse_ref[0, t, 0:1, :] = state[0] + jnp.log2(state[1])
        lse_ref[0, t, 1:2, :] = state[3] + jnp.log2(state[4])
        return 0

    lax.fori_loop(0, TILES, one_tile, 0)


def attend_forward(spans, clean_bounds, noisy_bounds, query, keys, values):
    count, cols = query.shape
    pairs = cols // LANES
    whole3 = lambda array: pl.BlockSpec(array.shape, lambda p, s: (0, 0, 0))
    row_spec = pl.BlockSpec((count, LANES), lambda p, s: (0, p))
    work = pairs * 2 * 2 * HALF * TOK_DEV
    return pl.pallas_call(
        forward_kernel,
        grid_spec=pltpu.PrefetchScalarGridSpec(
            num_scalar_prefetch=1,
            grid=(pairs,),
            in_specs=[whole3(clean_bounds), whole3(noisy_bounds)] + [row_spec] * 3,
            out_specs=[
                pl.BlockSpec((TOK_DEV, LANES), lambda p, s: (0, p)),
                pl.BlockSpec((1, TILES, 2, 2 * TILE), lambda p, s: (p, 0, 0, 0)),
            ],
        ),
        out_shape=[
            jax.ShapeDtypeStruct((TOK_DEV, cols), bf16),
            jax.ShapeDtypeStruct((pairs, TILES, 2, 2 * TILE), f32),
        ],
        name="attend_forward",
        cost_estimate=pl.CostEstimate(
            flops=4 * work * HD, bytes_accessed=8 * count * cols, transcendentals=work
        ),
    )(spans, clean_bounds, noisy_bounds, query, keys, values)


def backward_kernel(
    span_ref,
    clean_ref,
    noisy_ref,
    q_ref,
    k_ref,
    v_ref,
    o_ref,
    d_ref,
    lse_ref,
    cos_ref,
    sin_ref,
    out_ref,
    dk_ref,
    dv_ref,
):
    dk_ref[...] = jnp.zeros_like(dk_ref)
    dv_ref[...] = jnp.zeros_like(dv_ref)
    out_ref[0] = jnp.zeros_like(out_ref[0])

    def one_tile(t, _):
        clean_at = pl.multiple_of(CLEAN_OWN + t * TILE, TILE)
        noisy_at = pl.multiple_of(NOISY_OWN + t * TILE, EDGE)
        window_at = pl.multiple_of(NOISY_BASE + t * TILE, EDGE)
        low_at = pl.multiple_of(t * TILE, TILE)
        high_at = pl.multiple_of(HALF + t * TILE, TILE)

        def both(ref, low, high):
            return jnp.concatenate(
                [ref[pl.ds(low, TILE), :], ref[pl.ds(high, TILE), :]], axis=0
            )

        query = split_heads(both(q_ref, noisy_at, clean_at))
        d_rows = both(d_ref, low_at, high_at)
        o_rows = both(o_ref, low_at, high_at)
        product = (d_rows.astype(f32) * o_rows.astype(f32)).T
        d_out = split_heads(d_rows)
        inner = [
            jnp.sum(product[head * HD : (head + 1) * HD], axis=0, keepdims=True)
            for head in range(2)
        ]
        lse = [lse_ref[0, t, head : head + 1, :] for head in range(2)]
        key_low, key_high = clean_ref[t, 0:1, :], clean_ref[t, 1:2, :]
        own_low, own_high = noisy_ref[t, 0:1, :], noisy_ref[t, 1:2, :]

        def accumulate(at, rows, cols, allowed, d_query):
            keys = k_ref[pl.ds(at, rows), :]
            values = v_ref[pl.ds(at, rows), :]
            keys_t = keys.T
            weights, d_scores, after = [], [], []
            for head in range(2):
                scores = dot(keys, query[head][:cols], NT) * to_base2
                scores = jnp.where(allowed, scores - lse[head][:, :cols], neg_large)
                probs = jnp.exp2(scores)
                d_probs = dot(values, d_out[head][:cols], NT)
                d_score = (probs * (d_probs - inner[head][:, :cols]) * 0.125).astype(bf16)
                weights.append(probs.astype(bf16))
                d_scores.append(d_score)
                after.append(
                    d_query[head] + dot(keys_t[head * HD : (head + 1) * HD], d_score)
                )
            stack = lambda parts: jnp.concatenate([part[:cols] for part in parts], axis=0)
            dv_ref[pl.ds(at, rows), :] += dot(
                jnp.concatenate(weights, axis=1), stack(d_out)
            )
            dk_ref[pl.ds(at, rows), :] += dot(
                jnp.concatenate(d_scores, axis=1), stack(query)
            )
            return tuple(after)

        allowed = between((WINDOW, TILE), 0, own_low, own_high)
        zero = jnp.zeros((HD, TILE), f32)
        start = accumulate(window_at, WINDOW, TILE, allowed, (zero, zero))
        start = tuple(jnp.concatenate([part, zero], axis=1) for part in start)
        first_key, trips = span_ref[t, 0], span_ref[t, 1]

        def one_step(j, d_query):
            at = pl.multiple_of(first_key + j * KEY_TILE, EDGE)
            allowed = between((KEY_TILE, 2 * TILE), at, key_low, key_high)
            return accumulate(at, KEY_TILE, 2 * TILE, allowed, d_query)

        d_query = lax.fori_loop(0, trips, one_step, start)
        d_query = jnp.concatenate(d_query, axis=0).T
        for at, part in ((noisy_at, d_query[:TILE]), (clean_at, d_query[TILE:])):
            turned = turn(part, cos_ref[pl.ds(at, TILE), :], -sin_ref[pl.ds(at, TILE), :])
            out_ref[0, pl.ds(at, TILE), :] = turned.astype(bf16)
        return 0

    lax.fori_loop(0, TILES, one_tile, 0)
    step = KEY_ROWS // 9

    def finish(i, _):
        rows = pl.ds(pl.multiple_of(i * step, EDGE), step)
        out_ref[1, rows, :] = turn(dk_ref[rows, :], cos_ref[rows, :], -sin_ref[rows, :]).astype(
            bf16
        )
        out_ref[2, rows, :] = dv_ref[rows, :].astype(bf16)
        return 0

    lax.fori_loop(0, 9, finish, 0)


def attend_backward(
    spans, clean_bounds, noisy_bounds, query, keys, values, attended, d_attended, lse, cosine, sine
):
    count, cols = query.shape
    pairs = cols // LANES
    whole2 = lambda array: pl.BlockSpec(array.shape, lambda p, s: (0, 0))
    whole3 = lambda array: pl.BlockSpec(array.shape, lambda p, s: (0, 0, 0))
    row_spec = pl.BlockSpec((count, LANES), lambda p, s: (0, p))
    own_spec = pl.BlockSpec((TOK_DEV, LANES), lambda p, s: (0, p))
    work = pairs * 2 * 2 * HALF * TOK_DEV
    return pl.pallas_call(
        backward_kernel,
        grid_spec=pltpu.PrefetchScalarGridSpec(
            num_scalar_prefetch=1,
            grid=(pairs,),
            in_specs=[whole3(clean_bounds), whole3(noisy_bounds)]
            + [row_spec] * 3
            + [own_spec] * 2
            + [
                pl.BlockSpec((1, TILES, 2, 2 * TILE), lambda p, s: (p, 0, 0, 0)),
                whole2(cosine),
                whole2(sine),
            ],
            out_specs=pl.BlockSpec((3, count, LANES), lambda p, s: (0, 0, p)),
            scratch_shapes=[pltpu.VMEM((count, LANES), f32)] * 2,
        ),
        out_shape=jax.ShapeDtypeStruct((3, count, cols), bf16),
        name="attend_backward",
        cost_estimate=pl.CostEstimate(
            flops=10 * work * HD, bytes_accessed=16 * count * cols, transcendentals=work
        ),
    )(
        spans,
        clean_bounds,
        noisy_bounds,
        query,
        keys,
        values,
        attended,
        d_attended,
        lse,
        cosine,
        sine,
    )


def key_layout(seq_lengths, block_len, part):
    index = jnp.arange(KEY_ROWS, dtype=jnp.int32)
    own = part * HALF
    token = jnp.where(
        index < NOISY_BASE, index + (own - HALF), index - NOISY_BASE + (own - EDGE)
    )
    ends = jnp.cumsum(seq_lengths)
    passed = token[:, None] >= ends[None, :]
    starts = jnp.sum(jnp.where(passed, seq_lengths[None, :], 0), axis=1)
    lengths_here = jnp.where(passed, 0, ends[None, :])
    stops = jnp.min(jnp.where(passed, TOK_DEV, lengths_here), axis=1)
    positions = token - starts
    block_start = starts + positions // block_len * block_len
    block_stop = jnp.minimum(block_start + block_len, stops)
    mine = slice(CLEAN_OWN, CLEAN_OWN + HALF)
    low, start, stop = starts[mine], block_start[mine], block_stop[mine]
    to_clean = own - HALF
    tiles = lambda column: column.reshape(TILES, 1, TILE)
    clean_bounds = jnp.concatenate(
        [
            jnp.concatenate([tiles(low - to_clean), tiles(low - to_clean)], axis=2),
            jnp.concatenate([tiles(start - to_clean), tiles(stop - to_clean)], axis=2),
        ],
        axis=1,
    )
    to_window = own - EDGE + TILE * jnp.arange(TILES, dtype=jnp.int32)[:, None, None]
    noisy_bounds = jnp.concatenate(
        [tiles(start) - to_window, tiles(stop) - to_window], axis=1
    )
    first = jnp.min(clean_bounds[:, 0], axis=1) // EDGE * EDGE
    last = jnp.max(clean_bounds[:, 1], axis=1)
    trips = (last - first + KEY_TILE - 1) // KEY_TILE
    spans = jnp.stack([first, trips], axis=1)
    lane = jnp.arange(LANES, dtype=jnp.int32)
    frequency = jnp.exp(
        (lane % (HD // 2)).astype(f32) * (-math.log(10000.0) / (HD // 2))
    )
    angles = positions.astype(f32)[:, None] * frequency[None, :]
    sign = jnp.where(lane % HD < HD // 2, -1.0, 1.0)
    return spans, clean_bounds, noisy_bounds, jnp.cos(angles), jnp.sin(angles) * sign


def half_of(array, which):
    size = array.shape[0] // 2
    return lax.dynamic_slice_in_dim(array, which * size, size, 0)


def in_order(bit, mine, theirs):
    flip = bit == 0
    return jnp.concatenate(
        [jnp.where(flip, mine, theirs), jnp.where(flip, theirs, mine)], axis=0
    )


def local(
    dp_size,
    tokens,
    lengths,
    block_size,
    cotangent,
    ln1_gain,
    ln1_bias,
    w_qkv,
    w_out,
    ln2_gain,
    ln2_bias,
    w_up,
    b_up,
    w_down,
    b_down,
):
    width = tokens.shape[2]
    part = lax.axis_index("mp")
    place = lax.axis_index("dp")
    bits = dp_size.bit_length() - 1
    across = [(0, 1), (1, 0)]
    flips = [[(i, i ^ (1 << b)) for i in range(dp_size)] for b in range(bits)]
    my_bit = [(place >> b) & 1 for b in range(bits)]

    def to_partner(array):
        return lax.ppermute(array, "mp", across)

    def to_flip(array, b):
        return lax.ppermute(array, "dp", flips[b])

    def fetch(weights):
        here = to_partner(half_of(weights, my_bit[0]))
        there = to_flip(here, 0)
        return in_order(my_bit[0], here, there)

    def reduce_over_all(mine, others):
        core = my_bit[0]
        got = to_flip(half_of(others, 1 - core).astype(bf16), 0)
        crossing = half_of(others, core) + got.astype(f32)
        got_own = to_flip(half_of(mine, 1 - core).astype(bf16), 0)
        total = half_of(mine, core) + got_own.astype(f32)
        total = total + to_partner(crossing.astype(bf16)).astype(f32)
        for b in range(1, bits):
            got = to_flip(half_of(total, 1 - my_bit[b]).astype(bf16), b)
            total = half_of(total, my_bit[b]) + got.astype(f32)
        total = total.astype(bf16)
        for b in reversed(range(bits)):
            total = in_order(my_bit[b], total, to_flip(total, b))
        return total.astype(f32)

    edge = jnp.where(part == 0, tokens[0, HALF - EDGE :], tokens[0, :EDGE])
    context = to_partner(jnp.concatenate([tokens[1], edge], axis=0))
    qkv_mine = w_qkv.transpose(1, 0, 2)
    qkv_other = fetch(w_qkv.transpose(1, 0, 2).reshape(-1, w_qkv.shape[2])).reshape(
        qkv_mine.shape
    )
    out_other = fetch(w_out)
    up_other = fetch(w_up)
    bias_other = to_partner(b_up)
    down_other = fetch(w_down)

    spans, clean_bounds, noisy_bounds, cosine, sine = key_layout(lengths[0], block_size[0], part)
    clean_other, edge_other = context[:HALF], context[HALF:]
    key_tokens = jnp.concatenate(
        [clean_other, tokens[1], clean_other[:EDGE], edge_other, tokens[0], edge_other], axis=0
    )
    normed1_keys = layer_norm(key_tokens.astype(f32), ln1_gain, ln1_bias).astype(bf16)

    saved = []
    for weights in (qkv_mine, qkv_other):
        query, keys, values = project(normed1_keys, weights, cosine, sine)
        attended, lse = attend_forward(spans, clean_bounds, noisy_bounds, query, keys, values)
        saved.append((query, keys, values, attended, lse))

    x_rows = tokens.astype(f32).reshape(TOK_DEV, width)
    branch = dot(saved[0][3], w_out) + dot(saved[1][3], out_other)
    mid = x_rows + branch
    normed2, norm2_back = jax.vjp(layer_norm, mid, ln2_gain, ln2_bias)
    mlp_rows = normed2.astype(bf16)
    d_low = cotangent.reshape(TOK_DEV, width)
    d_out_rows = d_low.astype(f32)
    grad_b_down = jnp.sum(d_out_rows, axis=0)
    down = 0.0
    d_normed2 = 0.0
    grad_down, grad_up, grad_up_bias = [], [], []
    for up, bias, down_w in ((w_up, b_up, w_down), (up_other, bias_other, down_other)):
        pre = dot(mlp_rows, up) + bias.astype(f32)
        act_low = gelu_tanh(pre).astype(bf16)
        down = down + dot(act_low, down_w)
        d_act = dot(d_low, down_w, NT)
        d_pre = jax.vjp(gelu_tanh, pre)[1](d_act)[0].astype(bf16)
        grad_down.append(jnp.einsum("rf,rd->fd", act_low, d_low, preferred_element_type=f32))
        grad_up.append(jnp.einsum("rd,rf->df", mlp_rows, d_pre, preferred_element_type=f32))
        grad_up_bias.append(jnp.sum(d_pre.astype(f32), axis=0))
        d_normed2 = d_normed2 + dot(d_pre, up, NT)
    out = (mid + down + b_down).astype(bf16).reshape(tokens.shape)
    grad_down = reduce_over_all(*grad_down)
    grad_up = reduce_over_all(*grad_up)

    d_mid_norm, grad_ln2_gain, grad_ln2_bias = norm2_back(d_normed2)
    d_mid = d_out_rows + d_mid_norm
    d_branch = d_mid.astype(bf16)
    grad_out = []
    d_attended = []
    for item, weights in zip(saved, (w_out, out_other)):
        grad_out.append(jnp.einsum("rf,rd->fd", item[3], d_branch, preferred_element_type=f32))
        d_attended.append(dot(d_branch, weights, NT).astype(bf16))
    grad_out = reduce_over_all(*grad_out)

    grad_qkv = [None, None]
    d_normed1_keys = 0.0
    for group, weights in ((1, qkv_other), (0, qkv_mine)):
        query, keys, values, attended, lse = saved[group]
        d_qkv = attend_backward(
            spans,
            clean_bounds,
            noisy_bounds,
            query,
            keys,
            values,
            attended,
            d_attended[group],
            lse,
            cosine,
            sine,
        )
        grad_qkv[group] = jnp.einsum(
            "rd,crf->cdf", normed1_keys, d_qkv, preferred_element_type=f32
        ).reshape(-1, d_qkv.shape[2])
        d_normed1_keys = d_normed1_keys + jnp.einsum(
            "crf,cdf->rd", d_qkv, weights, preferred_element_type=f32
        )
    grad_qkv = reduce_over_all(*grad_qkv).reshape(qkv_mine.shape).transpose(1, 0, 2)

    clean_back = d_normed1_keys[:HALF]
    clean_back = clean_back.at[:EDGE].add(d_normed1_keys[2 * HALF : 2 * HALF + EDGE])
    edge_back = d_normed1_keys[NOISY_BASE:NOISY_OWN] + d_normed1_keys[NOISY_OWN + HALF :]
    back = to_partner(jnp.concatenate([clean_back, edge_back], axis=0).astype(bf16)).astype(f32)
    at_end = jnp.concatenate([jnp.zeros((HALF - EDGE, width), f32), back[HALF:]], axis=0)
    at_start = jnp.concatenate([back[HALF:], jnp.zeros((HALF - EDGE, width), f32)], axis=0)
    d_normed1 = jnp.concatenate(
        [
            d_normed1_keys[NOISY_OWN : NOISY_OWN + HALF]
            + jnp.where(part == 0, at_end, at_start),
            d_normed1_keys[CLEAN_OWN : CLEAN_OWN + HALF] + back[:HALF],
        ],
        axis=0,
    )
    norm1_back = jax.vjp(layer_norm, x_rows, ln1_gain, ln1_bias)[1]
    d_x_norm, grad_ln1_gain, grad_ln1_bias = norm1_back(d_normed1)
    grad_tokens = (d_mid + d_x_norm).reshape(tokens.shape)

    bias_sum = to_partner(grad_up_bias[1]) + grad_up_bias[0]
    hidden = bias_sum.shape[0]
    own_bias = jnp.concatenate([jnp.where(part == 0, bias_sum, 0.0), jnp.where(part == 0, 0.0, bias_sum)])
    small = lax.psum(
        jnp.concatenate(
            [own_bias, grad_ln1_gain, grad_ln1_bias, grad_ln2_gain, grad_ln2_bias, grad_b_down]
        ),
        ("dp", "mp"),
    )
    grad_up_bias = lax.dynamic_slice_in_dim(small, part * hidden, hidden, 0)
    rest = [small[2 * hidden + i * width : 2 * hidden + (i + 1) * width] for i in range(5)]
    return (
        out,
        grad_tokens,
        rest[0],
        rest[1],
        grad_qkv,
        grad_out,
        rest[2],
        rest[3],
        grad_up,
        grad_up_bias,
        grad_down,
        rest[4],
    )


def solution(mesh):
    in_specs = (
        P(None, ("dp", "mp"), None),
        P("dp", None),
        P(),
        P(None, ("dp", "mp"), None),
        P(),
        P(),
        P(None, None, "mp"),
        P("mp", None),
        P(),
        P(),
        P(None, "mp"),
        P("mp"),
        P("mp", None),
        P(),
    )
    out_specs = (
        P(None, ("dp", "mp"), None),
        P(None, ("dp", "mp"), None),
        P(),
        P(),
        P(None, None, "mp"),
        P("mp", None),
        P(),
        P(),
        P(None, "mp"),
        P("mp"),
        P("mp", None),
        P(),
    )
    return jax.shard_map(
        functools.partial(local, mesh.shape["dp"]),
        mesh=mesh,
        in_specs=in_specs,
        out_specs=out_specs,
        check_vma=False,
    )
```

time: 1470 us -> 668 us (0.45)
  matrix products: 559 us -> 103 us
  waiting for transfers between devices: 583 us -> 175 us
  starting transfers between devices: 0.37 us -> 113 us
  Pallas kernels: 0 us -> 112 us
  local copies, waits for them, and re-layouts: 137 us -> 51.7 us
  blocking collectives: 76.1 us -> 39.7 us
  other arithmetic: 79.3 us -> 60.3 us
    dot_general x40 -> x22, matrix products: 559 us -> 103 us  [the longest x12 56.3 us: dot(): return lax.dot_general(left, right, dims, preferred_element_type=f32)]
    psum x1 -> x0, waiting for transfers between devices: 216 us -> none  [local(): lax.psum((grad_qkv, grad_out, grad_up, grad_up_bias, grad_down), 'dp')]
    reduce_scatter x4 -> x0, waiting for transfers between devices: 199 us -> none  [the longest x1 77.2 us: local(): lax.psum_scatter(branch, 'mp', scatter_dimension=1, tiled=True)]
    ppermute x0 -> x52, waiting for transfers between devices: none -> 175 us  [the longest x12 88.6 us: to_partner(): return lax.ppermute(array, 'mp', across)]
    all_gather x4 -> x0, waiting for transfers between devices: 168 us -> none  [the longest x1 45.1 us: local(): lax.all_gather(normed1_low, 'mp', axis=1, tiled=True)]
    ppermute x0 -> x52, starting transfers between devices: none -> 113 us  [the longest x12 60.9 us: to_partner(): return lax.ppermute(array, 'mp', across)]
    pallas_call x0 -> x6, Pallas kernels: none -> 112 us  [the longest x2 52.8 us: attend_backward(): pl.pallas_call(backward_kernel, grid_spec=pltpu.PrefetchScalarGridSpec(nu...]
    dynamic_update_slice x8 -> x0, local copies, waits for them, and re-layouts: 67.6 us -> none  [attend_forward(): return lax.map(one_block, items)]
  transfers between devices with their start and end apart: 9 -> 52, of which waited for: 9 -> 20; matrix products, arithmetic and copies ran while one was open for 4% -> 30% of each run, Pallas kernels for 0% -> 17%
where the time goes in v1:
time: 668 us; the launch traced here: 657 us
  waiting for transfers between devices  175 us (26%)
  starting transfers between devices  113 us (17%)
  Pallas kernels  112 us (17%)
  matrix products  103 us (15%)
  other arithmetic  60.3 us (9%)
  local copies, waits for them, and re-layouts  51.7 us (8%)
  blocking collectives  39.7 us (6%)
    ppermute x12, waiting for transfers between devices, to_partner(): return lax.ppermute(array, 'mp', across)  88.6 us
    ppermute x40, waiting for transfers between devices, to_flip(): return lax.ppermute(array, 'dp', flips[b])  86.6 us
    ppermute x12, starting transfers between devices, to_partner(): return lax.ppermute(array, 'mp', across)  60.9 us
    dot_general x12, matrix products, dot(): return lax.dot_general(left, right, dims, preferred_element_type=f32)  56.3 us
    pallas_call x2, Pallas kernels, attend_backward(): pl.pallas_call(backward_kernel, grid_spec=pltpu.PrefetchScalarGridSpec(nu...  52.8 us
    ppermute x40, starting transfers between devices, to_flip(): return lax.ppermute(array, 'dp', flips[b])  51.6 us
    psum x1, blocking collectives, local(): lax.psum(jnp.concatenate([own_bias, grad_ln1_gain, grad_ln1_bias, grad_ln...  39.7 us
    pallas_call x2, Pallas kernels, attend_forward(): pl.pallas_call(forward_kernel, grid_spec=pltpu.PrefetchScalarGridSpec(num...  38.8 us
  transfers between devices with their start and end apart: 52, of which 20 were waited for; matrix products, arithmetic and copies ran while one was open for 30% of the time, Pallas kernels for 17%

profile of v1, /device:TPU:0, one launch (start us, length us, event | category | flops | bytes accessed | tf_op | source)
XLA Modules:
  0.0 656.6 jit_solution(10540981099268633085)
XLA Ops:
  3.7 3.0 collective-permute-start
  18.4 4.4 fusion.49
  24.3 26.8 %collective-permute-done.3 = bf16[192,768]{1,0:T(8,128)(2,1)S(1)} collective-permute-done((bf16[192,768]{1,0:T(8,128)(2,1)S(1)}, bf16[192,768]{1,0:T(8,128)(2,1)S(1)}, u32[]{:S(2)}, u32[]{:S(2)}) %collective-permute-start.3) | collective-permute-done | bytes 294944 | tf_op jit(solution)/shard_map/ppermute | solution.py:439
  52.3 2.4 constant_dynamic-slice_fusion.1
  55.3 20.4 %collective-permute-done.7 = bf16[1536]{0:T(1024)(128)(2,1)S(1)} collective-permute-done((bf16[1536]{0:T(1024)(128)(2,1)S(1)}, bf16[1536]{0:T(1024)(128)(2,1)S(1)}, u32[]{:S(2)}, u32[]{:S(2)}) %collective-permute-start.7) | collective-permute-done | bytes 3104 | tf_op jit(solution)/shard_map/ppermute | solution.py:439
  85.4 10.0 %project.2 = (bf16[1584,384]{1,0:T(8,128)(2,1)}, bf16[1584,384]{1,0:T(8,128)(2,1)}, bf16[1584,384]{1,0:T(8,128)(2,1)}) custom-call(bf16[1584,768]{1,0:T(8,128)(2,1)} %fusion.24.rows_ref, bf16[3,768,384]{2,1,0:T(8,128)(2,1)} %bitcast.146, f32[1584,128]{1,0:T(8,128)} %get-tuple-element.118.cos_ref, f32[1584,128]{1,0:T(8,128)} %get-tuple-element.117.sin_ref), custom_call_target="tpu_custom_call" | custom-call | flops 2802843648 | bytes 7852032 | tf_op jit(solution)/shard_map/project/pallas_call | solution.py:85
  95.4 19.5 %attend_forward.2 = (bf16[1024,384]{1,0:T(8,128)(2,1)}, f32[3,4,2,256]{3,2,1,0:T(2,128)}) custom-call(s32[4,2]{1,0:T(4,128)} %pad_add_fusion.1.span_ref, s32[4,2,256]{2,1,0:T(2,128)} %add_add_fusion.4.clean_ref, s32[4,2,128]{2,1,0:T(2,128)} %pad_add_fusion.noisy_ref, bf16[1584,384]{1,0:T(8,128)(2,1)} %get-tuple-element.34.q_ref, ...), custom_call_target="tpu_custom_call" | custom-call | flops 1610612736 | bytes 4866048 | tf_op jit(solution)/shard_map/attend_forward/pallas_call | solution.py:189
  114.8 3.8 fusion.88
  118.6 4.7 collective-permute-start.9
  126.4 10.0 %project.3 = (bf16[1584,384]{1,0:T(8,128)(2,1)}, bf16[1584,384]{1,0:T(8,128)(2,1)}, bf16[1584,384]{1,0:T(8,128)(2,1)}) custom-call(bf16[1584,768]{1,0:T(8,128)(2,1)} %fusion.24.rows_ref, bf16[3,768,384]{2,1,0:T(8,128)(2,1)} %bitcast.143, f32[1584,128]{1,0:T(8,128)} %get-tuple-element.118.cos_ref, f32[1584,128]{1,0:T(8,128)} %get-tuple-element.117.sin_ref), custom_call_target="tpu_custom_call" | custom-call | flops 2802843648 | bytes 7852032 | tf_op jit(solution)/shard_map/project/pallas_call | solution.py:85
  136.4 19.3 %attend_forward.3 = (bf16[1024,384]{1,0:T(8,128)(2,1)}, f32[3,4,2,256]{3,2,1,0:T(2,128)}) custom-call(s32[4,2]{1,0:T(4,128)} %pad_add_fusion.1.span_ref, s32[4,2,256]{2,1,0:T(2,128)} %add_add_fusion.4.clean_ref, s32[4,2,128]{2,1,0:T(2,128)} %pad_add_fusion.noisy_ref, bf16[1584,384]{1,0:T(8,128)(2,1)} %get-tuple-element.38.q_ref, ...), custom_call_target="tpu_custom_call" | custom-call | flops 1610612736 | bytes 4866048 | tf_op jit(solution)/shard_map/attend_forward/pallas_call | solution.py:189
  155.7 3.7 fusion.87
  162.2 2.6 fusion.89
  164.8 9.3 %convert_reduce_fusion = (f32[1536]{0:T(1024)S(1)}, bf16[1024,1536]{1,0:T(8,128)(2,1)S(1)}, bf16[1024,1536]{1,0:T(8,128)(2,1)S(1)}) fusion(f32[1024,1536]{1,0:T(8,128)S(1)} %fusion.89, f32[1536]{0:T(1024)S(1)} %copy-done.39, bf16[1024,768]{1,0:T(8,128)(2,1)S(1)} %bitcast.127, bf16[1536,768]{1,0:T(8,128)(2,1)S(1)} %copy-done), kind=kOutput, calls=%fused_computation.26 | convolution fusion | flops 2461530624 | bytes 16527360 | tf_op jit(solution)/shard_map/dot_general | solution.py:36
  174.1 4.2 fusion.90
  178.4 2.6 fusion.94
  184.4 4.7 collective-permute-start.32
  189.1 2.8 fusion.96
  191.9 2.6 fusion.91
  197.5 2.6 fusion.48
  200.1 3.6 broadcast_select_fusion.3
  203.7 10.4 %convert_reduce_fusion.1 = (f32[1536]{0:T(1024)}, bf16[1024,1536]{1,0:T(8,128)(2,1)S(1)}) fusion(f32[1024,1536]{1,0:T(8,128)S(1)} %fusion.48, f32[1536]{0:T(1024)S(1)} %copy-done.40, bf16[1024,768]{1,0:T(8,128)(2,1)S(1)} %bitcast.129, bf16[768,768]{1,0:T(8,128)(2,1)S(1)} %get-tuple-element.79, bf16[768,768]{1,0:T(8,128)(2,1)S(1)} %get-tuple-element.78), kind=kOutput, calls=%fused_computation.27 | convolution fusion | flops 2463103488 | bytes 13381632 | tf_op jit(solution)/shard_map/dot_general | solution.py:36
  214.1 3.9 multiply_reduce_fusion
  225.0 26.3 %attend_backward.3 = bf16[3,1584,384]{2,1,0:T(8,128)(2,1)} custom-call(s32[4,2]{1,0:T(4,128)} %pad_add_fusion.1.span_ref, s32[4,2,256]{2,1,0:T(2,128)} %add_add_fusion.4.clean_ref, s32[4,2,128]{2,1,0:T(2,128)} %pad_add_fusion.noisy_ref, bf16[1584,384]{1,0:T(8,128)(2,1)} %get-tuple-element.34.q_ref, bf16[1584,384]{1,0:T(8,128)(2,1)} %get-tuple-element.35.k_ref, ...), custom_call_target="tpu_custom_call" | custom-call | flops 4026531840 | bytes 9732096 | tf_op jit(solution)/shard_map/attend_backward/pallas_call | solution.py:323
  251.3 8.3 %fusion.74 = f32[1584,768,1]{1,0,2:T(8,128)} fusion(bf16[3,1584,384]{2,1,0:T(8,128)(2,1)} %attend_backward.3, bf16[768,3,384]{2,0,1:T(8,128)(2,1)} %param.22), kind=kOutput, calls=%fused_computation.275 | convolution fusion | flops 2802843648 | bytes 10285056 | tf_op jit(solution)/shard_map/crf,cdf->rd/dot_general | solution.py:543
  259.6 5.2 fusion.41
  265.7 3.4 fusion.92
  269.1 4.3 fusion.95
  273.5 5.4 fusion.77
  278.8 26.6 %attend_backward.2 = bf16[3,1584,384]{2,1,0:T(8,128)(2,1)} custom-call(s32[4,2]{1,0:T(4,128)} %pad_add_fusion.1.span_ref, s32[4,2,256]{2,1,0:T(2,128)} %add_add_fusion.4.clean_ref, s32[4,2,128]{2,1,0:T(2,128)} %pad_add_fusion.noisy_ref, bf16[1584,384]{1,0:T(8,128)(2,1)} %get-tuple-element.38.q_ref, bf16[1584,384]{1,0:T(8,128)(2,1)} %get-tuple-element.39.k_ref, ...), custom_call_target="tpu_custom_call" | custom-call | flops 4026531840 | bytes 9732096 | tf_op jit(solution)/shard_map/attend_backward/pallas_call | solution.py:323
  305.4 8.2 %fusion.44 = f32[3,768,384]{1,2,0:T(8,128)} fusion(bf16[3,1584,384]{2,1,0:T(8,128)(2,1)} %attend_backward.2, bf16[1584,768]{1,0:T(8,128)(2,1)} %fusion.24.rows_ref), kind=kOutput, calls=%fused_computation.85 | convolution fusion | flops 2802843648 | bytes 9621504 | tf_op jit(solution)/shard_map/rd,crf->cdf/dot_general | solution.py:540
  313.6 5.3 bitcast_add_fusion
  322.1 44.7 %collective-permute-start.10 = (bf16[528,768]{1,0:T(8,128)(2,1)}, bf16[528,768]{1,0:T(8,128)(2,1)}, u32[]{:S(2)}, u32[]{:S(2)}) collective-permute-start(bf16[528,768]{1,0:T(8,128)(2,1)} %pad_maximum_fusion.13), channel_id=1, source_target_pairs={{0,1},{1,0},{2,3},{3,2},{4,5},{5,4},{6,7},{7,6},{8,9},{9,8},{10,11... | collective-permute-start | bytes 2433032 | tf_op jit(solution)/shard_map/ppermute | solution.py:439
  366.8 5.3 copy.44
  372.1 5.2 copy.43
  377.3 2.6 dynamic-slice_convert_fusion.4
  380.0 2.5 dynamic-slice_convert_fusion.5
  382.7 9.4 %add_convert_fusion = bf16[1024,768]{1,0:T(8,128)(2,1)} fusion(f32[1024,768]{1,0:T(8,128)S(1)} %copy-done.6, f32[1024,768]{1,0:T(8,128)} %fusion.90, f32[768]{0:T(1024)S(1)} %copy-done.48, bf16[768,768]{1,0:T(8,128)(2,1)} %copy-done.30, bf16[768,768]{1,0:T(8,128)(2,1)S(1)} %copy-done.29, f32[1024,1536]{1,0:T(8,128)} %copy-done.49, f32[1536]{0:T(1024)S(1)} %copy-done.42), kind=kOutput, calls=%fused_computation.65 | convolution fusion | flops 2439512064 | bytes 16524288 | tf_op jit(solution)/shard_map/dot_general | solution.py:36
  392.6 3.0 dynamic-slice_convert_fusion.2
  397.7 2.9 dynamic-slice_convert_fusion
  402.4 2.6 collective-permute-done.24
  410.6 19.3 %collective-permute-start.26 = (bf16[48,768]{1,0:T(8,128)(2,1)S(1)}, bf16[48,768]{1,0:T(8,128)(2,1)S(1)}, u32[]{:S(2)}, u32[]{:S(2)}) collective-permute-start(bf16[48,768]{1,0:T(8,128)(2,1)S(1)} %dynamic-slice_convert_fusion.18), channel_id=1, source_target_pairs={{0,8},{2,10},{4,12},{6,14},{8,0},{10,2},{12,4},{14,6},{16,24},{18,... | collective-permute-start | bytes 221192 | tf_op jit(solution)/shard_map/ppermute | solution.py:442
  439.6 3.1 fusion.26
  445.4 3.0 collective-permute-start.28
  448.9 39.7 %psum.7 = f32[6912]{0:T(1024)S(1)} all-reduce(f32[6912]{0:T(1024)} %constant_dynamic-update-slice_fusion.2), channel_id=1, replica_groups=mesh['dp'=16,'mp'=2] {'dp','mp'}, use_global_device_ids=true, to_apply=%region_24.25 | all-reduce | flops 6912 | bytes 55296 | tf_op jit(solution)/shard_map/psum | solution.py:569
  497.0 3.5 collective-permute-done.30
  501.2 12.1 %collective-permute-done.14 = bf16[1152,384]{1,0:T(8,128)(2,1)S(1)} collective-permute-done((bf16[1152,384]{1,0:T(8,128)(2,1)S(1)}, bf16[1152,384]{1,0:T(8,128)(2,1)S(1)}, u32[]{:S(2)}, u32[]{:S(2)}) %collective-permute-start.14) | collective-permute-done | bytes 884768 | tf_op jit(solution)/shard_map/ppermute | solution.py:439
  520.3 7.2 %collective-permute-done.15 = bf16[576,384]{1,0:T(8,128)(2,1)S(1)} collective-permute-done((bf16[576,384]{1,0:T(8,128)(2,1)S(1)}, bf16[576,384]{1,0:T(8,128)(2,1)S(1)}, u32[]{:S(2)}, u32[]{:S(2)}) %collective-permute-start.15) | collective-permute-done | bytes 442400 | tf_op jit(solution)/shard_map/ppermute | solution.py:442
  530.4 5.3 collective-permute-done.16
  536.2 10.8 %collective-permute-done.34 = bf16[384,1536]{1,0:T(8,128)(2,1)S(1)} collective-permute-done((bf16[384,1536]{1,0:T(8,128)(2,1)S(1)}, bf16[384,1536]{1,0:T(8,128)(2,1)S(1)}, u32[]{:S(2)}, u32[]{:S(2)}) %collective-permute-start.34) | collective-permute-done | bytes 1179680 | tf_op jit(solution)/shard_map/ppermute | solution.py:439
  550.4 5.2 collective-permute-done.18
  555.8 15.9 %collective-permute-done.44 = bf16[768,768]{1,0:T(8,128)(2,1)S(1)} collective-permute-done((bf16[768,768]{1,0:T(8,128)(2,1)S(1)}, bf16[768,768]{1,0:T(8,128)(2,1)S(1)}, u32[]{:S(2)}, u32[]{:S(2)}) %collective-permute-start.44) | collective-permute-done | bytes 1179680 | tf_op jit(solution)/shard_map/ppermute | solution.py:439
  574.9 13.4 %collective-permute-done.45 = bf16[384,768]{1,0:T(8,128)(2,1)S(1)} collective-permute-done((bf16[384,768]{1,0:T(8,128)(2,1)S(1)}, bf16[384,768]{1,0:T(8,128)(2,1)S(1)}, u32[]{:S(2)}, u32[]{:S(2)}) %collective-permute-start.45) | collective-permute-done | bytes 589856 | tf_op jit(solution)/shard_map/ppermute | solution.py:442
  590.9 6.7 %collective-permute-done.46 = bf16[192,768]{1,0:T(8,128)(2,1)S(1)} collective-permute-done((bf16[192,768]{1,0:T(8,128)(2,1)S(1)}, bf16[192,768]{1,0:T(8,128)(2,1)S(1)}, u32[]{:S(2)}, u32[]{:S(2)}) %collective-permute-start.46) | collective-permute-done | bytes 294944 | tf_op jit(solution)/shard_map/ppermute | solution.py:442
  598.0 3.0 collective-permute-start.38
  601.0 6.7 %collective-permute-done.47 = bf16[96,768]{1,0:T(8,128)(2,1)S(1)} collective-permute-done((bf16[96,768]{1,0:T(8,128)(2,1)S(1)}, bf16[96,768]{1,0:T(8,128)(2,1)S(1)}, u32[]{:S(2)}, u32[]{:S(2)}) %collective-permute-start.47) | collective-permute-done | bytes 147488 | tf_op jit(solution)/shard_map/ppermute | solution.py:442
  607.8 5.7 collective-permute-done.38
  613.6 2.8 collective-permute-done.48
  616.6 7.0 %collective-permute-done.39 = bf16[96,1536]{1,0:T(8,128)(2,1)S(1)} collective-permute-done((bf16[96,1536]{1,0:T(8,128)(2,1)S(1)}, bf16[96,1536]{1,0:T(8,128)(2,1)S(1)}, u32[]{:S(2)}, u32[]{:S(2)}) %collective-permute-start.39) | collective-permute-done | bytes 294944 | tf_op jit(solution)/shard_map/ppermute | solution.py:442
  624.9 3.0 collective-permute-done.49
  629.0 11.1 %collective-permute-done.40 = bf16[192,1536]{1,0:T(8,128)(2,1)S(1)} collective-permute-done((bf16[192,1536]{1,0:T(8,128)(2,1)S(1)}, bf16[192,1536]{1,0:T(8,128)(2,1)S(1)}, u32[]{:S(2)}, u32[]{:S(2)}) %collective-permute-start.40) | collective-permute-done | bytes 589856 | tf_op jit(solution)/shard_map/ppermute | solution.py:442
  641.0 6.7 %collective-permute-done.50 = bf16[384,768]{1,0:T(8,128)(2,1)S(1)} collective-permute-done((bf16[384,768]{1,0:T(8,128)(2,1)S(1)}, bf16[384,768]{1,0:T(8,128)(2,1)S(1)}, u32[]{:S(2)}, u32[]{:S(2)}) %collective-permute-start.50) | collective-permute-done | bytes 589856 | tf_op jit(solution)/shard_map/ppermute | solution.py:442
  650.6 2.8 maximum_convert_fusion
  653.9 2.5 maximum_convert_fusion.1
  (354 shorter events, 108.8 us)
Async XLA Ops:
  3.7 74.3 %collective-permute-start = (bf16[528,768]{1,0:T(8,128)(2,1)}, bf16[528,768]{1,0:T(8,128)(2,1)}, u32[]{:S(2)}, u32[]{:S(2)}) collective-permute-start(bf16[528,768]{1,0:T(8,128)(2,1)} %pad_maximum_fusion.12), channel_id=1, source_target_pairs={{0,1},{1,0},{2,3},{3,2},{4,5},{5,4},{6,7},{7,6},{8,9},{9,8},{10,11... | collective-permute-start | bytes 2433032 | tf_op jit(solution)/shard_map/ppermute | solution.py:439
  8.9 74.1 %collective-permute-start.1 = (bf16[1152,384]{1,0:T(8,128)(2,1)}, bf16[1152,384]{1,0:T(8,128)(2,1)}, u32[]{:S(2)}, u32[]{:S(2)}) collective-permute-start(bf16[1152,384]{1,0:T(8,128)(2,1)} %constant_dynamic-slice_fusion.3), channel_id=1, source_target_pairs={{0,1},{1,0},{2,3},{3,2},{4,5},{5,4},{6,7},{7,6},{8,9},{9,8},{10,11... | collective-permute-start | bytes 2654216 | tf_op jit(solution)/shard_map/ppermute | solution.py:439
  9.9 41.2 %collective-permute-start.3 = (bf16[192,768]{1,0:T(8,128)(2,1)S(1)}, bf16[192,768]{1,0:T(8,128)(2,1)S(1)}, u32[]{:S(2)}, u32[]{:S(2)}) collective-permute-start(bf16[192,768]{1,0:T(8,128)(2,1)S(1)} %constant_dynamic-slice_fusion.2), channel_id=1, source_target_pairs={{0,1},{1,0},{2,3},{3,2},{4,5},{5,4},{6,7},{7,6},{8,9},{9,8},{10,11... | collective-permute-start | bytes 884744 | tf_op jit(solution)/shard_map/ppermute | solution.py:439
  13.0 105.6 %collective-permute-start.8 = (bf16[768,768]{1,0:T(8,128)(2,1)}, bf16[768,768]{1,0:T(8,128)(2,1)}, u32[]{:S(2)}, u32[]{:S(2)}) collective-permute-start(bf16[768,768]{1,0:T(8,128)(2,1)} %constant_dynamic-slice_fusion), channel_id=1, source_target_pairs={{0,1},{1,0},{2,3},{3,2},{4,5},{5,4},{6,7},{7,6},{8,9},{9,8},{10,11... | collective-permute-start | bytes 3538952 | tf_op jit(solution)/shard_map/ppermute | solution.py:439
  13.1 62.6 %collective-permute-start.7 = (bf16[1536]{0:T(1024)(128)(2,1)S(1)}, bf16[1536]{0:T(1024)(128)(2,1)S(1)}, u32[]{:S(2)}, u32[]{:S(2)}) collective-permute-start(bf16[1536]{0:T(1024)(128)(2,1)S(1)} %copy-done.45), channel_id=1, source_target_pairs={{0,1},{1,0},{2,3},{3,2},{4,5},{5,4},{6,7},{7,6},{8,9},{9,8},{10,11... | collective-permute-start | bytes 9224 | tf_op jit(solution)/shard_map/ppermute | solution.py:439
  51.1 26.9 %collective-permute-start.4 = (bf16[192,768]{1,0:T(8,128)(2,1)S(1)}, bf16[192,768]{1,0:T(8,128)(2,1)S(1)}, u32[]{:S(2)}, u32[]{:S(2)}) collective-permute-start(bf16[192,768]{1,0:T(8,128)(2,1)S(1)} %collective-permute-done.3), channel_id=1, source_target_pairs={{0,2},{2,0},{4,6},{6,4},{8,10},{10,8},{12,14},{14,12},{16,18},{18,... | collective-permute-start | bytes 884744 | tf_op jit(solution)/shard_map/ppermute | solution.py:442
  55.3 24.0 %copy-start.3 = (bf16[2,512,768]{2,1,0:T(8,128)(2,1)S(1)}, bf16[2,512,768]{2,1,0:T(8,128)(2,1)}, u32[]{:S(2)}) copy-start(bf16[2,512,768]{2,1,0:T(8,128)(2,1)} %param.16) | copy-start | bytes 4718596
  75.7 47.7 %collective-permute-start.5 = (bf16[384,1536]{1,0:T(8,128)(2,1)}, bf16[384,1536]{1,0:T(8,128)(2,1)}, u32[]{:S(2)}, u32[]{:S(2)}) collective-permute-start(bf16[384,1536]{1,0:T(8,128)(2,1)} %constant_dynamic-slice_fusion.1), channel_id=1, source_target_pairs={{0,1},{1,0},{2,3},{3,2},{4,5},{5,4},{6,7},{7,6},{8,9},{9,8},{10,11... | collective-permute-start | bytes 3538952 | tf_op jit(solution)/shard_map/ppermute | solution.py:439
  82.9 40.5 %collective-permute-start.2 = (bf16[1152,384]{1,0:T(8,128)(2,1)}, bf16[1152,384]{1,0:T(8,128)(2,1)}, u32[]{:S(2)}, u32[]{:S(2)}) collective-permute-start(bf16[1152,384]{1,0:T(8,128)(2,1)} %collective-permute-done.1), channel_id=1, source_target_pairs={{0,2},{2,0},{4,6},{6,4},{8,10},{10,8},{12,14},{14,12},{16,18},{18,... | collective-permute-start | bytes 2654216 | tf_op jit(solution)/shard_map/ppermute | solution.py:442
  118.6 81.5 %collective-permute-start.9 = (bf16[768,768]{1,0:T(8,128)(2,1)}, bf16[768,768]{1,0:T(8,128)(2,1)}, u32[]{:S(2)}, u32[]{:S(2)}) collective-permute-start(bf16[768,768]{1,0:T(8,128)(2,1)} %collective-permute-done.8), channel_id=1, source_target_pairs={{0,2},{2,0},{4,6},{6,4},{8,10},{10,8},{12,14},{14,12},{16,18},{18,... | collective-permute-start | bytes 3538952 | tf_op jit(solution)/shard_map/ppermute | solution.py:442
  123.3 72.4 %collective-permute-start.6 = (bf16[384,1536]{1,0:T(8,128)(2,1)}, bf16[384,1536]{1,0:T(8,128)(2,1)}, u32[]{:S(2)}, u32[]{:S(2)}) collective-permute-start(bf16[384,1536]{1,0:T(8,128)(2,1)} %collective-permute-done.5), channel_id=1, source_target_pairs={{0,2},{2,0},{4,6},{6,4},{8,10},{10,8},{12,14},{14,12},{16,18},{18,... | collective-permute-start | bytes 3538952 | tf_op jit(solution)/shard_map/ppermute | solution.py:442
  159.4 58.7 %copy-start.5 = (f32[1024,768]{1,0:T(8,128)}, f32[1024,768]{1,0:T(8,128)S(1)}, u32[]{:S(2)}) copy-start(f32[1024,768]{1,0:T(8,128)S(1)} %get-tuple-element.133) | copy-start | bytes 9437188
  162.2 35.3 %copy-start.10 = (bf16[1024,768]{1,0:T(8,128)(2,1)}, bf16[1024,768]{1,0:T(8,128)(2,1)S(1)}, u32[]{:S(2)}) copy-start(bf16[1024,768]{1,0:T(8,128)(2,1)S(1)} %add_convert_fusion.1) | copy-start | bytes 4718596
  184.4 351.8 %collective-permute-start.32 = (bf16[384,1536]{1,0:T(8,128)(2,1)}, bf16[384,1536]{1,0:T(8,128)(2,1)}, u32[]{:S(2)}, u32[]{:S(2)}) collective-permute-start(bf16[384,1536]{1,0:T(8,128)(2,1)} %dynamic-slice_convert_fusion.3), channel_id=1, source_target_pairs={{0,2},{2,0},{4,6},{6,4},{8,10},{10,8},{12,14},{14,12},{16,18},{18,... | collective-permute-start | bytes 3538952 | tf_op jit(solution)/shard_map/ppermute | solution.py:442
  221.2 43.7 %copy-start.12 = (bf16[1024,768]{1,0:T(8,128)(2,1)}, bf16[1024,768]{1,0:T(8,128)(2,1)S(1)}, u32[]{:S(2)}) copy-start(bf16[1024,768]{1,0:T(8,128)(2,1)S(1)} %fusion.47) | copy-start | bytes 4718596
  322.1 88.4 %collective-permute-start.10 = (bf16[528,768]{1,0:T(8,128)(2,1)}, bf16[528,768]{1,0:T(8,128)(2,1)}, u32[]{:S(2)}, u32[]{:S(2)}) collective-permute-start(bf16[528,768]{1,0:T(8,128)(2,1)} %pad_maximum_fusion.13), channel_id=1, source_target_pairs={{0,1},{1,0},{2,3},{3,2},{4,5},{5,4},{6,7},{7,6},{8,9},{9,8},{10,11... | collective-permute-start | bytes 2433032 | tf_op jit(solution)/shard_map/ppermute | solution.py:439
  366.8 33.8 %collective-permute-start.11 = (f32[1536]{0:T(1024)}, f32[1536]{0:T(1024)}, u32[]{:S(2)}, u32[]{:S(2)}) collective-permute-start(f32[1536]{0:T(1024)} %get-tuple-element.135), channel_id=1, source_target_pairs={{0,1},{1,0},{2,3},{3,2},{4,5},{5,4},{6,7},{7,6},{8,9},{9,8},{10,11... | collective-permute-start | bytes 18440 | tf_op jit(solution)/shard_map/ppermute | solution.py:439
  382.5 13.0 %collective-permute-start.23 = (bf16[192,768]{1,0:T(8,128)(2,1)S(1)}, bf16[192,768]{1,0:T(8,128)(2,1)S(1)}, u32[]{:S(2)}, u32[]{:S(2)}) collective-permute-start(bf16[192,768]{1,0:T(8,128)(2,1)S(1)} %dynamic-slice_convert_fusion.11), channel_id=1, source_target_pairs={{0,2},{2,0},{4,6},{6,4},{8,10},{10,8},{12,14},{14,12},{16,18},{18,... | collective-permute-start | bytes 884744 | tf_op jit(solution)/shard_map/ppermute | solution.py:442
  392.1 9.8 %collective-permute-start.22 = (bf16[192,768]{1,0:T(8,128)(2,1)S(1)}, bf16[192,768]{1,0:T(8,128)(2,1)S(1)}, u32[]{:S(2)}, u32[]{:S(2)}) collective-permute-start(bf16[192,768]{1,0:T(8,128)(2,1)S(1)} %dynamic-slice_convert_fusion.12), channel_id=1, source_target_pairs={{0,2},{2,0},{4,6},{6,4},{8,10},{10,8},{12,14},{14,12},{16,18},{18,... | collective-permute-start | bytes 884744 | tf_op jit(solution)/shard_map/ppermute | solution.py:442
  392.6 39.2 %slice-start.2 = ((s8[4866048]{0:T(1024)(128)(4,1)}), s8[4194304]{0:T(1024)(128)(4,1)S(1)}, s32[]{:S(2)}) async-start(s8[4866048]{0:T(1024)(128)(4,1)} %bitcast.136), calls=%async_computation.2 | async-start | bytes 8388608
  395.6 36.2 %slice-start.3 = ((s8[4866048]{0:T(1024)(128)(4,1)}), s8[671744]{0:T(1024)(128)(4,1)S(1)}, s32[]{:S(2)}) async-start(s8[4866048]{0:T(1024)(128)(4,1)} %bitcast.136), calls=%async_computation.3 | async-start | bytes 1343488
  395.7 9.3 %collective-permute-start.24 = (bf16[192,768]{1,0:T(8,128)(2,1)S(1)}, bf16[192,768]{1,0:T(8,128)(2,1)S(1)}, u32[]{:S(2)}, u32[]{:S(2)}) collective-permute-start(bf16[192,768]{1,0:T(8,128)(2,1)S(1)} %add_convert_fusion.5), channel_id=1, source_target_pairs={{0,1},{1,0},{2,3},{3,2},{4,5},{5,4},{6,7},{7,6},{8,9},{9,8},{10,11... | collective-permute-start | bytes 884744 | tf_op jit(solution)/shard_map/ppermute | solution.py:439
  400.6 90.2 %collective-permute-start.13 = (bf16[1152,384]{1,0:T(8,128)(2,1)}, bf16[1152,384]{1,0:T(8,128)(2,1)}, u32[]{:S(2)}, u32[]{:S(2)}) collective-permute-start(bf16[1152,384]{1,0:T(8,128)(2,1)} %dynamic-slice_convert_fusion.4), channel_id=1, source_target_pairs={{0,2},{2,0},{4,6},{6,4},{8,10},{10,8},{12,14},{14,12},{16,18},{18,... | collective-permute-start | bytes 2654216 | tf_op jit(solution)/shard_map/ppermute | solution.py:442
  401.9 98.7 %collective-permute-start.12 = (bf16[1152,384]{1,0:T(8,128)(2,1)}, bf16[1152,384]{1,0:T(8,128)(2,1)}, u32[]{:S(2)}, u32[]{:S(2)}) collective-permute-start(bf16[1152,384]{1,0:T(8,128)(2,1)} %dynamic-slice_convert_fusion.5), channel_id=1, source_target_pairs={{0,2},{2,0},{4,6},{6,4},{8,10},{10,8},{12,14},{14,12},{16,18},{18,... | collective-permute-start | bytes 2654216 | tf_op jit(solution)/shard_map/ppermute | solution.py:442
  405.1 5.4 collective-permute-start.25
  410.5 104.3 %collective-permute-start.33 = (bf16[384,1536]{1,0:T(8,128)(2,1)}, bf16[384,1536]{1,0:T(8,128)(2,1)S(1)}, u32[]{:S(2)}, u32[]{:S(2)}) collective-permute-start(bf16[384,1536]{1,0:T(8,128)(2,1)} %dynamic-slice_convert_fusion.2), channel_id=1, source_target_pairs={{0,2},{2,0},{4,6},{6,4},{8,10},{10,8},{12,14},{14,12},{16,18},{18,... | collective-permute-start | bytes 3538952 | tf_op jit(solution)/shard_map/ppermute | solution.py:442
  410.6 26.3 %collective-permute-start.26 = (bf16[48,768]{1,0:T(8,128)(2,1)S(1)}, bf16[48,768]{1,0:T(8,128)(2,1)S(1)}, u32[]{:S(2)}, u32[]{:S(2)}) collective-permute-start(bf16[48,768]{1,0:T(8,128)(2,1)S(1)} %dynamic-slice_convert_fusion.18), channel_id=1, source_target_pairs={{0,8},{2,10},{4,12},{6,14},{8,0},{10,2},{12,4},{14,6},{16,24},{18,... | collective-permute-start | bytes 221192 | tf_op jit(solution)/shard_map/ppermute | solution.py:442
  436.9 8.4 %collective-permute-start.27 = (bf16[24,768]{1,0:T(8,128)(2,1)S(1)}, bf16[24,768]{1,0:T(8,128)(2,1)S(1)}, u32[]{:S(2)}, u32[]{:S(2)}) collective-permute-start(bf16[24,768]{1,0:T(8,128)(2,1)S(1)} %dynamic-slice_convert_fusion.19), channel_id=1, source_target_pairs={{0,16},{2,18},{4,20},{6,22},{8,24},{10,26},{12,28},{14,30},{16,0},... | collective-permute-start | bytes 110600 | tf_op jit(solution)/shard_map/ppermute | solution.py:442
  445.4 43.3 %collective-permute-start.28 = (bf16[24,768]{1,0:T(8,128)(2,1)S(1)}, bf16[24,768]{1,0:T(8,128)(2,1)S(1)}, u32[]{:S(2)}, u32[]{:S(2)}) collective-permute-start(bf16[24,768]{1,0:T(8,128)(2,1)S(1)} %add_convert_fusion.9), channel_id=1, source_target_pairs={{0,16},{2,18},{4,20},{6,22},{8,24},{10,26},{12,28},{14,30},{16,0},... | collective-permute-start | bytes 110600 | tf_op jit(solution)/shard_map/ppermute | solution.py:442
  488.7 24.6 %copy-start.17 = (f32[3,768,384]{2,1,0:T(8,128)S(1)}, f32[3,768,384]{2,1,0:T(8,128)}, u32[]{:S(2)}) copy-start(f32[3,768,384]{2,1,0:T(8,128)} %copy.43) | copy-start | bytes 10616836
  488.7 6.5 collective-permute-start.29
  490.8 29.2 %slice-start.6 = ((s8[4718592]{0:T(1024)(128)(4,1)}), s8[4194304]{0:T(1024)(128)(4,1)S(1)}, s32[]{:S(2)}) async-start(s8[4718592]{0:T(1024)(128)(4,1)} %bitcast.141), calls=%async_computation.6 | async-start | bytes 8388608
  492.9 20.4 %collective-permute-start.14 = (bf16[1152,384]{1,0:T(8,128)(2,1)S(1)}, bf16[1152,384]{1,0:T(8,128)(2,1)S(1)}, u32[]{:S(2)}, u32[]{:S(2)}) collective-permute-start(bf16[1152,384]{1,0:T(8,128)(2,1)S(1)} %add_convert_fusion.4), channel_id=1, source_target_pairs={{0,1},{1,0},{2,3},{3,2},{4,5},{5,4},{6,7},{7,6},{8,9},{9,8},{10,11... | collective-permute-start | bytes 2654216 | tf_op jit(solution)/shard_map/ppermute | solution.py:439
  495.3 5.2 collective-permute-start.30
  500.5 55.3 %collective-permute-start.42 = (bf16[768,768]{1,0:T(8,128)(2,1)}, bf16[768,768]{1,0:T(8,128)(2,1)S(1)}, u32[]{:S(2)}, u32[]{:S(2)}) collective-permute-start(bf16[768,768]{1,0:T(8,128)(2,1)} %dynamic-slice_convert_fusion.1), channel_id=1, source_target_pairs={{0,2},{2,0},{4,6},{6,4},{8,10},{10,8},{12,14},{14,12},{16,18},{18,... | collective-permute-start | bytes 3538952 | tf_op jit(solution)/shard_map/ppermute | solution.py:442
  500.6 17.6 %collective-permute-start.43 = (bf16[768,768]{1,0:T(8,128)(2,1)S(1)}, bf16[768,768]{1,0:T(8,128)(2,1)S(1)}, u32[]{:S(2)}, u32[]{:S(2)}) collective-permute-start(bf16[768,768]{1,0:T(8,128)(2,1)S(1)} %copy-done.31), channel_id=1, source_target_pairs={{0,2},{2,0},{4,6},{6,4},{8,10},{10,8},{12,14},{14,12},{16,18},{18,... | collective-permute-start | bytes 3538952 | tf_op jit(solution)/shard_map/ppermute | solution.py:442
  513.3 15.5 %collective-permute-start.31 = (bf16[192,768]{1,0:T(8,128)(2,1)S(1)}, bf16[192,768]{1,0:T(8,128)(2,1)S(1)}, u32[]{:S(2)}, u32[]{:S(2)}) collective-permute-start(bf16[192,768]{1,0:T(8,128)(2,1)S(1)} %pad_maximum_fusion.20), channel_id=1, source_target_pairs={{0,2},{2,0},{4,6},{6,4},{8,10},{10,8},{12,14},{14,12},{16,18},{18,... | collective-permute-start | bytes 884744 | tf_op jit(solution)/shard_map/ppermute | solution.py:442
  514.8 12.6 %collective-permute-start.15 = (bf16[576,384]{1,0:T(8,128)(2,1)S(1)}, bf16[576,384]{1,0:T(8,128)(2,1)S(1)}, u32[]{:S(2)}, u32[]{:S(2)}) collective-permute-start(bf16[576,384]{1,0:T(8,128)(2,1)S(1)} %dynamic-slice_convert_fusion.8), channel_id=1, source_target_pairs={{0,4},{2,6},{4,0},{6,2},{8,12},{10,14},{12,8},{14,10},{16,20},{18,... | collective-permute-start | bytes 1327112 | tf_op jit(solution)/shard_map/ppermute | solution.py:442
  516.0 31.0 %slice-start = ((s8[4718592]{0:T(1024)(128)(4,1)}), s8[4194304]{0:T(1024)(128)(4,1)S(1)}, s32[]{:S(2)}) async-start(s8[4718592]{0:T(1024)(128)(4,1)} %bitcast.125), calls=%async_computation | async-start | bytes 8388608
  518.2 28.9 %slice-start.1 = ((s8[4718592]{0:T(1024)(128)(4,1)}), s8[524288]{0:T(1024)(128)(4,1)S(1)}, s32[]{:S(2)}) async-start(s8[4718592]{0:T(1024)(128)(4,1)} %bitcast.125), calls=%async_computation.1 | async-start | bytes 1048576
  518.2 28.9 %collective-permute-start.34 = (bf16[384,1536]{1,0:T(8,128)(2,1)S(1)}, bf16[384,1536]{1,0:T(8,128)(2,1)S(1)}, u32[]{:S(2)}, u32[]{:S(2)}) collective-permute-start(bf16[384,1536]{1,0:T(8,128)(2,1)S(1)} %add_convert_fusion.3), channel_id=1, source_target_pairs={{0,1},{1,0},{2,3},{3,2},{4,5},{5,4},{6,7},{7,6},{8,9},{9,8},{10,11... | collective-permute-start | bytes 3538952 | tf_op jit(solution)/shard_map/ppermute | solution.py:439
  527.5 44.1 %collective-permute-start.44 = (bf16[768,768]{1,0:T(8,128)(2,1)S(1)}, bf16[768,768]{1,0:T(8,128)(2,1)S(1)}, u32[]{:S(2)}, u32[]{:S(2)}) collective-permute-start(bf16[768,768]{1,0:T(8,128)(2,1)S(1)} %add_convert_fusion.2), channel_id=1, source_target_pairs={{0,1},{1,0},{2,3},{3,2},{4,5},{5,4},{6,7},{7,6},{8,9},{9,8},{10,11... | collective-permute-start | bytes 3538952 | tf_op jit(solution)/shard_map/ppermute | solution.py:439
  528.8 6.8 %collective-permute-start.16 = (bf16[288,384]{1,0:T(8,128)(2,1)S(1)}, bf16[288,384]{1,0:T(8,128)(2,1)S(1)}, u32[]{:S(2)}, u32[]{:S(2)}) collective-permute-start(bf16[288,384]{1,0:T(8,128)(2,1)S(1)} %dynamic-slice_convert_fusion.13), channel_id=1, source_target_pairs={{0,8},{2,10},{4,12},{6,14},{8,0},{10,2},{12,4},{14,6},{16,24},{18,... | collective-permute-start | bytes 663560 | tf_op jit(solution)/shard_map/ppermute | solution.py:442
  535.7 35.9 %slice-start.4 = ((s8[4718592]{0:T(1024)(128)(4,1)}), s8[4194304]{0:T(1024)(128)(4,1)S(1)}, s32[]{:S(2)}) async-start(s8[4718592]{0:T(1024)(128)(4,1)} %bitcast.139), calls=%async_computation.4 | async-start | bytes 8388608
  535.7 35.9 %slice-start.5 = ((s8[4718592]{0:T(1024)(128)(4,1)}), s8[524288]{0:T(1024)(128)(4,1)S(1)}, s32[]{:S(2)}) async-start(s8[4718592]{0:T(1024)(128)(4,1)} %bitcast.139), calls=%async_computation.5 | async-start | bytes 1048576
  535.7 13.1 %collective-permute-start.17 = (bf16[144,384]{1,0:T(8,128)(2,1)S(1)}, bf16[144,384]{1,0:T(8,128)(2,1)S(1)}, u32[]{:S(2)}, u32[]{:S(2)}) collective-permute-start(bf16[144,384]{1,0:T(8,128)(2,1)S(1)} %dynamic-slice_convert_fusion.17), channel_id=1, source_target_pairs={{0,16},{2,18},{4,20},{6,22},{8,24},{10,26},{12,28},{14,30},{16,0},... | collective-permute-start | bytes 331784 | tf_op jit(solution)/shard_map/ppermute | solution.py:442
  548.9 6.8 %collective-permute-start.18 = (bf16[144,384]{1,0:T(8,128)(2,1)S(1)}, bf16[144,384]{1,0:T(8,128)(2,1)S(1)}, u32[]{:S(2)}, u32[]{:S(2)}) collective-permute-start(bf16[144,384]{1,0:T(8,128)(2,1)S(1)} %add_convert_fusion.8), channel_id=1, source_target_pairs={{0,16},{2,18},{4,20},{6,22},{8,24},{10,26},{12,28},{14,30},{16,0},... | collective-permute-start | bytes 331784 | tf_op jit(solution)/shard_map/ppermute | solution.py:442
  549.4 24.9 %collective-permute-start.35 = (bf16[192,1536]{1,0:T(8,128)(2,1)S(1)}, bf16[192,1536]{1,0:T(8,128)(2,1)S(1)}, u32[]{:S(2)}, u32[]{:S(2)}) collective-permute-start(bf16[192,1536]{1,0:T(8,128)(2,1)S(1)} %dynamic-slice_convert_fusion.7), channel_id=1, source_target_pairs={{0,4},{2,6},{4,0},{6,2},{8,12},{10,14},{12,8},{14,10},{16,20},{18,... | collective-permute-start | bytes 1769480 | tf_op jit(solution)/shard_map/ppermute | solution.py:442
  555.7 17.3 %collective-permute-start.19 = (bf16[288,384]{1,0:T(8,128)(2,1)S(1)}, bf16[288,384]{1,0:T(8,128)(2,1)S(1)}, u32[]{:S(2)}, u32[]{:S(2)}) collective-permute-start(bf16[288,384]{1,0:T(8,128)(2,1)S(1)} %pad_maximum_fusion.23), channel_id=1, source_target_pairs={{0,8},{2,10},{4,12},{6,14},{8,0},{10,2},{12,4},{14,6},{16,24},{18,... | collective-permute-start | bytes 663560 | tf_op jit(solution)/shard_map/ppermute | solution.py:442
  572.0 16.3 %collective-permute-start.45 = (bf16[384,768]{1,0:T(8,128)(2,1)S(1)}, bf16[384,768]{1,0:T(8,128)(2,1)S(1)}, u32[]{:S(2)}, u32[]{:S(2)}) collective-permute-start(bf16[384,768]{1,0:T(8,128)(2,1)S(1)} %dynamic-slice_convert_fusion.6), channel_id=1, source_target_pairs={{0,4},{2,6},{4,0},{6,2},{8,12},{10,14},{12,8},{14,10},{16,20},{18,... | collective-permute-start | bytes 1769480 | tf_op jit(solution)/shard_map/ppermute | solution.py:442
  573.2 24.6 %collective-permute-start.20 = (bf16[576,384]{1,0:T(8,128)(2,1)S(1)}, bf16[576,384]{1,0:T(8,128)(2,1)S(1)}, u32[]{:S(2)}, u32[]{:S(2)}) collective-permute-start(bf16[576,384]{1,0:T(8,128)(2,1)S(1)} %pad_maximum_fusion.17), channel_id=1, source_target_pairs={{0,4},{2,6},{4,0},{6,2},{8,12},{10,14},{12,8},{14,10},{16,20},{18,... | collective-permute-start | bytes 1327112 | tf_op jit(solution)/shard_map/ppermute | solution.py:442
  574.5 14.4 %collective-permute-start.36 = (bf16[96,1536]{1,0:T(8,128)(2,1)S(1)}, bf16[96,1536]{1,0:T(8,128)(2,1)S(1)}, u32[]{:S(2)}, u32[]{:S(2)}) collective-permute-start(bf16[96,1536]{1,0:T(8,128)(2,1)S(1)} %dynamic-slice_convert_fusion.10), channel_id=1, source_target_pairs={{0,8},{2,10},{4,12},{6,14},{8,0},{10,2},{12,4},{14,6},{16,24},{18,... | collective-permute-start | bytes 884744 | tf_op jit(solution)/shard_map/ppermute | solution.py:442
  588.5 9.0 %collective-permute-start.46 = (bf16[192,768]{1,0:T(8,128)(2,1)S(1)}, bf16[192,768]{1,0:T(8,128)(2,1)S(1)}, u32[]{:S(2)}, u32[]{:S(2)}) collective-permute-start(bf16[192,768]{1,0:T(8,128)(2,1)S(1)} %dynamic-slice_convert_fusion.9), channel_id=1, source_target_pairs={{0,8},{2,10},{4,12},{6,14},{8,0},{10,2},{12,4},{14,6},{16,24},{18,... | collective-permute-start | bytes 884744 | tf_op jit(solution)/shard_map/ppermute | solution.py:442
  589.0 8.9 %collective-permute-start.37 = (bf16[48,1536]{1,0:T(8,128)(2,1)S(1)}, bf16[48,1536]{1,0:T(8,128)(2,1)S(1)}, u32[]{:S(2)}, u32[]{:S(2)}) collective-permute-start(bf16[48,1536]{1,0:T(8,128)(2,1)S(1)} %dynamic-slice_convert_fusion.15), channel_id=1, source_target_pairs={{0,16},{2,18},{4,20},{6,22},{8,24},{10,26},{12,28},{14,30},{16,0},... | collective-permute-start | bytes 442376 | tf_op jit(solution)/shard_map/ppermute | solution.py:442
  597.7 10.0 %collective-permute-start.47 = (bf16[96,768]{1,0:T(8,128)(2,1)S(1)}, bf16[96,768]{1,0:T(8,128)(2,1)S(1)}, u32[]{:S(2)}, u32[]{:S(2)}) collective-permute-start(bf16[96,768]{1,0:T(8,128)(2,1)S(1)} %dynamic-slice_convert_fusion.14), channel_id=1, source_target_pairs={{0,16},{2,18},{4,20},{6,22},{8,24},{10,26},{12,28},{14,30},{16,0},... | collective-permute-start | bytes 442376 | tf_op jit(solution)/shard_map/ppermute | solution.py:442
  598.0 15.5 %collective-permute-start.38 = (bf16[48,1536]{1,0:T(8,128)(2,1)S(1)}, bf16[48,1536]{1,0:T(8,128)(2,1)S(1)}, u32[]{:S(2)}, u32[]{:S(2)}) collective-permute-start(bf16[48,1536]{1,0:T(8,128)(2,1)S(1)} %add_convert_fusion.7), channel_id=1, source_target_pairs={{0,16},{2,18},{4,20},{6,22},{8,24},{10,26},{12,28},{14,30},{16,0},... | collective-permute-start | bytes 442376 | tf_op jit(solution)/shard_map/ppermute | solution.py:442
  607.7 8.7 %collective-permute-start.48 = (bf16[96,768]{1,0:T(8,128)(2,1)S(1)}, bf16[96,768]{1,0:T(8,128)(2,1)S(1)}, u32[]{:S(2)}, u32[]{:S(2)}) collective-permute-start(bf16[96,768]{1,0:T(8,128)(2,1)S(1)} %add_convert_fusion.6), channel_id=1, source_target_pairs={{0,16},{2,18},{4,20},{6,22},{8,24},{10,26},{12,28},{14,30},{16,0},... | collective-permute-start | bytes 442376 | tf_op jit(solution)/shard_map/ppermute | solution.py:442
  613.5 10.0 %collective-permute-start.39 = (bf16[96,1536]{1,0:T(8,128)(2,1)S(1)}, bf16[96,1536]{1,0:T(8,128)(2,1)S(1)}, u32[]{:S(2)}, u32[]{:S(2)}) collective-permute-start(bf16[96,1536]{1,0:T(8,128)(2,1)S(1)} %pad_maximum_fusion.21), channel_id=1, source_target_pairs={{0,8},{2,10},{4,12},{6,14},{8,0},{10,2},{12,4},{14,6},{16,24},{18,... | collective-permute-start | bytes 884744 | tf_op jit(solution)/shard_map/ppermute | solution.py:442
  616.5 11.3 %collective-permute-start.49 = (bf16[192,768]{1,0:T(8,128)(2,1)S(1)}, bf16[192,768]{1,0:T(8,128)(2,1)S(1)}, u32[]{:S(2)}, u32[]{:S(2)}) collective-permute-start(bf16[192,768]{1,0:T(8,128)(2,1)S(1)} %pad_maximum_fusion.22), channel_id=1, source_target_pairs={{0,8},{2,10},{4,12},{6,14},{8,0},{10,2},{12,4},{14,6},{16,24},{18,... | collective-permute-start | bytes 884744 | tf_op jit(solution)/shard_map/ppermute | solution.py:442
  623.7 16.3 %collective-permute-start.40 = (bf16[192,1536]{1,0:T(8,128)(2,1)S(1)}, bf16[192,1536]{1,0:T(8,128)(2,1)S(1)}, u32[]{:S(2)}, u32[]{:S(2)}) collective-permute-start(bf16[192,1536]{1,0:T(8,128)(2,1)S(1)} %pad_maximum_fusion.15), channel_id=1, source_target_pairs={{0,4},{2,6},{4,0},{6,2},{8,12},{10,14},{12,8},{14,10},{16,20},{18,... | collective-permute-start | bytes 1769480 | tf_op jit(solution)/shard_map/ppermute | solution.py:442
  624.8 15.7 %collective-permute-start.21 = (bf16[1152,384]{1,0:T(8,128)(2,1)S(1)}, bf16[1152,384]{1,0:T(8,128)(2,1)S(1)}, u32[]{:S(2)}, u32[]{:S(2)}) collective-permute-start(bf16[1152,384]{1,0:T(8,128)(2,1)S(1)} %pad_maximum_fusion.11), channel_id=1, source_target_pairs={{0,2},{2,0},{4,6},{6,4},{8,10},{10,8},{12,14},{14,12},{16,18},{18,... | collective-permute-start | bytes 2654216 | tf_op jit(solution)/shard_map/ppermute | solution.py:442
  628.0 19.7 %collective-permute-start.50 = (bf16[384,768]{1,0:T(8,128)(2,1)S(1)}, bf16[384,768]{1,0:T(8,128)(2,1)S(1)}, u32[]{:S(2)}, u32[]{:S(2)}) collective-permute-start(bf16[384,768]{1,0:T(8,128)(2,1)S(1)} %pad_maximum_fusion.16), channel_id=1, source_target_pairs={{0,4},{2,6},{4,0},{6,2},{8,12},{10,14},{12,8},{14,10},{16,20},{18,... | collective-permute-start | bytes 1769480 | tf_op jit(solution)/shard_map/ppermute | solution.py:442
  640.4 9.8 %collective-permute-start.41 = (bf16[384,1536]{1,0:T(8,128)(2,1)S(1)}, bf16[384,1536]{1,0:T(8,128)(2,1)S(1)}, u32[]{:S(2)}, u32[]{:S(2)}) collective-permute-start(bf16[384,1536]{1,0:T(8,128)(2,1)S(1)} %pad_maximum_fusion.9), channel_id=1, source_target_pairs={{0,2},{2,0},{4,6},{6,4},{8,10},{10,8},{12,14},{14,12},{16,18},{18,... | collective-permute-start | bytes 3538952 | tf_op jit(solution)/shard_map/ppermute | solution.py:442
  648.0 5.4 collective-permute-start.51
  (50 other events, 316.0 us)

commit v2 on v1

--- a/solution.py
+++ b/solution.py
@@ -220,13 +220,15 @@
     lse_ref,
     cos_ref,
     sin_ref,
+    rows_ref,
     out_ref,
+    grad_ref,
     dk_ref,
     dv_ref,
 ):
     dk_ref[...] = jnp.zeros_like(dk_ref)
     dv_ref[...] = jnp.zeros_like(dv_ref)
-    out_ref[0] = jnp.zeros_like(out_ref[0])
+    out_ref[:, :LANES] = jnp.zeros((KEY_ROWS, LANES), bf16)
 
     def one_tile(t, _):
         clean_at = pl.multiple_of(CLEAN_OWN + t * TILE, TILE)
@@ -293,7 +295,7 @@
         d_query = jnp.concatenate(d_query, axis=0).T
         for at, part in ((noisy_at, d_query[:TILE]), (clean_at, d_query[TILE:])):
             turned = turn(part, cos_ref[pl.ds(at, TILE), :], -sin_ref[pl.ds(at, TILE), :])
-            out_ref[0, pl.ds(at, TILE), :] = turned.astype(bf16)
+            out_ref[pl.ds(at, TILE), :LANES] = turned.astype(bf16)
         return 0
 
     lax.fori_loop(0, TILES, one_tile, 0)
@@ -301,45 +303,72 @@
 
     def finish(i, _):
         rows = pl.ds(pl.multiple_of(i * step, EDGE), step)
-        out_ref[1, rows, :] = turn(dk_ref[rows, :], cos_ref[rows, :], -sin_ref[rows, :]).astype(
-            bf16
-        )
-        out_ref[2, rows, :] = dv_ref[rows, :].astype(bf16)
+        out_ref[rows, LANES : 2 * LANES] = turn(
+            dk_ref[rows, :], cos_ref[rows, :], -sin_ref[rows, :]
+        ).astype(bf16)
+        out_ref[rows, 2 * LANES :] = dv_ref[rows, :].astype(bf16)
         return 0
 
     lax.fori_loop(0, 9, finish, 0)
 
+    def weight_rows(i, _):
+        rows = pl.ds(pl.multiple_of(i * LANES, LANES), LANES)
+        grad = dot(rows_ref[rows, :], out_ref[...])
+        for c in range(3):
+            grad_ref[c, rows, :] = grad[:, c * LANES : (c + 1) * LANES]
+        return 0
+
+    lax.fori_loop(0, rows_ref.shape[0] // LANES, weight_rows, 0)
+
 
 def attend_backward(
-    spans, clean_bounds, noisy_bounds, query, keys, values, attended, d_attended, lse, cosine, sine
+    pair,
+    spans,
+    clean_bounds,
+    noisy_bounds,
+    query,
+    keys,
+    values,
+    attended,
+    d_attended,
+    lse,
+    cosine,
+    sine,
+    rows_t,
 ):
-    count, cols = query.shape
-    pairs = cols // LANES
-    whole2 = lambda array: pl.BlockSpec(array.shape, lambda p, s: (0, 0))
-    whole3 = lambda array: pl.BlockSpec(array.shape, lambda p, s: (0, 0, 0))
-    row_spec = pl.BlockSpec((count, LANES), lambda p, s: (0, p))
-    own_spec = pl.BlockSpec((TOK_DEV, LANES), lambda p, s: (0, p))
-    work = pairs * 2 * 2 * HALF * TOK_DEV
+    count = query.shape[0]
+    width = rows_t.shape[0]
+    whole2 = lambda array: pl.BlockSpec(array.shape, lambda i, s: (0, 0))
+    whole3 = lambda array: pl.BlockSpec(array.shape, lambda i, s: (0, 0, 0))
+    row_spec = pl.BlockSpec((count, LANES), lambda i, s: (0, pair))
+    own_spec = pl.BlockSpec((TOK_DEV, LANES), lambda i, s: (0, pair))
     return pl.pallas_call(
         backward_kernel,
         grid_spec=pltpu.PrefetchScalarGridSpec(
             num_scalar_prefetch=1,
-            grid=(pairs,),
+            grid=(1,),
             in_specs=[whole3(clean_bounds), whole3(noisy_bounds)]
             + [row_spec] * 3
             + [own_spec] * 2
             + [
-                pl.BlockSpec((1, TILES, 2, 2 * TILE), lambda p, s: (p, 0, 0, 0)),
+                pl.BlockSpec((1, TILES, 2, 2 * TILE), lambda i, s: (pair, 0, 0, 0)),
                 whole2(cosine),
                 whole2(sine),
+                whole2(rows_t),
             ],
-            out_specs=pl.BlockSpec((3, count, LANES), lambda p, s: (0, 0, p)),
+            out_specs=[
+                pl.BlockSpec((count, 3 * LANES), lambda i, s: (0, 0)),
+                pl.BlockSpec((3, width, LANES), lambda i, s: (0, 0, 0)),
+            ],
             scratch_shapes=[pltpu.VMEM((count, LANES), f32)] * 2,
         ),
-        out_shape=jax.ShapeDtypeStruct((3, count, cols), bf16),
+        out_shape=[
+            jax.ShapeDtypeStruct((count, 3 * LANES), bf16),
+            jax.ShapeDtypeStruct((3, width, LANES), f32),
+        ],
         name="attend_backward",
         cost_estimate=pl.CostEstimate(
-            flops=10 * work * HD, bytes_accessed=16 * count * cols, transcendentals=work
+            flops=12 * 10**9, bytes_accessed=12 * 10**6, transcendentals=2 * 10**6
         ),
     )(
         spans,
@@ -353,7 +382,36 @@
         lse,
         cosine,
         sine,
-    )
+        rows_t,
+    )
+
+
+def rows_back_kernel(*refs):
+    *grads, weights, out_ref = refs
+    total = dot(grads[0][...], weights[0], NT)
+    for i, grad in enumerate(grads[1:]):
+        total = total + dot(grad[...], weights[i + 1], NT)
+    out_ref[...] = total
+
+
+def rows_back(grads, weights):
+    count, cols = grads[0].shape
+    step = count // 9
+    width = weights.shape[1]
+    return pl.pallas_call(
+        rows_back_kernel,
+        grid=(9,),
+        in_specs=[pl.BlockSpec((step, cols), lambda i: (i, 0))] * len(grads)
+        + [pl.BlockSpec(weights.shape, lambda i: (0, 0, 0))],
+        out_specs=pl.BlockSpec((step, width), lambda i: (i, 0)),
+        out_shape=jax.ShapeDtypeStruct((count, width), f32),
+        name="rows_back",
+        cost_estimate=pl.CostEstimate(
+            flops=2 * count * cols * width * len(grads),
+            bytes_accessed=16 * 10**6,
+            transcendentals=0,
+        ),
+    )(*grads, weights)
 
 
 def key_layout(seq_lengths, block_len, part):
@@ -408,6 +466,22 @@
     return jnp.concatenate(
         [jnp.where(flip, mine, theirs), jnp.where(flip, theirs, mine)], axis=0
     )
+
+
+def low(array):
+    return array.astype(bf16)
+
+
+class Job:
+    def __init__(self, steps):
+        self.steps = steps
+        self.pending = None
+        self.result = None
+        self.routes = None
+
+
+def tie(first, second):
+    return lax.optimization_barrier((first, second))
 
 
 def local(
@@ -431,46 +505,108 @@
     part = lax.axis_index("mp")
     place = lax.axis_index("dp")
     bits = dp_size.bit_length() - 1
-    across = [(0, 1), (1, 0)]
-    flips = [[(i, i ^ (1 << b)) for i in range(dp_size)] for b in range(bits)]
     my_bit = [(place >> b) & 1 for b in range(bits)]
 
-    def to_partner(array):
-        return lax.ppermute(array, "mp", across)
-
-    def to_flip(array, b):
-        return lax.ppermute(array, "dp", flips[b])
-
-    def fetch(weights):
-        here = to_partner(half_of(weights, my_bit[0]))
-        there = to_flip(here, 0)
-        return in_order(my_bit[0], here, there)
-
-    def reduce_over_all(mine, others):
+    def send(array, route):
+        mask, cross = route
+        if cross:
+            return lax.ppermute(array, "mp", [(0, 1), (1, 0)])
+        return lax.ppermute(array, "dp", [(i, i ^ mask) for i in range(dp_size)])
+
+    across, sibling, beside = (0, 1), (1, 0), (2, 0)
+
+    def fetch(half):
+        here = send(half, across)
+        return here, send(here, sibling)
+
+    def cross_steps(others):
         core = my_bit[0]
-        got = to_flip(half_of(others, 1 - core).astype(bf16), 0)
-        crossing = half_of(others, core) + got.astype(f32)
-        got_own = to_flip(half_of(mine, 1 - core).astype(bf16), 0)
-        total = half_of(mine, core) + got_own.astype(f32)
-        total = total + to_partner(crossing.astype(bf16)).astype(f32)
-        for b in range(1, bits):
-            got = to_flip(half_of(total, 1 - my_bit[b]).astype(bf16), b)
-            total = half_of(total, my_bit[b]) + got.astype(f32)
-        total = total.astype(bf16)
-        for b in reversed(range(bits)):
-            total = in_order(my_bit[b], total, to_flip(total, b))
-        return total.astype(f32)
-
+        (got,) = yield [(low(half_of(others, 1 - core)), sibling)]
+        (got,) = yield [(low(half_of(others, core) + got.astype(f32)), across)]
+        return got
+
+    def sum_steps(mine, crossed):
+        core = my_bit[0]
+        (got,) = yield [(low(half_of(mine, 1 - core)), sibling)]
+        total = half_of(mine, core) + got.astype(f32) + crossed().astype(f32)
+        (got,) = yield [(low(half_of(total, 1 - my_bit[1])), beside)]
+        total = half_of(total, my_bit[1]) + got.astype(f32)
+        spans = [(b, min(2, bits - b)) for b in range(2, bits, 2)]
+        for b, n in spans:
+            size = total.shape[0] >> n
+            spot = (place >> b) & ((1 << n) - 1)
+            piece = lambda s: lax.dynamic_slice_in_dim(total, s * size, size, 0)
+            got = yield [(low(piece(spot ^ k)), (k << b, 0)) for k in range(1, 1 << n)]
+            total = piece(spot)
+            for item in got:
+                total = total + item.astype(f32)
+        total = low(total)
+        for b, n in reversed(spans):
+            got = yield [(total, (k << b, 0)) for k in range(1, 1 << n)]
+            if n == 1:
+                total = in_order(my_bit[b], total, got[0])
+            else:
+                total = in_order(
+                    my_bit[b + 1],
+                    in_order(my_bit[b], total, got[0]),
+                    in_order(my_bit[b], got[1], got[2]),
+                )
+        (got,) = yield [(total, beside)]
+        total = in_order(my_bit[1], total, got)
+        (got,) = yield [(total, sibling)]
+        return in_order(my_bit[0], total, got).astype(f32)
+
+    def small_steps(mine, others):
+        (got,) = yield [(others, across)]
+        total = mine + got
+        for b in range(bits):
+            (got,) = yield [(total, (1 << b, 0))]
+            total = total + got
+        return total
+
+    def advance(after, before, jobs):
+        arrived = [job.pending for job in jobs]
+        after, arrived = tie(after, arrived)
+        outgoing = []
+        for job, got in zip(jobs, arrived):
+            job.pending = None
+            try:
+                orders = job.steps.send(got)
+                job.routes = [route for _, route in orders]
+                outgoing.append([array for array, _ in orders])
+            except StopIteration as stop:
+                job.result = stop.value
+                job.routes = []
+                outgoing.append([])
+        before, outgoing = tie(before, outgoing)
+        for job, arrays in zip(jobs, outgoing):
+            job.pending = [send(array, route) for array, route in zip(arrays, job.routes)]
+        return before
+
+    def finish(job):
+        if job.result is None:
+            while True:
+                try:
+                    orders = job.steps.send(job.pending)
+                except StopIteration as stop:
+                    job.result = stop.value
+                    break
+                job.pending = [send(array, route) for array, route in orders]
+        return job.result
+
+    core = my_bit[0]
     edge = jnp.where(part == 0, tokens[0, HALF - EDGE :], tokens[0, :EDGE])
-    context = to_partner(jnp.concatenate([tokens[1], edge], axis=0))
+    context = send(jnp.concatenate([tokens[1], edge], axis=0), across)
     qkv_mine = w_qkv.transpose(1, 0, 2)
-    qkv_other = fetch(w_qkv.transpose(1, 0, 2).reshape(-1, w_qkv.shape[2])).reshape(
-        qkv_mine.shape
-    )
-    out_other = fetch(w_out)
-    up_other = fetch(w_up)
-    bias_other = to_partner(b_up)
-    down_other = fetch(w_down)
+    halves = [
+        half_of(qkv_mine.reshape(-1, w_qkv.shape[2]), core),
+        half_of(w_out, core),
+        half_of(w_up, core),
+        half_of(w_down, core),
+    ]
+    context, halves = tie(context, halves)
+    fetched = [fetch(half) for half in halves]
+    bias_other = send(b_up, across)
 
     spans, clean_bounds, noisy_bounds, cosine, sine = key_layout(lengths[0], block_size[0], part)
     clean_other, edge_other = context[:HALF], context[HALF:]
@@ -478,37 +614,54 @@
         [clean_other, tokens[1], clean_other[:EDGE], edge_other, tokens[0], edge_other], axis=0
     )
     normed1_keys = layer_norm(key_tokens.astype(f32), ln1_gain, ln1_bias).astype(bf16)
-
-    saved = []
-    for weights in (qkv_mine, qkv_other):
+    normed1_t = normed1_keys.T
+
+    def attention(weights):
         query, keys, values = project(normed1_keys, weights, cosine, sine)
         attended, lse = attend_forward(spans, clean_bounds, noisy_bounds, query, keys, values)
-        saved.append((query, keys, values, attended, lse))
+        return (query, keys, values, attended, lse)
+
+    mine = attention(qkv_mine)
+    fetched[0] = tie(fetched[0], mine[3])[0]
+    qkv_other = in_order(core, *fetched[0]).reshape(qkv_mine.shape)
+    other = attention(qkv_other)
+    fetched[1:] = tie(fetched[1:], other[3])[0]
+    out_other, up_other, down_other = [in_order(core, *pieces) for pieces in fetched[1:]]
+    saved = (mine, other)
 
     x_rows = tokens.astype(f32).reshape(TOK_DEV, width)
-    branch = dot(saved[0][3], w_out) + dot(saved[1][3], out_other)
+    branch = dot(mine[3], w_out) + dot(other[3], out_other)
     mid = x_rows + branch
     normed2, norm2_back = jax.vjp(layer_norm, mid, ln2_gain, ln2_bias)
     mlp_rows = normed2.astype(bf16)
     d_low = cotangent.reshape(TOK_DEV, width)
     d_out_rows = d_low.astype(f32)
     grad_b_down = jnp.sum(d_out_rows, axis=0)
-    down = 0.0
-    d_normed2 = 0.0
-    grad_down, grad_up, grad_up_bias = [], [], []
-    for up, bias, down_w in ((w_up, b_up, w_down), (up_other, bias_other, down_other)):
+
+    def hidden_units(mlp_rows, d_low, up, bias, down_w):
         pre = dot(mlp_rows, up) + bias.astype(f32)
         act_low = gelu_tanh(pre).astype(bf16)
-        down = down + dot(act_low, down_w)
+        down = dot(act_low, down_w)
         d_act = dot(d_low, down_w, NT)
         d_pre = jax.vjp(gelu_tanh, pre)[1](d_act)[0].astype(bf16)
-        grad_down.append(jnp.einsum("rf,rd->fd", act_low, d_low, preferred_element_type=f32))
-        grad_up.append(jnp.einsum("rd,rf->df", mlp_rows, d_pre, preferred_element_type=f32))
-        grad_up_bias.append(jnp.sum(d_pre.astype(f32), axis=0))
-        d_normed2 = d_normed2 + dot(d_pre, up, NT)
-    out = (mid + down + b_down).astype(bf16).reshape(tokens.shape)
-    grad_down = reduce_over_all(*grad_down)
-    grad_up = reduce_over_all(*grad_up)
+        grad_down = jnp.einsum("rf,rd->fd", act_low, d_low, preferred_element_type=f32)
+        grad_up = jnp.einsum("rd,rf->df", mlp_rows, d_pre, preferred_element_type=f32)
+        grad_bias = jnp.sum(d_pre.astype(f32), axis=0)
+        return down, dot(d_pre, up, NT), grad_down, grad_up, grad_bias
+
+    down2, d_two, down_o, up_o, bias_o = hidden_units(
+        mlp_rows, d_low, up_other, bias_other, down_other
+    )
+    down_cross, up_cross = Job(cross_steps(down_o)), Job(cross_steps(up_o))
+    rows_here, d_here = advance(
+        [d_two, down2], (mlp_rows, d_low), [down_cross, up_cross]
+    )
+    down1, d_one, down_m, up_m, bias_m = hidden_units(rows_here, d_here, w_up, b_up, w_down)
+    out = (mid + (down1 + down2) + b_down).astype(bf16).reshape(tokens.shape)
+    d_normed2 = d_one + d_two
+    down_sum = Job(sum_steps(down_m, lambda: down_cross.result))
+    up_sum = Job(sum_steps(up_m, lambda: up_cross.result))
+    d_normed2 = advance([d_normed2], d_normed2, [down_cross, up_cross, down_sum, up_sum])
 
     d_mid_norm, grad_ln2_gain, grad_ln2_bias = norm2_back(d_normed2)
     d_mid = d_out_rows + d_mid_norm
@@ -518,37 +671,78 @@
     for item, weights in zip(saved, (w_out, out_other)):
         grad_out.append(jnp.einsum("rf,rd->fd", item[3], d_branch, preferred_element_type=f32))
         d_attended.append(dot(d_branch, weights, NT).astype(bf16))
-    grad_out = reduce_over_all(*grad_out)
-
-    grad_qkv = [None, None]
-    d_normed1_keys = 0.0
-    for group, weights in ((1, qkv_other), (0, qkv_mine)):
+    out_cross = Job(cross_steps(grad_out[1]))
+    out_sum = Job(sum_steps(grad_out[0], lambda: out_cross.result))
+    norms = jnp.concatenate([grad_ln2_gain, grad_ln2_bias, grad_b_down])
+    small = Job(
+        small_steps(
+            jnp.concatenate([bias_m, norms]), jnp.concatenate([bias_o, norms])
+        )
+    )
+    pairs = mine[0].shape[1] // LANES
+    qkv_cross, qkv_sum = [], []
+    plan = [
+        [out_cross, out_sum, small],
+        [down_cross, down_sum, out_cross, small],
+        [up_cross, up_sum, down_sum, small, "cross"],
+        [down_sum, up_sum, out_cross, out_sum, small, "cross"],
+        [down_sum, up_sum, out_sum, small, "cross", "sum"],
+        [down_sum, up_sum, out_sum, small, "cross", "sum"],
+        [down_sum, up_sum, out_sum, small, "cross", "sum"],
+    ]
+    token = spans
+    token = advance(d_attended, token, plan[0])
+    d_qkv = [[], []]
+    grad_qkv = [[], []]
+    turn_at = 0
+    for group in (1, 0):
         query, keys, values, attended, lse = saved[group]
-        d_qkv = attend_backward(
-            spans,
-            clean_bounds,
-            noisy_bounds,
-            query,
-            keys,
-            values,
-            attended,
-            d_attended[group],
-            lse,
-            cosine,
-            sine,
-        )
-        grad_qkv[group] = jnp.einsum(
-            "rd,crf->cdf", normed1_keys, d_qkv, preferred_element_type=f32
-        ).reshape(-1, d_qkv.shape[2])
-        d_normed1_keys = d_normed1_keys + jnp.einsum(
-            "crf,cdf->rd", d_qkv, weights, preferred_element_type=f32
-        )
-    grad_qkv = reduce_over_all(*grad_qkv).reshape(qkv_mine.shape).transpose(1, 0, 2)
-
+        for pair in range(pairs):
+            d_fields, grad = attend_backward(
+                pair,
+                token,
+                clean_bounds,
+                noisy_bounds,
+                query,
+                keys,
+                values,
+                attended,
+                d_attended[group],
+                lse,
+                cosine,
+                sine,
+                normed1_t,
+            )
+            d_qkv[group].append(d_fields)
+            turn_at += 1
+            flat = grad.reshape(-1, LANES)
+            if group == 1:
+                qkv_cross.append(Job(cross_steps(flat)))
+            else:
+                cross = qkv_cross[pair]
+                qkv_sum.append(Job(sum_steps(flat, lambda cross=cross: cross.result)))
+            jobs = []
+            for item in plan[turn_at]:
+                if item == "cross":
+                    jobs += [job for job in qkv_cross if job.result is None]
+                elif item == "sum":
+                    jobs += qkv_sum
+                elif item.result is None:
+                    jobs.append(item)
+            token = advance([d_fields], token, jobs)
+
+    def by_pair(weights):
+        split = weights.reshape(3, width, pairs, LANES)
+        return split.transpose(2, 1, 0, 3).reshape(pairs, width, 3 * LANES)
+
+    d_normed1_keys = rows_back(
+        d_qkv[0] + d_qkv[1],
+        jnp.concatenate([by_pair(qkv_mine), by_pair(qkv_other)], axis=0),
+    )
     clean_back = d_normed1_keys[:HALF]
     clean_back = clean_back.at[:EDGE].add(d_normed1_keys[2 * HALF : 2 * HALF + EDGE])
     edge_back = d_normed1_keys[NOISY_BASE:NOISY_OWN] + d_normed1_keys[NOISY_OWN + HALF :]
-    back = to_partner(jnp.concatenate([clean_back, edge_back], axis=0).astype(bf16)).astype(f32)
+    back = send(low(jnp.concatenate([clean_back, edge_back], axis=0)), across).astype(f32)
     at_end = jnp.concatenate([jnp.zeros((HALF - EDGE, width), f32), back[HALF:]], axis=0)
     at_start = jnp.concatenate([back[HALF:], jnp.zeros((HALF - EDGE, width), f32)], axis=0)
     d_normed1 = jnp.concatenate(
@@ -562,31 +756,29 @@
     norm1_back = jax.vjp(layer_norm, x_rows, ln1_gain, ln1_bias)[1]
     d_x_norm, grad_ln1_gain, grad_ln1_bias = norm1_back(d_normed1)
     grad_tokens = (d_mid + d_x_norm).reshape(tokens.shape)
-
-    bias_sum = to_partner(grad_up_bias[1]) + grad_up_bias[0]
-    hidden = bias_sum.shape[0]
-    own_bias = jnp.concatenate([jnp.where(part == 0, bias_sum, 0.0), jnp.where(part == 0, 0.0, bias_sum)])
-    small = lax.psum(
-        jnp.concatenate(
-            [own_bias, grad_ln1_gain, grad_ln1_bias, grad_ln2_gain, grad_ln2_bias, grad_b_down]
-        ),
-        ("dp", "mp"),
-    )
-    grad_up_bias = lax.dynamic_slice_in_dim(small, part * hidden, hidden, 0)
-    rest = [small[2 * hidden + i * width : 2 * hidden + (i + 1) * width] for i in range(5)]
+    norms1 = jnp.concatenate([grad_ln1_gain, grad_ln1_bias])
+    first_norm = finish(Job(small_steps(norms1, norms1)))
+
+    grad_down, grad_up, grad_out = finish(down_sum), finish(up_sum), finish(out_sum)
+    small = finish(small)
+    grad_qkv = jnp.concatenate(
+        [finish(job).reshape(3, width, LANES) for job in qkv_sum], axis=2
+    ).transpose(1, 0, 2)
+    hidden = b_up.shape[0]
+    rest = [small[hidden + i * width : hidden + (i + 1) * width] for i in range(3)]
     return (
         out,
         grad_tokens,
+        first_norm[:width],
+        first_norm[width:],
+        grad_qkv,
+        grad_out,
         rest[0],
         rest[1],
-        grad_qkv,
-        grad_out,
+        grad_up,
+        small[:hidden],
+        grad_down,
         rest[2],
-        rest[3],
-        grad_up,
-        grad_up_bias,
-        grad_down,
-        rest[4],
     )
 
 

time: 668 us -> 710 us (1.063)
  Pallas kernels: 112 us -> 169 us
  waiting for transfers between devices: 175 us -> 121 us
  local copies, waits for them, and re-layouts: 51.7 us -> 92.8 us
  blocking collectives: 39.7 us -> 0 us
  other arithmetic: 60.3 us -> 96.5 us
  starting transfers between devices: 113 us -> 139 us
  matrix products: 103 us -> 78.9 us
    ppermute x52 -> x93, waiting for transfers between devices: 175 us -> 121 us  [the longest x78 73.2 us: send(): return lax.ppermute(array, 'dp', [(i, i ^ mask) for i in range(dp_size)])]
    psum x1 -> x0, blocking collectives: 39.7 us -> none  [local(): lax.psum(jnp.concatenate([own_bias, grad_ln1_gain, grad_ln1_bias, grad_ln...]
    pallas_call x2 -> x6, Pallas kernels: 52.8 us -> 90.2 us  [attend_backward(): pl.pallas_call(backward_kernel, grid_spec=pltpu.PrefetchScalarGridSpec(nu...]
    dot_general x8 -> x4, matrix products: 42.1 us -> 14 us  [the longest x2 8.66 us: hidden_units(): jnp.einsum('rf,rd->fd', act_low, d_low, preferred_element_type=f32)]
    ppermute x52 -> x93, starting transfers between devices: 113 us -> 139 us  [the longest x78 91.2 us: send(): return lax.ppermute(array, 'dp', [(i, i ^ mask) for i in range(dp_size)])]
    pallas_call x0 -> x1, Pallas kernels: none -> 15.5 us  [rows_back(): pl.pallas_call(rows_back_kernel, grid=(9,), in_specs=[pl.BlockSpec((step,...]
    convert_element_type x14 -> x18, other arithmetic: 13.6 us -> 24 us  [the longest x12 15.1 us: low(): return array.astype(bf16)]
    slice x1 -> x11, local copies, waits for them, and re-layouts: 0.61 us -> 10.1 us  [the longest x3 4.33 us: local(): clean_other, edge_other = (context[:HALF], context[HALF:])]
  transfers between devices with their start and end apart: 52 -> 93, of which waited for: 20 -> 32; matrix products, arithmetic and copies ran while one was open for 30% -> 18% of each run, Pallas kernels for 17% -> 20%
where the time goes in v2:
time: 710 us; the launch traced here: 700 us
  Pallas kernels  169 us (24%)
  starting transfers between devices  139 us (20%)
  waiting for transfers between devices  121 us (17%)
  other arithmetic  96.5 us (14%)
  local copies, waits for them, and re-layouts  92.8 us (13%)
  matrix products  78.9 us (11%)
    ppermute x78, starting transfers between devices, send(): return lax.ppermute(array, 'dp', [(i, i ^ mask) for i in range(dp_size)])  91.2 us
    pallas_call x6, Pallas kernels, attend_backward(): pl.pallas_call(backward_kernel, grid_spec=pltpu.PrefetchScalarGridSpec(nu...  90.2 us
    ppermute x78, waiting for transfers between devices, send(): return lax.ppermute(array, 'dp', [(i, i ^ mask) for i in range(dp_size)])  73.2 us
    dot_general x12, matrix products, dot(): return lax.dot_general(left, right, dims, preferred_element_type=f32)  63.3 us
    ppermute x15, waiting for transfers between devices, send(): return lax.ppermute(array, 'mp', [(0, 1), (1, 0)])  47.8 us
    ppermute x15, starting transfers between devices, send(): return lax.ppermute(array, 'mp', [(0, 1), (1, 0)])  47.6 us
    pallas_call x2, Pallas kernels, attend_forward(): pl.pallas_call(forward_kernel, grid_spec=pltpu.PrefetchScalarGridSpec(num...  42.9 us
    pallas_call x2, Pallas kernels, project(): pl.pallas_call(project_kernel, grid=(9,), in_specs=[row_spec, pl.BlockSpe...  20.3 us
  transfers between devices with their start and end apart: 93, of which 32 were waited for; matrix products, arithmetic and copies ran while one was open for 18% of the time, Pallas kernels for 20%

profile of v2, /device:TPU:0, one launch (start us, length us, event | category | flops | bytes accessed | tf_op | source)
XLA Modules:
  0.0 700.3 jit_solution(7395973240101202405)
XLA Ops:
  9.2 3.0 collective-permute-start
  27.7 4.4 fusion.39
  34.5 3.8 copy.91
  38.3 2.8 copy.92
  41.1 3.8 copy.94
  52.2 5.3 concatenate.161
  65.2 4.4 copy.89.rows_ref
  72.2 10.0 %project.2 = (bf16[1584,384]{1,0:T(8,128)(2,1)}, bf16[1584,384]{1,0:T(8,128)(2,1)}, bf16[1584,384]{1,0:T(8,128)(2,1)}) custom-call(bf16[1584,768]{1,0:T(8,128)(2,1)} %copy.89.rows_ref, bf16[3,768,384]{2,1,0:T(8,128)(2,1)} %bitcast.123, f32[1584,128]{1,0:T(8,128)} %get-tuple-element.438.cos_ref, f32[1584,128]{1,0:T(8,128)} %get-tuple-element.437.sin_ref), custom_call_target="tpu_custom_call" | custom-call | flops 2802843648 | bytes 7852032 | tf_op jit(solution)/shard_map/project/pallas_call | solution.py:85
  82.2 21.5 %attend_forward.2 = (bf16[1024,384]{1,0:T(8,128)(2,1)}, f32[3,4,2,256]{3,2,1,0:T(2,128)}) custom-call(s32[4,2]{1,0:T(4,128)} %pad_add_fusion.1.span_ref, s32[4,2,256]{2,1,0:T(2,128)} %add_add_fusion.4.clean_ref, s32[4,2,128]{2,1,0:T(2,128)} %pad_add_fusion.noisy_ref, bf16[1584,384]{1,0:T(8,128)(2,1)} %get-tuple-element.170.q_ref, ...), custom_call_target="tpu_custom_call" | custom-call | flops 1610612736 | bytes 4866048 | tf_op jit(solution)/shard_map/attend_forward/pallas_call | solution.py:189
  104.3 4.2 fusion.119.rows_ref
  111.2 4.1 collective-permute-done.5
  115.3 23.7 %collective-permute-done.7 = bf16[768,768]{1,0:T(8,128)(2,1)S(1)} collective-permute-done((bf16[768,768]{1,0:T(8,128)(2,1)}, bf16[768,768]{1,0:T(8,128)(2,1)S(1)}, u32[]{:S(2)}, u32[]{:S(2)}) %collective-permute-start.7) | collective-permute-done | bytes 1179680 | tf_op jit(solution)/shard_map/ppermute | solution.py:513
  141.7 5.6 reshape_reshape.3
  147.3 5.3 copy.93
  152.6 3.8 copy.95
  156.4 10.3 %project.3 = (bf16[1584,384]{1,0:T(8,128)(2,1)}, bf16[1584,384]{1,0:T(8,128)(2,1)}, bf16[1584,384]{1,0:T(8,128)(2,1)}) custom-call(bf16[1584,768]{1,0:T(8,128)(2,1)} %copy.89.rows_ref, bf16[3,768,384]{2,1,0:T(8,128)(2,1)} %bitcast.117, f32[1584,128]{1,0:T(8,128)} %get-tuple-element.438.cos_ref, f32[1584,128]{1,0:T(8,128)} %get-tuple-element.437.sin_ref), custom_call_target="tpu_custom_call" | custom-call | flops 2802843648 | bytes 7852032 | tf_op jit(solution)/shard_map/project/pallas_call | solution.py:85
  166.7 21.5 %attend_forward.3 = (bf16[1024,384]{1,0:T(8,128)(2,1)}, f32[3,4,2,256]{3,2,1,0:T(2,128)}) custom-call(s32[4,2]{1,0:T(4,128)} %pad_add_fusion.1.span_ref, s32[4,2,256]{2,1,0:T(2,128)} %add_add_fusion.4.clean_ref, s32[4,2,128]{2,1,0:T(2,128)} %pad_add_fusion.noisy_ref, bf16[1584,384]{1,0:T(8,128)(2,1)} %get-tuple-element.177.q_ref, ...), custom_call_target="tpu_custom_call" | custom-call | flops 1610612736 | bytes 4866048 | tf_op jit(solution)/shard_map/attend_forward/pallas_call | solution.py:189
  189.3 3.7 fusion.81
  198.0 4.6 fusion.38
  202.6 5.9 fusion.67
  208.5 10.7 %convert_reduce_fusion.2 = (f32[1536]{0:T(1024)S(1)}, bf16[1024,1536]{1,0:T(8,128)(2,1)S(1)}) fusion(f32[1024,1536]{1,0:T(8,128)} %fusion.38, f32[1536]{0:T(1024)S(1)} %copy-done.86, bf16[1024,768]{1,0:T(8,128)(2,1)S(1)} %bitcast.111, bf16[768,768]{1,0:T(8,128)(2,1)S(1)} %get-tuple-element.347, bf16[768,768]{1,0:T(8,128)(2,1)S(1)} %get-tuple-element.346), kind=kOutput, calls=%fused_computation.29 | convolution fusion | flops 2463103488 | bytes 13381632 | tf_op jit(solution)/shard_map/dot_general | solution.py:36
  219.3 2.7 fusion.83
  223.6 4.6 fusion.84
  228.2 11.6 %convert_reduce_fusion.1 = (f32[1536]{0:T(1024)}, bf16[1024,1536]{1,0:T(8,128)(2,1)S(1)}, bf16[1024,1536]{1,0:T(8,128)(2,1)}) fusion(f32[1024,1536]{1,0:T(8,128)} %fusion.84, f32[1536]{0:T(1024)S(1)} %copy-done.88, bf16[1024,768]{1,0:T(8,128)(2,1)S(1)} %bitcast.112, bf16[1536,768]{1,0:T(8,128)(2,1)S(1)} %copy-done), kind=kOutput, calls=%fused_computation.28 | convolution fusion | flops 2461530624 | bytes 16527360 | tf_op jit(solution)/shard_map/dot_general | solution.py:36
  239.8 4.3 fusion.86
  244.1 2.6 fusion.88
  246.7 2.7 collective-permute-start.10
  249.5 2.8 fusion.87
  256.0 4.5 convolution_add_fusion
  274.8 12.4 %collective-permute-start.12 = (bf16[768,768]{1,0:T(8,128)(2,1)}, bf16[768,768]{1,0:T(8,128)(2,1)}, u32[]{:S(2)}, u32[]{:S(2)}) collective-permute-start(bf16[768,768]{1,0:T(8,128)(2,1)} %add_convert_fusion.3), channel_id=1, source_target_pairs={{0,1},{1,0},{2,3},{3,2},{4,5},{5,4},{6,7},{7,6},{8,9},{9,8},{10,11... | collective-permute-start | bytes 3538952 | tf_op jit(solution)/shard_map/ppermute | solution.py:513
  289.7 15.0 %attend_backward.6 = (bf16[1584,384]{1,0:T(8,128)(2,1)}, f32[3,768,128]{2,1,0:T(8,128)}) custom-call(s32[4,2]{1,0:T(4,128)} %pad_add_fusion.1.span_ref, s32[4,2,256]{2,1,0:T(2,128)} %add_add_fusion.4.clean_ref, s32[4,2,128]{2,1,0:T(2,128)} %pad_add_fusion.noisy_ref, bf16[1584,384]{1,0:T(8,128)(2,1)} %get-tuple-element.177.q_ref, ...), custom_call_target="tpu_custom_call" | custom-call | flops 12000000000 | bytes 12000000 | tf_op jit(solution)/shard_map/attend_backward/pallas_call | solution.py:345
  306.5 8.1 %collective-permute-done.15 = f32[3840]{0:T(1024)S(1)} collective-permute-done((f32[3840]{0:T(1024)}, f32[3840]{0:T(1024)S(1)}, u32[]{:S(2)}, u32[]{:S(2)}) %collective-permute-start.15) | collective-permute-done | bytes 15392 | tf_op jit(solution)/shard_map/ppermute | solution.py:513
  316.8 2.7 convert_add_fusion.1
  321.9 15.0 %attend_backward.7 = (bf16[1584,384]{1,0:T(8,128)(2,1)}, f32[3,768,128]{2,1,0:T(8,128)}) custom-call(s32[4,2]{1,0:T(4,128)} %pad_add_fusion.1.span_ref, s32[4,2,256]{2,1,0:T(2,128)} %add_add_fusion.4.clean_ref, s32[4,2,128]{2,1,0:T(2,128)} %pad_add_fusion.noisy_ref, bf16[1584,384]{1,0:T(8,128)(2,1)} %get-tuple-element.177.q_ref, ...), custom_call_target="tpu_custom_call" | custom-call | flops 12000000000 | bytes 12000000 | tf_op jit(solution)/shard_map/attend_backward/pallas_call | solution.py:345
  339.7 5.6 collective-permute-start.24
  345.3 3.0 convert_add_fusion
  350.5 5.2 collective-permute-start.20
  358.2 15.3 %attend_backward.8 = (bf16[1584,384]{1,0:T(8,128)(2,1)}, f32[3,768,128]{2,1,0:T(8,128)}) custom-call(s32[4,2]{1,0:T(4,128)} %pad_add_fusion.1.span_ref, s32[4,2,256]{2,1,0:T(2,128)} %add_add_fusion.4.clean_ref, s32[4,2,128]{2,1,0:T(2,128)} %pad_add_fusion.noisy_ref, bf16[1584,384]{1,0:T(8,128)(2,1)} %get-tuple-element.177.q_ref, ...), custom_call_target="tpu_custom_call" | custom-call | flops 12000000000 | bytes 12000000 | tf_op jit(solution)/shard_map/attend_backward/pallas_call | solution.py:345
  373.5 2.8 collective-permute-start.21
  378.8 8.3 %collective-permute-done.21 = bf16[96,768]{1,0:T(8,128)(2,1)S(1)} collective-permute-done((bf16[96,768]{1,0:T(8,128)(2,1)}, bf16[96,768]{1,0:T(8,128)(2,1)S(1)}, u32[]{:S(2)}, u32[]{:S(2)}) %collective-permute-start.21) | collective-permute-done | bytes 147488 | tf_op jit(solution)/shard_map/ppermute | solution.py:514
  396.8 3.7 collective-permute-start.29
  407.1 4.4 collective-permute-done.36
  411.5 3.7 collective-permute-start.33
  415.2 4.6 collective-permute-start.37
  420.6 15.0 %attend_backward.9 = (bf16[1584,384]{1,0:T(8,128)(2,1)}, f32[3,768,128]{2,1,0:T(8,128)}) custom-call(s32[4,2]{1,0:T(4,128)} %pad_add_fusion.1.span_ref, s32[4,2,256]{2,1,0:T(2,128)} %add_add_fusion.4.clean_ref, s32[4,2,128]{2,1,0:T(2,128)} %pad_add_fusion.noisy_ref, bf16[1584,384]{1,0:T(8,128)(2,1)} %get-tuple-element.170.q_ref, ...), custom_call_target="tpu_custom_call" | custom-call | flops 12000000000 | bytes 12000000 | tf_op jit(solution)/shard_map/attend_backward/pallas_call | solution.py:345
  439.8 4.4 collective-permute-done.34
  462.3 6.1 collective-permute-start.48
  468.4 15.0 %attend_backward.10 = (bf16[1584,384]{1,0:T(8,128)(2,1)}, f32[3,768,128]{2,1,0:T(8,128)}) custom-call(s32[4,2]{1,0:T(4,128)} %pad_add_fusion.1.span_ref, s32[4,2,256]{2,1,0:T(2,128)} %add_add_fusion.4.clean_ref, s32[4,2,128]{2,1,0:T(2,128)} %pad_add_fusion.noisy_ref, bf16[1584,384]{1,0:T(8,128)(2,1)} %get-tuple-element.170.q_ref, ...), custom_call_target="tpu_custom_call" | custom-call | flops 12000000000 | bytes 12000000 | tf_op jit(solution)/shard_map/attend_backward/pallas_call | solution.py:345
  489.3 8.2 %collective-permute-done.42 = bf16[48,1536]{1,0:T(8,128)(2,1)S(1)} collective-permute-done((bf16[48,1536]{1,0:T(8,128)(2,1)}, bf16[48,1536]{1,0:T(8,128)(2,1)S(1)}, u32[]{:S(2)}, u32[]{:S(2)}) %collective-permute-start.42) | collective-permute-done | bytes 147488 | tf_op jit(solution)/shard_map/ppermute | solution.py:514
  508.1 15.0 %attend_backward.11 = (bf16[1584,384]{1,0:T(8,128)(2,1)}, f32[3,768,128]{2,1,0:T(8,128)}) custom-call(s32[4,2]{1,0:T(4,128)} %pad_add_fusion.1.span_ref, s32[4,2,256]{2,1,0:T(2,128)} %add_add_fusion.4.clean_ref, s32[4,2,128]{2,1,0:T(2,128)} %pad_add_fusion.noisy_ref, bf16[1584,384]{1,0:T(8,128)(2,1)} %get-tuple-element.170.q_ref, ...), custom_call_target="tpu_custom_call" | custom-call | flops 12000000000 | bytes 12000000 | tf_op jit(solution)/shard_map/attend_backward/pallas_call | solution.py:345
  523.1 15.5 %rows_back.1 = f32[1584,768]{1,0:T(8,128)} custom-call(bf16[1584,384]{1,0:T(8,128)(2,1)} %get-tuple-element.243.refs_0_, bf16[1584,384]{1,0:T(8,128)(2,1)} %get-tuple-element.266.refs_1_, bf16[1584,384]{1,0:T(8,128)(2,1)} %get-tuple-element.288.refs_2_, bf16[1584,384]{1,0:T(8,128)(2,1)} %get-tuple-element.199.refs_3_, ...), custom_call_target="tpu_custom_call" | custom-call | flops 5605687296 | bytes 16000000 | tf_op jit(solution)/shard_map/rows_back/pallas_call | solution.py:401
  542.0 7.0 collective-permute-start.50
  550.2 6.2 fusion.85
  556.3 11.7 %collective-permute-done.50 = bf16[528,768]{1,0:T(8,128)(2,1)} collective-permute-done((bf16[528,768]{1,0:T(8,128)(2,1)}, bf16[528,768]{1,0:T(8,128)(2,1)}, u32[]{:S(2)}, u32[]{:S(2)}) %collective-permute-start.50) | collective-permute-done | bytes 811040 | tf_op jit(solution)/shard_map/ppermute | solution.py:513
  579.6 6.7 add_convert_fusion
  589.0 2.9 collective-permute-start.58
  593.7 10.0 %collective-permute-done.53 = f32[1536]{0:T(1024)S(1)} collective-permute-done((f32[1536]{0:T(1024)S(1)}, f32[1536]{0:T(1024)S(1)}, u32[]{:S(2)}, u32[]{:S(2)}) %collective-permute-start.53) | collective-permute-done | bytes 6176 | tf_op jit(solution)/shard_map/ppermute | solution.py:514
  607.5 3.2 collective-permute-start.55
  612.4 3.3 fusion.26
  658.9 3.0 collective-permute-done.77
  664.4 3.3 collective-permute-done.78
  684.8 2.8 collective-permute-done.87
  688.5 4.3 collective-permute-done.88
  697.3 2.8 maximum_convert_fusion
  (546 shorter events, 242.7 us)
Async XLA Ops:
  9.2 36.4 %collective-permute-start = (bf16[528,768]{1,0:T(8,128)(2,1)}, bf16[528,768]{1,0:T(8,128)(2,1)}, u32[]{:S(2)}, u32[]{:S(2)}) collective-permute-start(bf16[528,768]{1,0:T(8,128)(2,1)} %copy.83), channel_id=1, source_target_pairs={{0,1},{1,0},{2,3},{3,2},{4,5},{5,4},{6,7},{7,6},{8,9},{9,8},{10,11... | collective-permute-start | bytes 2433032 | tf_op jit(solution)/shard_map/ppermute | solution.py:513
  12.1 32.8 %collective-permute-start.9 = (bf16[1536]{0:T(1024)(128)(2,1)S(1)}, bf16[1536]{0:T(1024)(128)(2,1)S(1)}, u32[]{:S(2)}, u32[]{:S(2)}) collective-permute-start(bf16[1536]{0:T(1024)(128)(2,1)S(1)} %copy-done.91), channel_id=1, source_target_pairs={{0,1},{1,0},{2,3},{3,2},{4,5},{5,4},{6,7},{7,6},{8,9},{9,8},{10,11... | collective-permute-start | bytes 9224 | tf_op jit(solution)/shard_map/ppermute | solution.py:513
  60.7 42.9 %collective-permute-start.1 = (bf16[1152,384]{1,0:T(8,128)(2,1)}, bf16[1152,384]{1,0:T(8,128)(2,1)}, u32[]{:S(2)}, u32[]{:S(2)}) collective-permute-start(bf16[1152,384]{1,0:T(8,128)(2,1)} %constant_dynamic-slice_fusion.3), channel_id=1, source_target_pairs={{0,1},{1,0},{2,3},{3,2},{4,5},{5,4},{6,7},{7,6},{8,9},{9,8},{10,11... | collective-permute-start | bytes 2654216 | tf_op jit(solution)/shard_map/ppermute | solution.py:513
  69.6 41.5 %collective-permute-start.3 = (bf16[192,768]{1,0:T(8,128)(2,1)}, bf16[192,768]{1,0:T(8,128)(2,1)}, u32[]{:S(2)}, u32[]{:S(2)}) collective-permute-start(bf16[192,768]{1,0:T(8,128)(2,1)} %constant_dynamic-slice_fusion.2), channel_id=1, source_target_pairs={{0,1},{1,0},{2,3},{3,2},{4,5},{5,4},{6,7},{7,6},{8,9},{9,8},{10,11... | collective-permute-start | bytes 884744 | tf_op jit(solution)/shard_map/ppermute | solution.py:513
  70.1 45.2 %collective-permute-start.5 = (bf16[384,1536]{1,0:T(8,128)(2,1)}, bf16[384,1536]{1,0:T(8,128)(2,1)}, u32[]{:S(2)}, u32[]{:S(2)}) collective-permute-start(bf16[384,1536]{1,0:T(8,128)(2,1)} %constant_dynamic-slice_fusion.1), channel_id=1, source_target_pairs={{0,1},{1,0},{2,3},{3,2},{4,5},{5,4},{6,7},{7,6},{8,9},{9,8},{10,11... | collective-permute-start | bytes 3538952 | tf_op jit(solution)/shard_map/ppermute | solution.py:513
  71.6 67.4 %collective-permute-start.7 = (bf16[768,768]{1,0:T(8,128)(2,1)}, bf16[768,768]{1,0:T(8,128)(2,1)S(1)}, u32[]{:S(2)}, u32[]{:S(2)}) collective-permute-start(bf16[768,768]{1,0:T(8,128)(2,1)} %constant_dynamic-slice_fusion), channel_id=1, source_target_pairs={{0,1},{1,0},{2,3},{3,2},{4,5},{5,4},{6,7},{7,6},{8,9},{9,8},{10,11... | collective-permute-start | bytes 3538952 | tf_op jit(solution)/shard_map/ppermute | solution.py:513
  103.6 35.4 %collective-permute-start.2 = (bf16[1152,384]{1,0:T(8,128)(2,1)}, bf16[1152,384]{1,0:T(8,128)(2,1)S(1)}, u32[]{:S(2)}, u32[]{:S(2)}) collective-permute-start(bf16[1152,384]{1,0:T(8,128)(2,1)} %collective-permute-done.1), channel_id=1, source_target_pairs={{0,2},{2,0},{4,6},{6,4},{8,10},{10,8},{12,14},{14,12},{16,18},{18,... | collective-permute-start | bytes 2654216 | tf_op jit(solution)/shard_map/ppermute | solution.py:514
  111.1 77.1 %collective-permute-start.4 = (bf16[192,768]{1,0:T(8,128)(2,1)}, bf16[192,768]{1,0:T(8,128)(2,1)}, u32[]{:S(2)}, u32[]{:S(2)}) collective-permute-start(bf16[192,768]{1,0:T(8,128)(2,1)} %collective-permute-done.3), channel_id=1, source_target_pairs={{0,2},{2,0},{4,6},{6,4},{8,10},{10,8},{12,14},{14,12},{16,18},{18,... | collective-permute-start | bytes 884744 | tf_op jit(solution)/shard_map/ppermute | solution.py:514
  115.3 72.9 %collective-permute-start.6 = (bf16[384,1536]{1,0:T(8,128)(2,1)}, bf16[384,1536]{1,0:T(8,128)(2,1)}, u32[]{:S(2)}, u32[]{:S(2)}) collective-permute-start(bf16[384,1536]{1,0:T(8,128)(2,1)} %collective-permute-done.5), channel_id=1, source_target_pairs={{0,2},{2,0},{4,6},{6,4},{8,10},{10,8},{12,14},{14,12},{16,18},{18,... | collective-permute-start | bytes 3538952 | tf_op jit(solution)/shard_map/ppermute | solution.py:514
  139.0 49.2 %collective-permute-start.8 = (bf16[768,768]{1,0:T(8,128)(2,1)S(1)}, bf16[768,768]{1,0:T(8,128)(2,1)}, u32[]{:S(2)}, u32[]{:S(2)}) collective-permute-start(bf16[768,768]{1,0:T(8,128)(2,1)S(1)} %collective-permute-done.7), channel_id=1, source_target_pairs={{0,2},{2,0},{4,6},{6,4},{8,10},{10,8},{12,14},{14,12},{16,18},{18,... | collective-permute-start | bytes 3538952 | tf_op jit(solution)/shard_map/ppermute | solution.py:514
  246.7 13.8 %collective-permute-start.10 = (bf16[768,768]{1,0:T(8,128)(2,1)S(1)}, bf16[768,768]{1,0:T(8,128)(2,1)S(1)}, u32[]{:S(2)}, u32[]{:S(2)}) collective-permute-start(bf16[768,768]{1,0:T(8,128)(2,1)S(1)} %dynamic-slice_convert_fusion.3), channel_id=1, source_target_pairs={{0,2},{2,0},{4,6},{6,4},{8,10},{10,8},{12,14},{14,12},{16,18},{18,... | collective-permute-start | bytes 3538952 | tf_op jit(solution)/shard_map/ppermute | solution.py:514
  249.4 11.1 %collective-permute-start.11 = (bf16[384,1536]{1,0:T(8,128)(2,1)S(1)}, bf16[384,1536]{1,0:T(8,128)(2,1)S(1)}, u32[]{:S(2)}, u32[]{:S(2)}) collective-permute-start(bf16[384,1536]{1,0:T(8,128)(2,1)S(1)} %dynamic-slice_convert_fusion.2), channel_id=1, source_target_pairs={{0,2},{2,0},{4,6},{6,4},{8,10},{10,8},{12,14},{14,12},{16,18},{18,... | collective-permute-start | bytes 3538952 | tf_op jit(solution)/shard_map/ppermute | solution.py:514
  274.8 40.3 %collective-permute-start.12 = (bf16[768,768]{1,0:T(8,128)(2,1)}, bf16[768,768]{1,0:T(8,128)(2,1)}, u32[]{:S(2)}, u32[]{:S(2)}) collective-permute-start(bf16[768,768]{1,0:T(8,128)(2,1)} %add_convert_fusion.3), channel_id=1, source_target_pairs={{0,1},{1,0},{2,3},{3,2},{4,5},{5,4},{6,7},{7,6},{8,9},{9,8},{10,11... | collective-permute-start | bytes 3538952 | tf_op jit(solution)/shard_map/ppermute | solution.py:513
  287.2 27.9 %collective-permute-start.13 = (bf16[768,768]{1,0:T(8,128)(2,1)}, bf16[768,768]{1,0:T(8,128)(2,1)}, u32[]{:S(2)}, u32[]{:S(2)}) collective-permute-start(bf16[768,768]{1,0:T(8,128)(2,1)} %dynamic-slice_convert_fusion.1), channel_id=1, source_target_pairs={{0,2},{2,0},{4,6},{6,4},{8,10},{10,8},{12,14},{14,12},{16,18},{18,... | collective-permute-start | bytes 3538952 | tf_op jit(solution)/shard_map/ppermute | solution.py:514
  287.3 27.2 %collective-permute-start.14 = (bf16[192,768]{1,0:T(8,128)(2,1)}, bf16[192,768]{1,0:T(8,128)(2,1)}, u32[]{:S(2)}, u32[]{:S(2)}) collective-permute-start(bf16[192,768]{1,0:T(8,128)(2,1)} %dynamic-slice_convert_fusion.13), channel_id=1, source_target_pairs={{0,2},{2,0},{4,6},{6,4},{8,10},{10,8},{12,14},{14,12},{16,18},{18,... | collective-permute-start | bytes 884744 | tf_op jit(solution)/shard_map/ppermute | solution.py:514
  287.7 26.9 %collective-permute-start.15 = (f32[3840]{0:T(1024)}, f32[3840]{0:T(1024)S(1)}, u32[]{:S(2)}, u32[]{:S(2)}) collective-permute-start(f32[3840]{0:T(1024)} %pad_maximum_fusion.42), channel_id=1, source_target_pairs={{0,1},{1,0},{2,3},{3,2},{4,5},{5,4},{6,7},{7,6},{8,9},{9,8},{10,11... | collective-permute-start | bytes 46088 | tf_op jit(solution)/shard_map/ppermute | solution.py:513
  287.7 52.0 %collective-permute-start.16 = (bf16[384,1536]{1,0:T(8,128)(2,1)}, bf16[384,1536]{1,0:T(8,128)(2,1)}, u32[]{:S(2)}, u32[]{:S(2)}) collective-permute-start(bf16[384,1536]{1,0:T(8,128)(2,1)} %add_convert_fusion.2), channel_id=1, source_target_pairs={{0,1},{1,0},{2,3},{3,2},{4,5},{5,4},{6,7},{7,6},{8,9},{9,8},{10,11... | collective-permute-start | bytes 3538952 | tf_op jit(solution)/shard_map/ppermute | solution.py:513
  314.6 30.7 %collective-permute-start.17 = (bf16[384,1536]{1,0:T(8,128)(2,1)}, bf16[384,1536]{1,0:T(8,128)(2,1)}, u32[]{:S(2)}, u32[]{:S(2)}) collective-permute-start(bf16[384,1536]{1,0:T(8,128)(2,1)} %dynamic-slice_convert_fusion), channel_id=1, source_target_pairs={{0,2},{2,0},{4,6},{6,4},{8,10},{10,8},{12,14},{14,12},{16,18},{18,... | collective-permute-start | bytes 3538952 | tf_op jit(solution)/shard_map/ppermute | solution.py:514
  314.6 43.1 %collective-permute-start.25 = (bf16[192,768]{1,0:T(8,128)(2,1)}, bf16[192,768]{1,0:T(8,128)(2,1)}, u32[]{:S(2)}, u32[]{:S(2)}) collective-permute-start(bf16[192,768]{1,0:T(8,128)(2,1)} %dynamic-slice_convert_fusion.12), channel_id=1, source_target_pairs={{0,2},{2,0},{4,6},{6,4},{8,10},{10,8},{12,14},{14,12},{16,18},{18,... | collective-permute-start | bytes 884744 | tf_op jit(solution)/shard_map/ppermute | solution.py:514
  321.8 23.5 %collective-permute-start.18 = (bf16[384,768]{1,0:T(8,128)(2,1)S(1)}, bf16[384,768]{1,0:T(8,128)(2,1)S(1)}, u32[]{:S(2)}, u32[]{:S(2)}) collective-permute-start(bf16[384,768]{1,0:T(8,128)(2,1)S(1)} %dynamic-slice_convert_fusion.5), channel_id=1, source_target_pairs={{0,4},{2,6},{4,0},{6,2},{8,12},{10,14},{12,8},{14,10},{16,20},{18,... | collective-permute-start | bytes 1769480 | tf_op jit(solution)/shard_map/ppermute | solution.py:514
  336.9 8.4 %collective-permute-start.19 = (f32[3840]{0:T(1024)S(1)}, f32[3840]{0:T(1024)S(1)}, u32[]{:S(2)}, u32[]{:S(2)}) collective-permute-start(f32[3840]{0:T(1024)S(1)} %fusion.44), channel_id=1, source_target_pairs={{0,2},{2,0},{4,6},{6,4},{8,10},{10,8},{12,14},{14,12},{16,18},{18,... | collective-permute-start | bytes 46088 | tf_op jit(solution)/shard_map/ppermute | solution.py:514
  339.7 18.0 %collective-permute-start.24 = (bf16[192,768]{1,0:T(8,128)(2,1)}, bf16[192,768]{1,0:T(8,128)(2,1)}, u32[]{:S(2)}, u32[]{:S(2)}) collective-permute-start(bf16[192,768]{1,0:T(8,128)(2,1)} %add_convert_fusion.7), channel_id=1, source_target_pairs={{0,1},{1,0},{2,3},{3,2},{4,5},{5,4},{6,7},{7,6},{8,9},{9,8},{10,11... | collective-permute-start | bytes 884744 | tf_op jit(solution)/shard_map/ppermute | solution.py:513
  350.5 25.9 %collective-permute-start.20 = (bf16[96,768]{1,0:T(8,128)(2,1)}, bf16[96,768]{1,0:T(8,128)(2,1)}, u32[]{:S(2)}, u32[]{:S(2)}) collective-permute-start(bf16[96,768]{1,0:T(8,128)(2,1)} %get-tuple-element.222), channel_id=1, source_target_pairs={{0,8},{2,10},{4,12},{6,14},{8,0},{10,2},{12,4},{14,6},{16,24},{18,... | collective-permute-start | bytes 442376 | tf_op jit(solution)/shard_map/ppermute | solution.py:514
  355.7 31.4 %collective-permute-start.23 = (bf16[192,1536]{1,0:T(8,128)(2,1)}, bf16[192,1536]{1,0:T(8,128)(2,1)}, u32[]{:S(2)}, u32[]{:S(2)}) collective-permute-start(bf16[192,1536]{1,0:T(8,128)(2,1)} %dynamic-slice_convert_fusion.4), channel_id=1, source_target_pairs={{0,4},{2,6},{4,0},{6,2},{8,12},{10,14},{12,8},{14,10},{16,20},{18,... | collective-permute-start | bytes 1769480 | tf_op jit(solution)/shard_map/ppermute | solution.py:514
  356.5 17.0 %collective-permute-start.26 = (f32[3840]{0:T(1024)S(1)}, f32[3840]{0:T(1024)}, u32[]{:S(2)}, u32[]{:S(2)}) collective-permute-start(f32[3840]{0:T(1024)S(1)} %add.579), channel_id=1, source_target_pairs={{0,4},{2,6},{4,0},{6,2},{8,12},{10,14},{12,8},{14,10},{16,20},{18,... | collective-permute-start | bytes 46088 | tf_op jit(solution)/shard_map/ppermute | solution.py:514
  357.7 29.4 %collective-permute-start.27 = (bf16[1152,128]{1,0:T(8,128)(2,1)}, bf16[1152,128]{1,0:T(8,128)(2,1)}, u32[]{:S(2)}, u32[]{:S(2)}) collective-permute-start(bf16[1152,128]{1,0:T(8,128)(2,1)} %dynamic-slice_convert_fusion.11), channel_id=1, source_target_pairs={{0,2},{2,0},{4,6},{6,4},{8,10},{10,8},{12,14},{14,12},{16,18},{18,... | collective-permute-start | bytes 884744 | tf_op jit(solution)/shard_map/ppermute | solution.py:514
  357.7 29.4 %collective-permute-start.28 = (bf16[1152,128]{1,0:T(8,128)(2,1)}, bf16[1152,128]{1,0:T(8,128)(2,1)}, u32[]{:S(2)}, u32[]{:S(2)}) collective-permute-start(bf16[1152,128]{1,0:T(8,128)(2,1)} %dynamic-slice_convert_fusion.10), channel_id=1, source_target_pairs={{0,2},{2,0},{4,6},{6,4},{8,10},{10,8},{12,14},{14,12},{16,18},{18,... | collective-permute-start | bytes 884744 | tf_op jit(solution)/shard_map/ppermute | solution.py:514
  373.5 13.6 %collective-permute-start.21 = (bf16[96,768]{1,0:T(8,128)(2,1)}, bf16[96,768]{1,0:T(8,128)(2,1)S(1)}, u32[]{:S(2)}, u32[]{:S(2)}) collective-permute-start(bf16[96,768]{1,0:T(8,128)(2,1)} %get-tuple-element.223), channel_id=1, source_target_pairs={{0,16},{2,18},{4,20},{6,22},{8,24},{10,26},{12,28},{14,30},{16,0},... | collective-permute-start | bytes 442376 | tf_op jit(solution)/shard_map/ppermute | solution.py:514
  376.4 10.7 %collective-permute-start.22 = (bf16[96,768]{1,0:T(8,128)(2,1)}, bf16[96,768]{1,0:T(8,128)(2,1)S(1)}, u32[]{:S(2)}, u32[]{:S(2)}) collective-permute-start(bf16[96,768]{1,0:T(8,128)(2,1)} %get-tuple-element.224), channel_id=1, source_target_pairs={{0,24},{2,26},{4,28},{6,30},{8,16},{10,18},{12,20},{14,22},{16,8},... | collective-permute-start | bytes 442376 | tf_op jit(solution)/shard_map/ppermute | solution.py:514
  396.8 18.4 %collective-permute-start.29 = (bf16[96,768]{1,0:T(8,128)(2,1)S(1)}, bf16[96,768]{1,0:T(8,128)(2,1)S(1)}, u32[]{:S(2)}, u32[]{:S(2)}) collective-permute-start(bf16[96,768]{1,0:T(8,128)(2,1)S(1)} %add_convert_fusion.9), channel_id=1, source_target_pairs={{0,8},{2,10},{4,12},{6,14},{8,0},{10,2},{12,4},{14,6},{16,24},{18,... | collective-permute-start | bytes 442376 | tf_op jit(solution)/shard_map/ppermute | solution.py:514
  400.5 19.3 %collective-permute-start.30 = (bf16[96,768]{1,0:T(8,128)(2,1)S(1)}, bf16[96,768]{1,0:T(8,128)(2,1)S(1)}, u32[]{:S(2)}, u32[]{:S(2)}) collective-permute-start(bf16[96,768]{1,0:T(8,128)(2,1)S(1)} %add_convert_fusion.9), channel_id=1, source_target_pairs={{0,16},{2,18},{4,20},{6,22},{8,24},{10,26},{12,28},{14,30},{16,0},... | collective-permute-start | bytes 442376 | tf_op jit(solution)/shard_map/ppermute | solution.py:514
  401.7 18.2 %collective-permute-start.31 = (bf16[96,768]{1,0:T(8,128)(2,1)S(1)}, bf16[96,768]{1,0:T(8,128)(2,1)S(1)}, u32[]{:S(2)}, u32[]{:S(2)}) collective-permute-start(bf16[96,768]{1,0:T(8,128)(2,1)S(1)} %add_convert_fusion.9), channel_id=1, source_target_pairs={{0,24},{2,26},{4,28},{6,30},{8,16},{10,18},{12,20},{14,22},{16,8},... | collective-permute-start | bytes 442376 | tf_op jit(solution)/shard_map/ppermute | solution.py:514
  403.2 8.3 %collective-permute-start.36 = (f32[3840]{0:T(1024)S(1)}, f32[3840]{0:T(1024)S(1)}, u32[]{:S(2)}, u32[]{:S(2)}) collective-permute-start(f32[3840]{0:T(1024)S(1)} %add.593), channel_id=1, source_target_pairs={{0,8},{2,10},{4,12},{6,14},{8,0},{10,2},{12,4},{14,6},{16,24},{18,... | collective-permute-start | bytes 46088 | tf_op jit(solution)/shard_map/ppermute | solution.py:514
  405.9 29.6 %collective-permute-start.32 = (bf16[48,1536]{1,0:T(8,128)(2,1)}, bf16[48,1536]{1,0:T(8,128)(2,1)}, u32[]{:S(2)}, u32[]{:S(2)}) collective-permute-start(bf16[48,1536]{1,0:T(8,128)(2,1)} %get-tuple-element.247), channel_id=1, source_target_pairs={{0,8},{2,10},{4,12},{6,14},{8,0},{10,2},{12,4},{14,6},{16,24},{18,... | collective-permute-start | bytes 442376 | tf_op jit(solution)/shard_map/ppermute | solution.py:514
  411.5 26.5 %collective-permute-start.33 = (bf16[48,1536]{1,0:T(8,128)(2,1)}, bf16[48,1536]{1,0:T(8,128)(2,1)}, u32[]{:S(2)}, u32[]{:S(2)}) collective-permute-start(bf16[48,1536]{1,0:T(8,128)(2,1)} %get-tuple-element.248), channel_id=1, source_target_pairs={{0,16},{2,18},{4,20},{6,22},{8,24},{10,26},{12,28},{14,30},{16,0},... | collective-permute-start | bytes 442376 | tf_op jit(solution)/shard_map/ppermute | solution.py:514
  415.2 29.0 %collective-permute-start.37 = (bf16[1152,128]{1,0:T(8,128)(2,1)}, bf16[1152,128]{1,0:T(8,128)(2,1)}, u32[]{:S(2)}, u32[]{:S(2)}) collective-permute-start(bf16[1152,128]{1,0:T(8,128)(2,1)} %add_convert_fusion.6), channel_id=1, source_target_pairs={{0,1},{1,0},{2,3},{3,2},{4,5},{5,4},{6,7},{7,6},{8,9},{9,8},{10,11... | collective-permute-start | bytes 884744 | tf_op jit(solution)/shard_map/ppermute | solution.py:513
  419.8 24.4 %collective-permute-start.38 = (bf16[1152,128]{1,0:T(8,128)(2,1)}, bf16[1152,128]{1,0:T(8,128)(2,1)}, u32[]{:S(2)}, u32[]{:S(2)}) collective-permute-start(bf16[1152,128]{1,0:T(8,128)(2,1)} %add_convert_fusion.5), channel_id=1, source_target_pairs={{0,1},{1,0},{2,3},{3,2},{4,5},{5,4},{6,7},{7,6},{8,9},{9,8},{10,11... | collective-permute-start | bytes 884744 | tf_op jit(solution)/shard_map/ppermute | solution.py:513
  419.9 24.3 %collective-permute-start.39 = (bf16[1152,128]{1,0:T(8,128)(2,1)}, bf16[1152,128]{1,0:T(8,128)(2,1)}, u32[]{:S(2)}, u32[]{:S(2)}) collective-permute-start(bf16[1152,128]{1,0:T(8,128)(2,1)} %dynamic-slice_convert_fusion.9), channel_id=1, source_target_pairs={{0,2},{2,0},{4,6},{6,4},{8,10},{10,8},{12,14},{14,12},{16,18},{18,... | collective-permute-start | bytes 884744 | tf_op jit(solution)/shard_map/ppermute | solution.py:514
  435.5 8.6 %collective-permute-start.34 = (bf16[48,1536]{1,0:T(8,128)(2,1)}, bf16[48,1536]{1,0:T(8,128)(2,1)S(1)}, u32[]{:S(2)}, u32[]{:S(2)}) collective-permute-start(bf16[48,1536]{1,0:T(8,128)(2,1)} %get-tuple-element.249), channel_id=1, source_target_pairs={{0,24},{2,26},{4,28},{6,30},{8,16},{10,18},{12,20},{14,22},{16,8},... | collective-permute-start | bytes 442376 | tf_op jit(solution)/shard_map/ppermute | solution.py:514
  451.9 10.4 %collective-permute-start.44 = (bf16[24,768]{1,0:T(8,128)(2,1)S(1)}, bf16[24,768]{1,0:T(8,128)(2,1)}, u32[]{:S(2)}, u32[]{:S(2)}) collective-permute-start(bf16[24,768]{1,0:T(8,128)(2,1)S(1)} %get-tuple-element.271), channel_id=1, source_target_pairs={{0,8},{2,10},{4,12},{6,14},{8,0},{10,2},{12,4},{14,6},{16,24},{18,... | collective-permute-start | bytes 110600 | tf_op jit(solution)/shard_map/ppermute | solution.py:514
  454.5 13.9 %collective-permute-start.45 = (bf16[24,768]{1,0:T(8,128)(2,1)S(1)}, bf16[24,768]{1,0:T(8,128)(2,1)}, u32[]{:S(2)}, u32[]{:S(2)}) collective-permute-start(bf16[24,768]{1,0:T(8,128)(2,1)S(1)} %get-tuple-element.272), channel_id=1, source_target_pairs={{0,16},{2,18},{4,20},{6,22},{8,24},{10,26},{12,28},{14,30},{16,0},... | collective-permute-start | bytes 110600 | tf_op jit(solution)/shard_map/ppermute | solution.py:514
  459.6 37.9 %collective-permute-start.40 = (bf16[384,768]{1,0:T(8,128)(2,1)}, bf16[384,768]{1,0:T(8,128)(2,1)S(1)}, u32[]{:S(2)}, u32[]{:S(2)}) collective-permute-start(bf16[384,768]{1,0:T(8,128)(2,1)} %pad_maximum_fusion.14), channel_id=1, source_target_pairs={{0,4},{2,6},{4,0},{6,2},{8,12},{10,14},{12,8},{14,10},{16,20},{18,... | collective-permute-start | bytes 1769480 | tf_op jit(solution)/shard_map/ppermute | solution.py:514
  459.7 26.0 %collective-permute-start.41 = (bf16[48,1536]{1,0:T(8,128)(2,1)}, bf16[48,1536]{1,0:T(8,128)(2,1)}, u32[]{:S(2)}, u32[]{:S(2)}) collective-permute-start(bf16[48,1536]{1,0:T(8,128)(2,1)} %add_convert_fusion.8), channel_id=1, source_target_pairs={{0,8},{2,10},{4,12},{6,14},{8,0},{10,2},{12,4},{14,6},{16,24},{18,... | collective-permute-start | bytes 442376 | tf_op jit(solution)/shard_map/ppermute | solution.py:514
  460.3 23.0 %collective-permute-start.46 = (bf16[24,768]{1,0:T(8,128)(2,1)}, bf16[24,768]{1,0:T(8,128)(2,1)}, u32[]{:S(2)}, u32[]{:S(2)}) collective-permute-start(bf16[24,768]{1,0:T(8,128)(2,1)} %get-tuple-element.273), channel_id=1, source_target_pairs={{0,24},{2,26},{4,28},{6,30},{8,16},{10,18},{12,20},{14,22},{16,8},... | collective-permute-start | bytes 110600 | tf_op jit(solution)/shard_map/ppermute | solution.py:514
  462.3 35.2 %collective-permute-start.48 = (bf16[1152,128]{1,0:T(8,128)(2,1)}, bf16[1152,128]{1,0:T(8,128)(2,1)S(1)}, u32[]{:S(2)}, u32[]{:S(2)}) collective-permute-start(bf16[1152,128]{1,0:T(8,128)(2,1)} %add_convert_fusion.4), channel_id=1, source_target_pairs={{0,1},{1,0},{2,3},{3,2},{4,5},{5,4},{6,7},{7,6},{8,9},{9,8},{10,11... | collective-permute-start | bytes 884744 | tf_op jit(solution)/shard_map/ppermute | solution.py:513
  468.4 29.1 %collective-permute-start.49 = (bf16[1152,128]{1,0:T(8,128)(2,1)}, bf16[1152,128]{1,0:T(8,128)(2,1)S(1)}, u32[]{:S(2)}, u32[]{:S(2)}) collective-permute-start(bf16[1152,128]{1,0:T(8,128)(2,1)} %dynamic-slice_convert_fusion.8), channel_id=1, source_target_pairs={{0,2},{2,0},{4,6},{6,4},{8,10},{10,8},{12,14},{14,12},{16,18},{18,... | collective-permute-start | bytes 884744 | tf_op jit(solution)/shard_map/ppermute | solution.py:514
  483.4 14.1 %collective-permute-start.42 = (bf16[48,1536]{1,0:T(8,128)(2,1)}, bf16[48,1536]{1,0:T(8,128)(2,1)S(1)}, u32[]{:S(2)}, u32[]{:S(2)}) collective-permute-start(bf16[48,1536]{1,0:T(8,128)(2,1)} %add_convert_fusion.8), channel_id=1, source_target_pairs={{0,16},{2,18},{4,20},{6,22},{8,24},{10,26},{12,28},{14,30},{16,0},... | collective-permute-start | bytes 442376 | tf_op jit(solution)/shard_map/ppermute | solution.py:514
  485.7 11.8 %collective-permute-start.43 = (bf16[48,1536]{1,0:T(8,128)(2,1)}, bf16[48,1536]{1,0:T(8,128)(2,1)S(1)}, u32[]{:S(2)}, u32[]{:S(2)}) collective-permute-start(bf16[48,1536]{1,0:T(8,128)(2,1)} %add_convert_fusion.8), channel_id=1, source_target_pairs={{0,24},{2,26},{4,28},{6,30},{8,16},{10,18},{12,20},{14,22},{16,8},... | collective-permute-start | bytes 442376 | tf_op jit(solution)/shard_map/ppermute | solution.py:514
  542.0 26.0 %collective-permute-start.50 = (bf16[528,768]{1,0:T(8,128)(2,1)}, bf16[528,768]{1,0:T(8,128)(2,1)}, u32[]{:S(2)}, u32[]{:S(2)}) collective-permute-start(bf16[528,768]{1,0:T(8,128)(2,1)} %pad_maximum_fusion.12), channel_id=1, source_target_pairs={{0,1},{1,0},{2,3},{3,2},{4,5},{5,4},{6,7},{7,6},{8,9},{9,8},{10,11... | collective-permute-start | bytes 2433032 | tf_op jit(solution)/shard_map/ppermute | solution.py:513
  577.4 9.0 %collective-permute-start.51 = (f32[1536]{0:T(1024)S(1)}, f32[1536]{0:T(1024)S(1)}, u32[]{:S(2)}, u32[]{:S(2)}) collective-permute-start(f32[1536]{0:T(1024)S(1)} %pad_maximum_fusion.47), channel_id=1, source_target_pairs={{0,1},{1,0},{2,3},{3,2},{4,5},{5,4},{6,7},{7,6},{8,9},{9,8},{10,11... | collective-permute-start | bytes 18440 | tf_op jit(solution)/shard_map/ppermute | solution.py:513
  587.7 36.5 %collective-permute-start.56 = (bf16[768,768]{1,0:T(8,128)(2,1)S(1)}, bf16[768,768]{1,0:T(8,128)(2,1)S(1)}, u32[]{:S(2)}, u32[]{:S(2)}) collective-permute-start(bf16[768,768]{1,0:T(8,128)(2,1)S(1)} %copy-done.41), channel_id=1, source_target_pairs={{0,2},{2,0},{4,6},{6,4},{8,10},{10,8},{12,14},{14,12},{16,18},{18,... | collective-permute-start | bytes 3538952 | tf_op jit(solution)/shard_map/ppermute | solution.py:514
  588.2 36.0 %collective-permute-start.57 = (bf16[192,1536]{1,0:T(8,128)(2,1)S(1)}, bf16[192,1536]{1,0:T(8,128)(2,1)S(1)}, u32[]{:S(2)}, u32[]{:S(2)}) collective-permute-start(bf16[192,1536]{1,0:T(8,128)(2,1)S(1)} %copy-done.49), channel_id=1, source_target_pairs={{0,4},{2,6},{4,0},{6,2},{8,12},{10,14},{12,8},{14,10},{16,20},{18,... | collective-permute-start | bytes 1769480 | tf_op jit(solution)/shard_map/ppermute | solution.py:514
  589.0 26.8 %collective-permute-start.58 = (bf16[24,768]{1,0:T(8,128)(2,1)S(1)}, bf16[24,768]{1,0:T(8,128)(2,1)S(1)}, u32[]{:S(2)}, u32[]{:S(2)}) collective-permute-start(bf16[24,768]{1,0:T(8,128)(2,1)S(1)} %copy-done.57), channel_id=1, source_target_pairs={{0,8},{2,10},{4,12},{6,14},{8,0},{10,2},{12,4},{14,6},{16,24},{18,... | collective-permute-start | bytes 110600 | tf_op jit(solution)/shard_map/ppermute | solution.py:514
  592.0 26.3 %collective-permute-start.59 = (bf16[24,768]{1,0:T(8,128)(2,1)S(1)}, bf16[24,768]{1,0:T(8,128)(2,1)S(1)}, u32[]{:S(2)}, u32[]{:S(2)}) collective-permute-start(bf16[24,768]{1,0:T(8,128)(2,1)S(1)} %copy-done.57), channel_id=1, source_target_pairs={{0,16},{2,18},{4,20},{6,22},{8,24},{10,26},{12,28},{14,30},{16,0},... | collective-permute-start | bytes 110600 | tf_op jit(solution)/shard_map/ppermute | solution.py:514
  592.3 11.4 %collective-permute-start.53 = (f32[1536]{0:T(1024)S(1)}, f32[1536]{0:T(1024)S(1)}, u32[]{:S(2)}, u32[]{:S(2)}) collective-permute-start(f32[1536]{0:T(1024)S(1)} %add.622), channel_id=1, source_target_pairs={{0,4},{2,6},{4,0},{6,2},{8,12},{10,14},{12,8},{14,10},{16,20},{18,... | collective-permute-start | bytes 18440 | tf_op jit(solution)/shard_map/ppermute | solution.py:514
  612.3 11.8 %collective-permute-start.62 = (bf16[1152,128]{1,0:T(8,128)(2,1)S(1)}, bf16[1152,128]{1,0:T(8,128)(2,1)S(1)}, u32[]{:S(2)}, u32[]{:S(2)}) collective-permute-start(bf16[1152,128]{1,0:T(8,128)(2,1)S(1)} %copy-done.51), channel_id=1, source_target_pairs={{0,2},{2,0},{4,6},{6,4},{8,10},{10,8},{12,14},{14,12},{16,18},{18,... | collective-permute-start | bytes 884744 | tf_op jit(solution)/shard_map/ppermute | solution.py:514
  625.9 37.4 %collective-permute-start.80 = (bf16[1152,128]{1,0:T(8,128)(2,1)S(1)}, bf16[1152,128]{1,0:T(8,128)(2,1)S(1)}, u32[]{:S(2)}, u32[]{:S(2)}) collective-permute-start(bf16[1152,128]{1,0:T(8,128)(2,1)S(1)} %dynamic-slice_convert_fusion.6), channel_id=1, source_target_pairs={{0,2},{2,0},{4,6},{6,4},{8,10},{10,8},{12,14},{14,12},{16,18},{18,... | collective-permute-start | bytes 884744 | tf_op jit(solution)/shard_map/ppermute | solution.py:514
  626.0 19.0 %collective-permute-start.71 = (bf16[576,128]{1,0:T(8,128)(2,1)S(1)}, bf16[576,128]{1,0:T(8,128)(2,1)S(1)}, u32[]{:S(2)}, u32[]{:S(2)}) collective-permute-start(bf16[576,128]{1,0:T(8,128)(2,1)S(1)} %dynamic-slice_convert_fusion.15), channel_id=1, source_target_pairs={{0,4},{2,6},{4,0},{6,2},{8,12},{10,14},{12,8},{14,10},{16,20},{18,... | collective-permute-start | bytes 442376 | tf_op jit(solution)/shard_map/ppermute | solution.py:514
  632.6 14.3 %collective-permute-start.90 = (bf16[96,768]{1,0:T(8,128)(2,1)S(1)}, bf16[96,768]{1,0:T(8,128)(2,1)S(1)}, u32[]{:S(2)}, u32[]{:S(2)}) collective-permute-start(bf16[96,768]{1,0:T(8,128)(2,1)S(1)} %pad_maximum_fusion.29), channel_id=1, source_target_pairs={{0,4},{2,6},{4,0},{6,2},{8,12},{10,14},{12,8},{14,10},{16,20},{18,... | collective-permute-start | bytes 442376 | tf_op jit(solution)/shard_map/ppermute | solution.py:514
  643.4 53.4 %collective-permute-start.92 = (bf16[384,1536]{1,0:T(8,128)(2,1)S(1)}, bf16[384,1536]{1,0:T(8,128)(2,1)S(1)}, u32[]{:S(2)}, u32[]{:S(2)}) collective-permute-start(bf16[384,1536]{1,0:T(8,128)(2,1)S(1)} %pad_maximum_fusion.10), channel_id=1, source_target_pairs={{0,2},{2,0},{4,6},{6,4},{8,10},{10,8},{12,14},{14,12},{16,18},{18,... | collective-permute-start | bytes 3538952 | tf_op jit(solution)/shard_map/ppermute | solution.py:514
  651.1 12.0 %collective-permute-start.69 = (bf16[576,128]{1,0:T(8,128)(2,1)S(1)}, bf16[576,128]{1,0:T(8,128)(2,1)S(1)}, u32[]{:S(2)}, u32[]{:S(2)}) collective-permute-start(bf16[576,128]{1,0:T(8,128)(2,1)S(1)} %pad_maximum_fusion.30), channel_id=1, source_target_pairs={{0,4},{2,6},{4,0},{6,2},{8,12},{10,14},{12,8},{14,10},{16,20},{18,... | collective-permute-start | bytes 442376 | tf_op jit(solution)/shard_map/ppermute | solution.py:514
  658.9 14.1 %collective-permute-start.91 = (bf16[192,768]{1,0:T(8,128)(2,1)S(1)}, bf16[192,768]{1,0:T(8,128)(2,1)S(1)}, u32[]{:S(2)}, u32[]{:S(2)}) collective-permute-start(bf16[192,768]{1,0:T(8,128)(2,1)S(1)} %pad_maximum_fusion.28), channel_id=1, source_target_pairs={{0,2},{2,0},{4,6},{6,4},{8,10},{10,8},{12,14},{14,12},{16,18},{18,... | collective-permute-start | bytes 884744 | tf_op jit(solution)/shard_map/ppermute | solution.py:514
  663.2 25.2 %collective-permute-start.70 = (bf16[1152,128]{1,0:T(8,128)(2,1)S(1)}, bf16[1152,128]{1,0:T(8,128)(2,1)S(1)}, u32[]{:S(2)}, u32[]{:S(2)}) collective-permute-start(bf16[1152,128]{1,0:T(8,128)(2,1)S(1)} %pad_maximum_fusion.25), channel_id=1, source_target_pairs={{0,2},{2,0},{4,6},{6,4},{8,10},{10,8},{12,14},{14,12},{16,18},{18,... | collective-permute-start | bytes 884744 | tf_op jit(solution)/shard_map/ppermute | solution.py:514
  676.2 16.9 %collective-permute-start.79 = (bf16[1152,128]{1,0:T(8,128)(2,1)S(1)}, bf16[1152,128]{1,0:T(8,128)(2,1)S(1)}, u32[]{:S(2)}, u32[]{:S(2)}) collective-permute-start(bf16[1152,128]{1,0:T(8,128)(2,1)S(1)} %pad_maximum_fusion.26), channel_id=1, source_target_pairs={{0,2},{2,0},{4,6},{6,4},{8,10},{10,8},{12,14},{14,12},{16,18},{18,... | collective-permute-start | bytes 884744 | tf_op jit(solution)/shard_map/ppermute | solution.py:514
  (126 other events, 1235.4 us)

commit v3 on v1

--- a/solution.py
+++ b/solution.py
@@ -41,11 +41,6 @@
     centred = values - average
     variance = jnp.mean(centred * centred, axis=-1, keepdims=True)
     return centred * lax.rsqrt(variance + epsilon) * norm_gain + norm_bias
-
-
-def gelu_tanh(values):
-    inner = 0.7978845608028654 * (values + 0.044715 * values * values * values)
-    return 0.5 * values * (1.0 + jnp.tanh(inner))
 
 
 def low_lanes(shape):
@@ -220,13 +215,15 @@
     lse_ref,
     cos_ref,
     sin_ref,
+    rows_ref,
     out_ref,
+    grad_ref,
     dk_ref,
     dv_ref,
 ):
     dk_ref[...] = jnp.zeros_like(dk_ref)
     dv_ref[...] = jnp.zeros_like(dv_ref)
-    out_ref[0] = jnp.zeros_like(out_ref[0])
+    out_ref[0, :, :LANES] = jnp.zeros((KEY_ROWS, LANES), bf16)
 
     def one_tile(t, _):
         clean_at = pl.multiple_of(CLEAN_OWN + t * TILE, TILE)
@@ -293,7 +290,7 @@
         d_query = jnp.concatenate(d_query, axis=0).T
         for at, part in ((noisy_at, d_query[:TILE]), (clean_at, d_query[TILE:])):
             turned = turn(part, cos_ref[pl.ds(at, TILE), :], -sin_ref[pl.ds(at, TILE), :])
-            out_ref[0, pl.ds(at, TILE), :] = turned.astype(bf16)
+            out_ref[0, pl.ds(at, TILE), :LANES] = turned.astype(bf16)
         return 0
 
     lax.fori_loop(0, TILES, one_tile, 0)
@@ -301,25 +298,43 @@
 
     def finish(i, _):
         rows = pl.ds(pl.multiple_of(i * step, EDGE), step)
-        out_ref[1, rows, :] = turn(dk_ref[rows, :], cos_ref[rows, :], -sin_ref[rows, :]).astype(
-            bf16
-        )
-        out_ref[2, rows, :] = dv_ref[rows, :].astype(bf16)
+        out_ref[0, rows, LANES : 2 * LANES] = turn(
+            dk_ref[rows, :], cos_ref[rows, :], -sin_ref[rows, :]
+        ).astype(bf16)
+        out_ref[0, rows, 2 * LANES :] = dv_ref[rows, :].astype(bf16)
         return 0
 
     lax.fori_loop(0, 9, finish, 0)
 
+    def weight_rows(i, _):
+        rows = pl.ds(pl.multiple_of(i * LANES, LANES), LANES)
+        grad_ref[0, rows, :] = dot(rows_ref[rows, :], out_ref[0]).astype(bf16)
+        return 0
+
+    lax.fori_loop(0, rows_ref.shape[0] // LANES, weight_rows, 0)
+
 
 def attend_backward(
-    spans, clean_bounds, noisy_bounds, query, keys, values, attended, d_attended, lse, cosine, sine
+    spans,
+    clean_bounds,
+    noisy_bounds,
+    query,
+    keys,
+    values,
+    attended,
+    d_attended,
+    lse,
+    cosine,
+    sine,
+    rows_t,
 ):
     count, cols = query.shape
     pairs = cols // LANES
+    width = rows_t.shape[0]
     whole2 = lambda array: pl.BlockSpec(array.shape, lambda p, s: (0, 0))
     whole3 = lambda array: pl.BlockSpec(array.shape, lambda p, s: (0, 0, 0))
     row_spec = pl.BlockSpec((count, LANES), lambda p, s: (0, p))
     own_spec = pl.BlockSpec((TOK_DEV, LANES), lambda p, s: (0, p))
-    work = pairs * 2 * 2 * HALF * TOK_DEV
     return pl.pallas_call(
         backward_kernel,
         grid_spec=pltpu.PrefetchScalarGridSpec(
@@ -332,14 +347,21 @@
                 pl.BlockSpec((1, TILES, 2, 2 * TILE), lambda p, s: (p, 0, 0, 0)),
                 whole2(cosine),
                 whole2(sine),
+                whole2(rows_t),
             ],
-            out_specs=pl.BlockSpec((3, count, LANES), lambda p, s: (0, 0, p)),
+            out_specs=[
+                pl.BlockSpec((1, count, 3 * LANES), lambda p, s: (p, 0, 0)),
+                pl.BlockSpec((1, width, 3 * LANES), lambda p, s: (p, 0, 0)),
+            ],
             scratch_shapes=[pltpu.VMEM((count, LANES), f32)] * 2,
         ),
-        out_shape=jax.ShapeDtypeStruct((3, count, cols), bf16),
+        out_shape=[
+            jax.ShapeDtypeStruct((pairs, count, 3 * LANES), bf16),
+            jax.ShapeDtypeStruct((pairs, width, 3 * LANES), bf16),
+        ],
         name="attend_backward",
         cost_estimate=pl.CostEstimate(
-            flops=10 * work * HD, bytes_accessed=16 * count * cols, transcendentals=work
+            flops=36 * 10**9, bytes_accessed=36 * 10**6, transcendentals=6 * 10**6
         ),
     )(
         spans,
@@ -353,7 +375,523 @@
         lse,
         cosine,
         sine,
-    )
+        rows_t,
+    )
+
+
+def rows_back_kernel(grads_ref, grads2_ref, w_ref, w2_ref, out_ref):
+    total = 0.0
+    for grads, weights in ((grads_ref, w_ref), (grads2_ref, w2_ref)):
+        for pair in range(grads.shape[0]):
+            total = total + dot(grads[pair], weights[pair], NT)
+    out_ref[...] = total
+
+
+def rows_back(grads, grads2, weights, weights2):
+    pairs, count, cols = grads.shape
+    step = count // 9
+    width = weights.shape[1]
+    grad_spec = pl.BlockSpec((pairs, step, cols), lambda i: (0, i, 0))
+    w_spec = pl.BlockSpec(weights.shape, lambda i: (0, 0, 0))
+    return pl.pallas_call(
+        rows_back_kernel,
+        grid=(9,),
+        in_specs=[grad_spec, grad_spec, w_spec, w_spec],
+        out_specs=pl.BlockSpec((step, width), lambda i: (i, 0)),
+        out_shape=jax.ShapeDtypeStruct((count, width), f32),
+        name="rows_back",
+        cost_estimate=pl.CostEstimate(
+            flops=4 * pairs * count * cols * width,
+            bytes_accessed=16 * 10**6,
+            transcendentals=0,
+        ),
+    )(grads, grads2, weights, weights2)
+
+
+PIECES = 16
+MESH = pl.DeviceIdType.MESH
+
+
+def flip(value, mask):
+    result = value
+    for b in range(mask.bit_length()):
+        if mask >> b & 1:
+            result = result + (1 << b) * (1 - 2 * ((value // (1 << b)) % 2))
+    return result
+
+
+class Exchange:
+    names = ("a", "b", "c", "d", "e", "f", "g")
+
+    def __init__(self, bits, count, rows, width):
+        self.bits, self.count, self.rows, self.width = bits, count, rows, width
+        self.half, self.quarter, self.piece = rows // 2, rows // 4, rows // PIECES
+        self.extra = list(range(4, bits))
+
+    def scratch(self):
+        k, w = self.count, self.width
+        shapes = [
+            pltpu.VMEM((k, 2, self.half, w), bf16),
+            pltpu.VMEM((k, self.half, w), bf16),
+            pltpu.VMEM((k, self.half, w), bf16),
+            pltpu.VMEM((k, self.quarter, w), bf16),
+            pltpu.VMEM((k, self.quarter, w), bf16),
+            pltpu.VMEM((k, self.quarter, w), f32),
+            pltpu.VMEM((k, 3, self.piece, w), bf16),
+            pltpu.VMEM((k, 3, self.piece, w), bf16),
+        ]
+        for lanes in (2, 1, 1, 3, 3, 1, 1):
+            shapes += [pltpu.SemaphoreType.DMA((k, lanes))] * 2
+        if self.extra:
+            n = len(self.extra)
+            shapes += [pltpu.VMEM((k, 2 * n, self.piece, w), bf16)]
+            shapes += [pltpu.SemaphoreType.DMA((k, n))] * 2
+        return shapes
+
+    def bind(self, place, part, refs):
+        (self.a_in, self.b_out, self.b_in, self.c_out, self.c_in, self.keep) = refs[:6]
+        self.d_out, self.d_in = refs[6:8]
+        self.sems = {
+            name: (refs[8 + 2 * i], refs[9 + 2 * i]) for i, name in enumerate(self.names)
+        }
+        if self.extra:
+            self.x_buf, self.x_send, self.x_recv = refs[22:25]
+        self.place, self.part = place, part
+        self.core, self.x, self.z = place % 2, (place // 2) % 2, (place // 4) % 4
+        self.sibling = {"dp": flip(place, 1)}
+        self.beside = {"dp": flip(place, 2)}
+        self.across = {"mp": 1 - part}
+        self.peers = [{"dp": flip(place, j << 2)} for j in range(1, 4)]
+        self.partners = [self.sibling, self.beside, self.across] + self.peers
+        self.partners += [{"dp": flip(place, 1 << b)} for b in self.extra]
+        return self
+
+    def greet(self):
+        barrier = pltpu.get_barrier_semaphore()
+        for partner in self.partners:
+            pl.semaphore_signal(barrier, inc=1, device_id=partner, device_id_type=MESH)
+        pl.semaphore_wait(barrier, len(self.partners))
+
+    def copy(self, name, k, lane, source, target, device):
+        out, into = self.sems[name]
+        return pltpu.make_async_remote_copy(
+            src_ref=source,
+            dst_ref=target,
+            send_sem=out.at[k, lane],
+            recv_sem=into.at[k, lane],
+            device_id=device,
+            device_id_type=MESH,
+        )
+
+    def rows_at(self, start, size):
+        return pl.ds(pl.multiple_of(start, PIECES), size)
+
+    def copy_a(self, k, lane, grads):
+        source = grads.at[k, self.rows_at((1 - self.core) * self.half, self.half)]
+        return self.copy("a", k, lane, source, self.a_in.at[k, lane], self.sibling)
+
+    def copy_b(self, k):
+        return self.copy("b", k, 0, self.b_out.at[k], self.b_in.at[k], self.across)
+
+    def copy_c(self, k):
+        return self.copy("c", k, 0, self.c_out.at[k], self.c_in.at[k], self.beside)
+
+    def copy_d(self, k, j):
+        return self.copy("d", k, j, self.d_out.at[k, j], self.d_in.at[k, j], self.peers[j])
+
+    def spot(self, change=0):
+        start = self.core * self.half + self.x * self.quarter
+        return self.rows_at(start + flip(self.z, change) * self.piece, self.piece)
+
+    def copy_e(self, k, j, full):
+        rows = full.at[k, self.spot()]
+        return self.copy("e", k, j, rows, rows, self.peers[j])
+
+    def copy_f(self, k, full):
+        start = self.core * self.half + self.x * self.quarter
+        rows = full.at[k, self.rows_at(start, self.quarter)]
+        return self.copy("f", k, 0, rows, rows, self.beside)
+
+    def copy_g(self, k, full):
+        rows = full.at[k, self.rows_at(self.core * self.half, self.half)]
+        return self.copy("g", k, 0, rows, rows, self.sibling)
+
+    def start_a(self, k, lane, grads):
+        self.copy_a(k, lane, grads).start()
+
+    def stage_b(self, k, others):
+        self.copy_a(k, 0, others).wait()
+        mine = others[k, self.rows_at(self.core * self.half, self.half), :].astype(f32)
+        self.b_out[k] = (mine + self.a_in[k, 0].astype(f32)).astype(bf16)
+        self.copy_b(k).start()
+
+    def stage_c(self, k, grads):
+        self.copy_a(k, 1, grads).wait()
+        self.copy_b(k).wait()
+
+        def total(which):
+            inner = which * self.quarter
+            rows = self.rows_at(inner, self.quarter)
+            mine = grads[k, self.rows_at(self.core * self.half + inner, self.quarter), :]
+            got = self.a_in[k, 1, rows, :].astype(f32) + self.b_in[k, rows, :].astype(f32)
+            return mine.astype(f32) + got
+
+        self.c_out[k] = total(1 - self.x).astype(bf16)
+        self.copy_c(k).start()
+        self.keep[k] = total(self.x)
+
+    def stage_d(self, k):
+        self.copy_c(k).wait()
+        for j in range(4):
+            rows = self.rows_at(flip(self.z, j) * self.piece, self.piece)
+            total = self.keep[k, rows, :] + self.c_in[k, rows, :].astype(f32)
+            if j:
+                self.d_out[k, j - 1] = total.astype(bf16)
+                self.copy_d(k, j - 1).start()
+            else:
+                self.keep[k, rows, :] = total
+
+    def stage_e(self, k, full):
+        rows = self.rows_at(self.z * self.piece, self.piece)
+        total = self.keep[k, rows, :]
+        for j in range(3):
+            self.copy_d(k, j).wait()
+            total = total + self.d_in[k, j].astype(f32)
+        for i, b in enumerate(self.extra):
+            mine = self.x_buf.at[k, 2 * i]
+            mine[...] = total.astype(bf16)
+            swap = pltpu.make_async_remote_copy(
+                src_ref=mine,
+                dst_ref=self.x_buf.at[k, 2 * i + 1],
+                send_sem=self.x_send.at[k, i],
+                recv_sem=self.x_recv.at[k, i],
+                device_id={"dp": flip(self.place, 1 << b)},
+                device_id_type=MESH,
+            )
+            swap.start()
+            swap.wait()
+            total = total.astype(bf16).astype(f32) + self.x_buf[k, 2 * i + 1].astype(f32)
+        full[k, self.spot(), :] = total.astype(bf16)
+        for j in range(3):
+            self.copy_e(k, j, full).start()
+
+    def stage_f(self, k, full):
+        for j in range(3):
+            self.copy_e(k, j, full).wait()
+        self.copy_f(k, full).start()
+
+    def stage_g(self, k, full):
+        self.copy_f(k, full).wait()
+        self.copy_g(k, full).start()
+
+    def stage_h(self, k, full):
+        self.copy_g(k, full).wait()
+
+
+def at_step(step, count, action):
+    @pl.when(jnp.logical_and(step >= 0, step < count))
+    def _():
+        action(step)
+
+
+HIDDEN_TILE = 256
+ROW_TILE = 256
+
+
+def normal(values):
+    average = jnp.mean(values, axis=-1, keepdims=True)
+    centred = values - average
+    variance = jnp.mean(centred * centred, axis=-1, keepdims=True)
+    scale = lax.rsqrt(variance + epsilon)
+    return centred * scale, scale
+
+
+def middle_kernel(exchange, tiles, *refs):
+    (
+        x_ref,
+        att_ref,
+        att2_ref,
+        wout_ref,
+        wout2_ref,
+        dy_ref,
+        gain_ref,
+        shift_ref,
+        bdown_ref,
+        bup_ref,
+        up_hbm,
+        down_hbm,
+        out_ref,
+        mid_ref,
+        datt_ref,
+        datt2_ref,
+        gout_ref,
+        gout2_ref,
+        gbup_ref,
+        small_ref,
+        full_ref,
+        up_buf,
+        down_buf,
+        load_sem,
+        n2_ref,
+        total_ref,
+        dn2_ref,
+        act_ref,
+        dpre_ref,
+        grad_ref,
+        *rest,
+    ) = refs
+    place, part = lax.axis_index("dp"), lax.axis_index("mp")
+    ex = exchange.bind(place, part, rest)
+    count = ex.count
+    rows_all = x_ref.shape[0]
+    blocks = rows_all // ROW_TILE
+    width = x_ref.shape[1]
+
+    def loads(i):
+        slot = i % 2
+        cols = pl.ds(pl.multiple_of(i * HIDDEN_TILE, HIDDEN_TILE), HIDDEN_TILE)
+        return (
+            pltpu.make_async_copy(up_hbm.at[:, cols], up_buf.at[slot], load_sem.at[slot, 0]),
+            pltpu.make_async_copy(down_hbm.at[cols, :], down_buf.at[slot], load_sem.at[slot, 1]),
+        )
+
+    for load in loads(0):
+        load.start()
+    ex.greet()
+
+    def prologue(r, _):
+        rows = pl.ds(pl.multiple_of(r * ROW_TILE, ROW_TILE), ROW_TILE)
+        branch = dot(att_ref[rows, :], wout_ref[...]) + dot(att2_ref[rows, :], wout2_ref[...])
+        mid = x_ref[rows, :].astype(f32) + branch
+        mid_ref[rows, :] = mid
+        n2_ref[rows, :] = (normal(mid)[0] * gain_ref[...] + shift_ref[...]).astype(bf16)
+        total_ref[rows, :] = mid + bdown_ref[...]
+        dn2_ref[rows, :] = jnp.zeros((ROW_TILE, width), f32)
+        return 0
+
+    lax.fori_loop(0, blocks, prologue, 0)
+
+    def tile(i):
+        slot = i % 2
+        for load in loads(i):
+            load.wait()
+
+        @pl.when(i + 1 < tiles)
+        def _():
+            for load in loads(i + 1):
+                load.start()
+
+        up, down = up_buf.at[slot], down_buf.at[slot]
+        bias_grad = jnp.zeros((1, HIDDEN_TILE), f32)
+        for r in range(blocks):
+            rows = slice(r * ROW_TILE, (r + 1) * ROW_TILE)
+            pre = dot(n2_ref[rows, :], up[...]) + bup_ref[i]
+            square = pre * pre
+            bend = jnp.tanh(0.7978845608028654 * (pre + 0.044715 * square * pre))
+            part_one = 0.5 * (1.0 + bend)
+            act = (pre * part_one).astype(bf16)
+            slope = part_one + (0.5 * pre) * (1.0 - bend * bend) * (
+                0.7978845608028654 * (1.0 + 3.0 * 0.044715 * square)
+            )
+            d_act = dot(dy_ref[rows, :], down[...], NT)
+            d_pre = (d_act * slope).astype(bf16)
+            act_ref[rows, :] = act
+            dpre_ref[rows, :] = d_pre
+            bias_grad = bias_grad + jnp.sum(d_pre.astype(f32), axis=0, keepdims=True)
+            total_ref[rows, :] += dot(act, down[...])
+            dn2_ref[rows, :] += dot(d_pre, up[...], NT)
+        gbup_ref[i] = bias_grad
+        k = i % count
+        grad_ref[k, :, :width] = dot(act_ref[...].T, dy_ref[...]).astype(bf16)
+        grad_ref[k, :, width:] = dot(dpre_ref[...].T, n2_ref[...]).astype(bf16)
+
+    def steps(i, lanes):
+        at_step(i - count - 7, count, lambda k: ex.stage_h(k, full_ref))
+        at_step(i - count - 6, count, lambda k: ex.stage_g(k, full_ref))
+        at_step(i - count - 5, count, lambda k: ex.stage_f(k, full_ref))
+        at_step(i - count - 4, count, lambda k: ex.stage_e(k, full_ref))
+        at_step(i - count - 3, count, lambda k: ex.stage_d(k))
+        at_step(i - count - 2, count, lambda k: ex.stage_c(k, grad_ref))
+        at_step(i - 1, count, lambda k: ex.stage_b(k, grad_ref))
+
+    def main(i, _):
+        tile(i)
+        at_step(i, count, lambda k: ex.start_a(k, 0, grad_ref))
+        at_step(i - count, count, lambda k: ex.start_a(k, 1, grad_ref))
+        steps(i, None)
+        return 0
+
+    lax.fori_loop(0, tiles, main, 0)
+
+    def epilogue(r, sums):
+        rows = pl.ds(pl.multiple_of(r * ROW_TILE, ROW_TILE), ROW_TILE)
+        out_ref[rows, :] = total_ref[rows, :].astype(bf16)
+        unit, scale = normal(mid_ref[rows, :])
+        d_rows = dn2_ref[rows, :]
+        dy = dy_ref[rows, :].astype(f32)
+        lean = d_rows * gain_ref[...]
+        d_mid = dy + scale * (
+            lean
+            - jnp.mean(lean, axis=-1, keepdims=True)
+            - unit * jnp.mean(lean * unit, axis=-1, keepdims=True)
+        )
+        mid_ref[rows, :] = d_mid
+        d_branch = d_mid.astype(bf16)
+        n2_ref[rows, :] = d_branch
+        datt_ref[rows, :] = dot(d_branch, wout_ref[...], NT).astype(bf16)
+        datt2_ref[rows, :] = dot(d_branch, wout2_ref[...], NT).astype(bf16)
+        add = lambda values: jnp.sum(values, axis=0, keepdims=True)
+        return (sums[0] + add(d_rows * unit), sums[1] + add(d_rows), sums[2] + add(dy))
+
+    zero = jnp.zeros((1, width), f32)
+    sums = lax.fori_loop(0, blocks, epilogue, (zero, zero, zero))
+    for j in range(3):
+        small_ref[j : j + 1, :] = sums[j]
+    gout_ref[...] = dot(att_ref[...].T, n2_ref[...]).astype(bf16)
+    gout2_ref[...] = dot(att2_ref[...].T, n2_ref[...]).astype(bf16)
+
+    def drain(i, _):
+        steps(i, None)
+        return 0
+
+    lax.fori_loop(tiles, tiles + count + 2, drain, 0)
+
+
+def middle(bits, x, att, att2, wout, wout2, dy, gain, shift, bdown, bup, up, down):
+    rows, width = x.shape
+    hidden = up.shape[1]
+    tiles = hidden // HIDDEN_TILE
+    count = tiles // 2
+    exchange = Exchange(bits, count, HIDDEN_TILE, 2 * width)
+    vmem = pl.BlockSpec(memory_space=pltpu.VMEM)
+    hbm = pl.BlockSpec(memory_space=pl.ANY)
+    shape = jax.ShapeDtypeStruct
+    return pl.pallas_call(
+        functools.partial(middle_kernel, exchange, tiles),
+        in_specs=[vmem] * 10 + [hbm] * 2,
+        out_specs=[vmem] * 9,
+        out_shape=[
+            shape((rows, width), bf16),
+            shape((rows, width), f32),
+            shape(att.shape, bf16),
+            shape(att2.shape, bf16),
+            shape(wout.shape, bf16),
+            shape(wout2.shape, bf16),
+            shape((tiles, 1, HIDDEN_TILE), f32),
+            shape((8, width), f32),
+            shape((count, HIDDEN_TILE, 2 * width), bf16),
+        ],
+        scratch_shapes=[
+            pltpu.VMEM((2, width, HIDDEN_TILE), bf16),
+            pltpu.VMEM((2, HIDDEN_TILE, width), bf16),
+            pltpu.SemaphoreType.DMA((2, 2)),
+            pltpu.VMEM((rows, width), bf16),
+            pltpu.VMEM((rows, width), f32),
+            pltpu.VMEM((rows, width), f32),
+            pltpu.VMEM((rows, HIDDEN_TILE), bf16),
+            pltpu.VMEM((rows, HIDDEN_TILE), bf16),
+            pltpu.VMEM((count, HIDDEN_TILE, 2 * width), bf16),
+        ]
+        + exchange.scratch(),
+        compiler_params=pltpu.CompilerParams(
+            collective_id=0, has_side_effects=True, vmem_limit_bytes=67043328
+        ),
+        name="middle",
+        cost_estimate=pl.CostEstimate(
+            flops=40 * 10**9, bytes_accessed=40 * 10**6, transcendentals=4 * 10**6
+        ),
+    )(x, att, att2, wout, wout2, dy, gain, shift, bdown, bup, up, down)
+
+
+def sum_kernel(
+    exchange, mine_ref, others_ref, small_ref, small2_ref, full_ref, sums_ref, got_ref, work_ref, small_send, small_recv, *rest
+):
+    place, part = lax.axis_index("dp"), lax.axis_index("mp")
+    ex = exchange.bind(place, part, rest)
+    count, bits = ex.count, ex.bits
+    ex.greet()
+
+    def small_copy(s):
+        source = small2_ref if s == 0 else work_ref.at[s - 1]
+        device = ex.across if s == 0 else {"dp": flip(place, 1 << (s - 1))}
+        return pltpu.make_async_remote_copy(
+            src_ref=source,
+            dst_ref=got_ref.at[s],
+            send_sem=small_send.at[s],
+            recv_sem=small_recv.at[s],
+            device_id=device,
+            device_id_type=MESH,
+        )
+
+    def small_step(s):
+        small_copy(s).wait()
+        before = small_ref[...] if s == 0 else work_ref[s - 1]
+        work_ref[s] = before + got_ref[s]
+        if s < bits:
+            small_copy(s + 1).start()
+        else:
+            sums_ref[...] = work_ref[s]
+
+    def begin(k, _):
+        ex.start_a(k, 0, others_ref)
+        return 0
+
+    lax.fori_loop(0, count, begin, 0)
+    small_copy(0).start()
+
+    def second(k, _):
+        ex.start_a(k, 1, mine_ref)
+        return 0
+
+    lax.fori_loop(0, count, second, 0)
+
+    def cross(k, _):
+        ex.stage_b(k, others_ref)
+        return 0
+
+    lax.fori_loop(0, count, cross, 0)
+
+    def steps(i, _):
+        at_step(i - 5, count, lambda k: ex.stage_h(k, full_ref))
+        at_step(i - 4, count, lambda k: ex.stage_g(k, full_ref))
+        at_step(i - 3, count, lambda k: ex.stage_f(k, full_ref))
+        at_step(i - 2, count, lambda k: ex.stage_e(k, full_ref))
+        at_step(i - 1, count, lambda k: ex.stage_d(k))
+        at_step(i, count, lambda k: ex.stage_c(k, mine_ref))
+        for s in range(bits + 1):
+            pl.when(i == s + 1)(functools.partial(small_step, s))
+        return 0
+
+    lax.fori_loop(0, count + 6, steps, 0)
+
+
+def sum_chunks(bits, mine, others, small, small2):
+    count, rows, width = mine.shape
+    exchange = Exchange(bits, count, rows, width)
+    vmem = pl.BlockSpec(memory_space=pltpu.VMEM)
+    return pl.pallas_call(
+        functools.partial(sum_kernel, exchange),
+        in_specs=[vmem] * 4,
+        out_specs=[vmem] * 2,
+        out_shape=[
+            jax.ShapeDtypeStruct(mine.shape, bf16),
+            jax.ShapeDtypeStruct(small.shape, f32),
+        ],
+        scratch_shapes=[
+            pltpu.VMEM((bits + 1,) + small.shape, f32),
+            pltpu.VMEM((bits + 1,) + small.shape, f32),
+            pltpu.SemaphoreType.DMA((bits + 1,)),
+            pltpu.SemaphoreType.DMA((bits + 1,)),
+        ]
+        + exchange.scratch(),
+        compiler_params=pltpu.CompilerParams(
+            collective_id=1, has_side_effects=True, vmem_limit_bytes=67043328
+        ),
+        name="sum_chunks",
+        cost_estimate=pl.CostEstimate(
+            flops=40 * 10**9, bytes_accessed=40 * 10**6, transcendentals=0
+        ),
+    )(mine, others, small, small2)
 
 
 def key_layout(seq_lengths, block_len, part):
@@ -408,6 +946,10 @@
     return jnp.concatenate(
         [jnp.where(flip, mine, theirs), jnp.where(flip, theirs, mine)], axis=0
     )
+
+
+def tie(first, second):
+    return lax.optimization_barrier((first, second))
 
 
 def local(
@@ -431,46 +973,30 @@
     part = lax.axis_index("mp")
     place = lax.axis_index("dp")
     bits = dp_size.bit_length() - 1
-    across = [(0, 1), (1, 0)]
-    flips = [[(i, i ^ (1 << b)) for i in range(dp_size)] for b in range(bits)]
-    my_bit = [(place >> b) & 1 for b in range(bits)]
-
-    def to_partner(array):
-        return lax.ppermute(array, "mp", across)
-
-    def to_flip(array, b):
-        return lax.ppermute(array, "dp", flips[b])
-
-    def fetch(weights):
-        here = to_partner(half_of(weights, my_bit[0]))
-        there = to_flip(here, 0)
-        return in_order(my_bit[0], here, there)
-
-    def reduce_over_all(mine, others):
-        core = my_bit[0]
-        got = to_flip(half_of(others, 1 - core).astype(bf16), 0)
-        crossing = half_of(others, core) + got.astype(f32)
-        got_own = to_flip(half_of(mine, 1 - core).astype(bf16), 0)
-        total = half_of(mine, core) + got_own.astype(f32)
-        total = total + to_partner(crossing.astype(bf16)).astype(f32)
-        for b in range(1, bits):
-            got = to_flip(half_of(total, 1 - my_bit[b]).astype(bf16), b)
-            total = half_of(total, my_bit[b]) + got.astype(f32)
-        total = total.astype(bf16)
-        for b in reversed(range(bits)):
-            total = in_order(my_bit[b], total, to_flip(total, b))
-        return total.astype(f32)
-
+
+    def across(array):
+        return lax.ppermute(array, "mp", [(0, 1), (1, 0)])
+
+    def sibling(array):
+        return lax.ppermute(array, "dp", [(i, i ^ 1) for i in range(dp_size)])
+
+    def fetch(half):
+        here = across(half)
+        return here, sibling(here)
+
+    core = place & 1
     edge = jnp.where(part == 0, tokens[0, HALF - EDGE :], tokens[0, :EDGE])
-    context = to_partner(jnp.concatenate([tokens[1], edge], axis=0))
+    context = across(jnp.concatenate([tokens[1], edge], axis=0))
     qkv_mine = w_qkv.transpose(1, 0, 2)
-    qkv_other = fetch(w_qkv.transpose(1, 0, 2).reshape(-1, w_qkv.shape[2])).reshape(
-        qkv_mine.shape
-    )
-    out_other = fetch(w_out)
-    up_other = fetch(w_up)
-    bias_other = to_partner(b_up)
-    down_other = fetch(w_down)
+    halves = [
+        half_of(qkv_mine.reshape(-1, w_qkv.shape[2]), core),
+        half_of(w_out, core),
+        half_of(w_up, core),
+        half_of(w_down, core),
+    ]
+    context, halves = tie(context, halves)
+    fetched = [fetch(half) for half in halves]
+    bias_other = across(b_up)
 
     spans, clean_bounds, noisy_bounds, cosine, sine = key_layout(lengths[0], block_size[0], part)
     clean_other, edge_other = context[:HALF], context[HALF:]
@@ -478,53 +1004,47 @@
         [clean_other, tokens[1], clean_other[:EDGE], edge_other, tokens[0], edge_other], axis=0
     )
     normed1_keys = layer_norm(key_tokens.astype(f32), ln1_gain, ln1_bias).astype(bf16)
-
-    saved = []
-    for weights in (qkv_mine, qkv_other):
+    normed1_t = normed1_keys.T
+
+    def attention(weights):
         query, keys, values = project(normed1_keys, weights, cosine, sine)
         attended, lse = attend_forward(spans, clean_bounds, noisy_bounds, query, keys, values)
-        saved.append((query, keys, values, attended, lse))
-
-    x_rows = tokens.astype(f32).reshape(TOK_DEV, width)
-    branch = dot(saved[0][3], w_out) + dot(saved[1][3], out_other)
-    mid = x_rows + branch
-    normed2, norm2_back = jax.vjp(layer_norm, mid, ln2_gain, ln2_bias)
-    mlp_rows = normed2.astype(bf16)
-    d_low = cotangent.reshape(TOK_DEV, width)
-    d_out_rows = d_low.astype(f32)
-    grad_b_down = jnp.sum(d_out_rows, axis=0)
-    down = 0.0
-    d_normed2 = 0.0
-    grad_down, grad_up, grad_up_bias = [], [], []
-    for up, bias, down_w in ((w_up, b_up, w_down), (up_other, bias_other, down_other)):
-        pre = dot(mlp_rows, up) + bias.astype(f32)
-        act_low = gelu_tanh(pre).astype(bf16)
-        down = down + dot(act_low, down_w)
-        d_act = dot(d_low, down_w, NT)
-        d_pre = jax.vjp(gelu_tanh, pre)[1](d_act)[0].astype(bf16)
-        grad_down.append(jnp.einsum("rf,rd->fd", act_low, d_low, preferred_element_type=f32))
-        grad_up.append(jnp.einsum("rd,rf->df", mlp_rows, d_pre, preferred_element_type=f32))
-        grad_up_bias.append(jnp.sum(d_pre.astype(f32), axis=0))
-        d_normed2 = d_normed2 + dot(d_pre, up, NT)
-    out = (mid + down + b_down).astype(bf16).reshape(tokens.shape)
-    grad_down = reduce_over_all(*grad_down)
-    grad_up = reduce_over_all(*grad_up)
-
-    d_mid_norm, grad_ln2_gain, grad_ln2_bias = norm2_back(d_normed2)
-    d_mid = d_out_rows + d_mid_norm
-    d_branch = d_mid.astype(bf16)
-    grad_out = []
-    d_attended = []
-    for item, weights in zip(saved, (w_out, out_other)):
-        grad_out.append(jnp.einsum("rf,rd->fd", item[3], d_branch, preferred_element_type=f32))
-        d_attended.append(dot(d_branch, weights, NT).astype(bf16))
-    grad_out = reduce_over_all(*grad_out)
-
-    grad_qkv = [None, None]
-    d_normed1_keys = 0.0
-    for group, weights in ((1, qkv_other), (0, qkv_mine)):
-        query, keys, values, attended, lse = saved[group]
-        d_qkv = attend_backward(
+        return (query, keys, values, attended, lse)
+
+    mine = attention(qkv_mine)
+    fetched[0] = tie(fetched[0], mine[3])[0]
+    qkv_other = in_order(core, *fetched[0]).reshape(qkv_mine.shape)
+    other = attention(qkv_other)
+    fetched[1:] = tie(fetched[1:], other[3])[0]
+    out_other, up_other, down_other = [in_order(core, *pieces) for pieces in fetched[1:]]
+    up_all = jnp.concatenate([up_other, w_up], axis=1)
+    down_all = jnp.concatenate([down_other, w_down], axis=0)
+    bias_all = jnp.concatenate([bias_other, b_up]).astype(f32).reshape(-1, 1, HIDDEN_TILE)
+
+    as_row = lambda vector: vector.reshape(1, -1)
+    out, d_mid, d_att, d_att2, grad_out, grad_out2, grad_bias, norms, full = middle(
+        bits,
+        tokens.reshape(TOK_DEV, width),
+        mine[3],
+        other[3],
+        w_out,
+        out_other,
+        cotangent.reshape(TOK_DEV, width),
+        as_row(ln2_gain),
+        as_row(ln2_bias),
+        as_row(b_down),
+        bias_all,
+        up_all,
+        down_all,
+    )
+    hidden = b_up.shape[0]
+    grad_down = full[:, :, :width].reshape(hidden, width).astype(f32)
+    grad_up = full[:, :, width:].reshape(hidden, width).T.astype(f32)
+
+    d_qkv, grad_qkv = [], []
+    for saved, d_attended in ((other, d_att2), (mine, d_att)):
+        query, keys, values, attended, lse = saved
+        d_fields, grad = attend_backward(
             spans,
             clean_bounds,
             noisy_bounds,
@@ -532,23 +1052,25 @@
             keys,
             values,
             attended,
-            d_attended[group],
+            d_attended,
             lse,
             cosine,
             sine,
+            normed1_t,
         )
-        grad_qkv[group] = jnp.einsum(
-            "rd,crf->cdf", normed1_keys, d_qkv, preferred_element_type=f32
-        ).reshape(-1, d_qkv.shape[2])
-        d_normed1_keys = d_normed1_keys + jnp.einsum(
-            "crf,cdf->rd", d_qkv, weights, preferred_element_type=f32
-        )
-    grad_qkv = reduce_over_all(*grad_qkv).reshape(qkv_mine.shape).transpose(1, 0, 2)
-
+        d_qkv.append(d_fields)
+        grad_qkv.append(grad)
+    pairs = mine[0].shape[1] // LANES
+
+    def by_pair(weights):
+        split = weights.reshape(3, width, pairs, LANES)
+        return split.transpose(2, 1, 0, 3).reshape(pairs, width, 3 * LANES)
+
+    d_normed1_keys = rows_back(d_qkv[1], d_qkv[0], by_pair(qkv_mine), by_pair(qkv_other))
     clean_back = d_normed1_keys[:HALF]
     clean_back = clean_back.at[:EDGE].add(d_normed1_keys[2 * HALF : 2 * HALF + EDGE])
     edge_back = d_normed1_keys[NOISY_BASE:NOISY_OWN] + d_normed1_keys[NOISY_OWN + HALF :]
-    back = to_partner(jnp.concatenate([clean_back, edge_back], axis=0).astype(bf16)).astype(f32)
+    back = across(jnp.concatenate([clean_back, edge_back], axis=0).astype(bf16)).astype(f32)
     at_end = jnp.concatenate([jnp.zeros((HALF - EDGE, width), f32), back[HALF:]], axis=0)
     at_start = jnp.concatenate([back[HALF:], jnp.zeros((HALF - EDGE, width), f32)], axis=0)
     d_normed1 = jnp.concatenate(
@@ -559,34 +1081,49 @@
         ],
         axis=0,
     )
+    x_rows = tokens.astype(f32).reshape(TOK_DEV, width)
     norm1_back = jax.vjp(layer_norm, x_rows, ln1_gain, ln1_bias)[1]
     d_x_norm, grad_ln1_gain, grad_ln1_bias = norm1_back(d_normed1)
     grad_tokens = (d_mid + d_x_norm).reshape(tokens.shape)
-
-    bias_sum = to_partner(grad_up_bias[1]) + grad_up_bias[0]
-    hidden = bias_sum.shape[0]
-    own_bias = jnp.concatenate([jnp.where(part == 0, bias_sum, 0.0), jnp.where(part == 0, 0.0, bias_sum)])
-    small = lax.psum(
-        jnp.concatenate(
-            [own_bias, grad_ln1_gain, grad_ln1_bias, grad_ln2_gain, grad_ln2_bias, grad_b_down]
-        ),
-        ("dp", "mp"),
-    )
-    grad_up_bias = lax.dynamic_slice_in_dim(small, part * hidden, hidden, 0)
-    rest = [small[2 * hidden + i * width : 2 * hidden + (i + 1) * width] for i in range(5)]
+    shared = jnp.concatenate(
+        [norms[:3], as_row(grad_ln1_gain), as_row(grad_ln1_bias), jnp.zeros((1, width), f32)],
+        axis=0,
+    )
+    bias2, bias1 = grad_bias.reshape(2, hidden // width, width)
+
+    def chunks(of_qkv, of_out):
+        lanes = 3 * LANES
+        flat = jnp.concatenate([of_out[:, :lanes], of_out[:, lanes:]], axis=0)
+        return jnp.concatenate(
+            [of_qkv.reshape(-1, ROW_TILE, lanes), flat.reshape(-1, ROW_TILE, lanes)], axis=0
+        )
+
+    full2, sums = sum_chunks(
+        bits,
+        chunks(grad_qkv[1], grad_out),
+        chunks(grad_qkv[0], grad_out2),
+        jnp.concatenate([bias1, shared], axis=0),
+        jnp.concatenate([bias2, shared], axis=0),
+    )
+    split = pairs * width // ROW_TILE
+    grad_qkv = full2[:split].reshape(pairs, width, 3, LANES).transpose(1, 2, 0, 3)
+    grad_qkv = grad_qkv.reshape(w_qkv.shape).astype(f32)
+    flat = full2[split:].reshape(2, w_out.shape[0], 3 * LANES)
+    grad_out = jnp.concatenate([flat[0], flat[1]], axis=1).astype(f32)
+    lead = hidden // width
     return (
-        out,
+        out.reshape(tokens.shape),
         grad_tokens,
-        rest[0],
-        rest[1],
+        sums[lead + 3],
+        sums[lead + 4],
         grad_qkv,
         grad_out,
-        rest[2],
-        rest[3],
+        sums[lead],
+        sums[lead + 1],
         grad_up,
-        grad_up_bias,
+        sums[:lead].reshape(hidden),
         grad_down,
-        rest[4],
+        sums[lead + 2],
     )
 
 

time: 668 us -> 590 us (0.88)
  Pallas kernels: 112 us -> 366 us
  waiting for transfers between devices: 175 us -> 30.3 us
  matrix products: 103 us -> 0 us
  starting transfers between devices: 113 us -> 36.9 us
  blocking collectives: 39.7 us -> 0 us
  local copies, waits for them, and re-layouts: 51.7 us -> 80.6 us
    pallas_call x0 -> x3, Pallas kernels: none -> 221 us  [the longest x1 130 us: middle(): pl.pallas_call(functools.partial(middle_kernel, exchange, tiles), in_spec...]
    ppermute x52 -> x11, waiting for transfers between devices: 175 us -> 30.3 us  [the longest x7 30.3 us: across(): return lax.ppermute(array, 'mp', [(0, 1), (1, 0)])]
    dot_general x22 -> x0, matrix products: 103 us -> none  [the longest x12 56.3 us: dot(): return lax.dot_general(left, right, dims, preferred_element_type=f32)]
    ppermute x52 -> x11, starting transfers between devices: 113 us -> 36.9 us  [the longest x7 36.3 us: across(): return lax.ppermute(array, 'mp', [(0, 1), (1, 0)])]
    psum x1 -> x0, blocking collectives: 39.7 us -> none  [local(): lax.psum(jnp.concatenate([own_bias, grad_ln1_gain, grad_ln1_bias, grad_ln...]
    pallas_call x2, Pallas kernels: 52.8 us -> 77 us  [attend_backward(): pl.pallas_call(backward_kernel, grid_spec=pltpu.PrefetchScalarGridSpec(nu...]
    concatenate x1 -> x7, other arithmetic: 0.94 us -> 18.7 us  [the longest x1 11.1 us: local(): up_all = jnp.concatenate([up_other, w_up], axis=1)]
    slice x1 -> x15, local copies, waits for them, and re-layouts: 0.61 us -> 10.7 us  [the longest x1 2.68 us: local(): grad_down = full[:, :, :width].reshape(hidden, width).astype(f32)]
  transfers between devices with their start and end apart: 52 -> 11, of which waited for: 20 -> 2; matrix products, arithmetic and copies ran while one was open for 30% -> 12% of each run, Pallas kernels for 17% -> 12%
where the time goes in v3:
time: 590 us; the launch traced here: 580 us
  Pallas kernels  366 us (62%)
  local copies, waits for them, and re-layouts  80.6 us (14%)
  other arithmetic  63.6 us (11%)
  starting transfers between devices  36.9 us (6%)
  waiting for transfers between devices  30.3 us (5%)
    pallas_call x1, Pallas kernels, middle(): pl.pallas_call(functools.partial(middle_kernel, exchange, tiles), in_spec...  130 us
    pallas_call x2, Pallas kernels, attend_backward(): pl.pallas_call(backward_kernel, grid_spec=pltpu.PrefetchScalarGridSpec(nu...  77 us
    pallas_call x1, Pallas kernels, sum_chunks(): pl.pallas_call(functools.partial(sum_kernel, exchange), in_specs=[vmem] *...  76.5 us
    pallas_call x2, Pallas kernels, attend_forward(): pl.pallas_call(forward_kernel, grid_spec=pltpu.PrefetchScalarGridSpec(num...  47.4 us
    ppermute x7, starting transfers between devices, across(): return lax.ppermute(array, 'mp', [(0, 1), (1, 0)])  36.3 us
    ppermute x7, waiting for transfers between devices, across(): return lax.ppermute(array, 'mp', [(0, 1), (1, 0)])  30.3 us
    pallas_call x2, Pallas kernels, project(): pl.pallas_call(project_kernel, grid=(9,), in_specs=[row_spec, pl.BlockSpe...  20 us
    pallas_call x1, Pallas kernels, rows_back(): pl.pallas_call(rows_back_kernel, grid=(9,), in_specs=[grad_spec, grad_spe...  14.9 us
  transfers between devices with their start and end apart: 11, of which 2 were waited for; matrix products, arithmetic and copies ran while one was open for 12% of the time, Pallas kernels for 12%

profile of v3, /device:TPU:0, one launch (start us, length us, event | category | flops | bytes accessed | tf_op | source)
XLA Modules:
  0.0 579.7 jit_solution(13930586564340552126)
XLA Ops:
  1.4 2.4 fusion.35
  4.6 1.2 copy.95
  5.8 3.0 collective-permute-start
  11.6 2.4 constant_dynamic-slice_fusion
  14.0 1.1 constant_dynamic-slice_fusion.1
  15.1 2.3 constant_dynamic-slice_fusion.3
  19.4 4.4 fusion.10
  24.5 1.2 copy.114
  27.4 0.9 copy.105
  28.4 2.2 copy.108.w_ref
  33.4 1.5 copy.96
  34.9 0.8 copy.98
  35.9 0.9 slice.176
  36.8 3.9 concatenate.93
  41.9 2.0 collective-permute-start.1
  44.7 2.0 collective-permute-start.7
  46.7 2.4 fusion.5
  49.1 4.4 copy.101.rows_ref
  53.6 11.0 %collective-permute-done.1 = bf16[1152,384]{1,0:T(8,128)(2,1)} collective-permute-done((bf16[1152,384]{1,0:T(8,128)(2,1)S(1)}, bf16[1152,384]{1,0:T(8,128)(2,1)}, u32[]{:S(2)}, u32[]{:S(2)}) %collective-permute-start.1) | collective-permute-done | bytes 884768 | tf_op jit(solution)/shard_map/ppermute | solution.py:978
  64.5 2.4 fusion.41.rows_ref
  67.0 10.0 %project.2 = (bf16[1584,384]{1,0:T(8,128)(2,1)}, bf16[1584,384]{1,0:T(8,128)(2,1)}, bf16[1584,384]{1,0:T(8,128)(2,1)}) custom-call(bf16[1584,768]{1,0:T(8,128)(2,1)} %copy.101.rows_ref, bf16[3,768,384]{2,1,0:T(8,128)(2,1)} %bitcast.84, f32[1584,128]{1,0:T(8,128)} %get-tuple-element.186.cos_ref, f32[1584,128]{1,0:T(8,128)} %get-tuple-element.185.sin_ref), custom_call_target="tpu_custom_call" | custom-call | flops 2802843648 | bytes 7852032 | tf_op jit(solution)/shard_map/project/pallas_call | solution.py:80
  77.0 23.7 %attend_forward.2 = (bf16[1024,384]{1,0:T(8,128)(2,1)}, f32[3,4,2,256]{3,2,1,0:T(2,128)}) custom-call(s32[4,2]{1,0:T(4,128)} %pad_add_fusion.1.span_ref, s32[4,2,256]{2,1,0:T(2,128)} %add_add_fusion.2.clean_ref, s32[4,2,128]{2,1,0:T(2,128)} %pad_add_fusion.noisy_ref, bf16[1584,384]{1,0:T(8,128)(2,1)} %get-tuple-element.63.q_ref, ...), custom_call_target="tpu_custom_call" | custom-call | flops 1610612736 | bytes 4866048 | tf_op jit(solution)/shard_map/attend_forward/pallas_call | solution.py:184
  100.7 19.3 %collective-permute-done.3 = bf16[192,768]{1,0:T(8,128)(2,1)} collective-permute-done((bf16[192,768]{1,0:T(8,128)(2,1)}, bf16[192,768]{1,0:T(8,128)(2,1)}, u32[]{:S(2)}, u32[]{:S(2)}) %collective-permute-start.3) | collective-permute-done | bytes 294944 | tf_op jit(solution)/shard_map/ppermute | solution.py:978
  120.5 1.6 broadcast_select_fusion.5
  122.2 1.4 pad_maximum_fusion.5
  123.5 4.6 reshape_reshape.3
  128.1 3.2 copy.107
  131.3 3.9 copy.109.w2_ref
  135.2 10.0 %project.3 = (bf16[1584,384]{1,0:T(8,128)(2,1)}, bf16[1584,384]{1,0:T(8,128)(2,1)}, bf16[1584,384]{1,0:T(8,128)(2,1)}) custom-call(bf16[1584,768]{1,0:T(8,128)(2,1)} %copy.101.rows_ref, bf16[3,768,384]{2,1,0:T(8,128)(2,1)} %bitcast.78, f32[1584,128]{1,0:T(8,128)} %get-tuple-element.186.cos_ref, f32[1584,128]{1,0:T(8,128)} %get-tuple-element.185.sin_ref), custom_call_target="tpu_custom_call" | custom-call | flops 2802843648 | bytes 7852032 | tf_op jit(solution)/shard_map/project/pallas_call | solution.py:80
  145.2 23.7 %attend_forward.3 = (bf16[1024,384]{1,0:T(8,128)(2,1)}, f32[3,4,2,256]{3,2,1,0:T(2,128)}) custom-call(s32[4,2]{1,0:T(4,128)} %pad_add_fusion.1.span_ref, s32[4,2,256]{2,1,0:T(2,128)} %add_add_fusion.2.clean_ref, s32[4,2,128]{2,1,0:T(2,128)} %pad_add_fusion.noisy_ref, bf16[1584,384]{1,0:T(8,128)(2,1)} %get-tuple-element.70.q_ref, ...), custom_call_target="tpu_custom_call" | custom-call | flops 1610612736 | bytes 4866048 | tf_op jit(solution)/shard_map/attend_forward/pallas_call | solution.py:184
  169.0 1.9 broadcast_select_fusion.1
  171.3 2.4 pad_maximum_fusion.1.refs_11_
  173.7 1.6 broadcast_select_fusion.3
  175.8 11.1 %pad_maximum_fusion.refs_10_ = bf16[768,3072]{1,0:T(8,128)(2,1)} fusion(bf16[768,1536]{1,0:T(8,128)(2,1)S(1)} %copy-done.10, bf16[384,1536]{1,0:T(8,128)(2,1)S(1)} %get-tuple-element.168, bf16[384,1536]{1,0:T(8,128)(2,1)S(1)} %get-tuple-element.167), kind=kLoop, calls=%fused_computation.10 | loop fusion | flops 14155776 | bytes 9437184 | tf_op jit(solution)/shard_map/concatenate | solution.py:1020
  186.9 1.1 broadcast_select_fusion.7
  188.0 0.9 pad_maximum_fusion.8.refs_4_
  188.8 129.8 %middle.1 = (bf16[1024,768]{1,0:T(8,128)(2,1)}, f32[1024,768]{1,0:T(8,128)}, bf16[1024,384]{1,0:T(8,128)(2,1)}, bf16[1024,384]{1,0:T(8,128)(2,1)}, bf16[384,768]...) custom-call(bf16[1024,768]{1,0:T(8,128)(2,1)} %bitcast.70, ...), custom_call_target="tpu_custom_call" | custom-call | flops 40000000000 | bytes 40000000 | tf_op jit(solution)/shard_map/middle/pallas_call | solution.py:769
  318.7 38.5 %attend_backward.3 = (bf16[3,1584,384]{2,1,0:T(8,128)(2,1)}, bf16[3,768,384]{2,1,0:T(8,128)(2,1)}) custom-call(s32[4,2]{1,0:T(4,128)} %pad_add_fusion.1.span_ref, s32[4,2,256]{2,1,0:T(2,128)} %add_add_fusion.2.clean_ref, s32[4,2,128]{2,1,0:T(2,128)} %pad_add_fusion.noisy_ref, bf16[1584,384]{1,0:T(8,128)(2,1)} %get-tuple-element.70.q_ref, ...), custom_call_target="tpu_custom_call" | custom-call | flops 35999997952 | bytes 36000000 | tf_op jit(solution)/shard_map/attend_backward/pallas_call | solution.py:338
  357.2 38.5 %attend_backward.2 = (bf16[3,1584,384]{2,1,0:T(8,128)(2,1)}, bf16[3,768,384]{2,1,0:T(8,128)(2,1)}) custom-call(s32[4,2]{1,0:T(4,128)} %pad_add_fusion.1.span_ref, s32[4,2,256]{2,1,0:T(2,128)} %add_add_fusion.2.clean_ref, s32[4,2,128]{2,1,0:T(2,128)} %pad_add_fusion.noisy_ref, bf16[1584,384]{1,0:T(8,128)(2,1)} %get-tuple-element.63.q_ref, ...), custom_call_target="tpu_custom_call" | custom-call | flops 35999997952 | bytes 36000000 | tf_op jit(solution)/shard_map/attend_backward/pallas_call | solution.py:338
  395.7 14.9 %rows_back.1 = f32[1584,768]{1,0:T(8,128)} custom-call(bf16[3,1584,384]{2,1,0:T(8,128)(2,1)} %get-tuple-element.87.grads_ref, bf16[3,1584,384]{2,1,0:T(8,128)(2,1)} %get-tuple-element.90.grads2_ref, bf16[3,768,384]{2,1,0:T(8,128)(2,1)} %copy.108.w_ref, bf16[3,768,384]{2,1,0:T(8,128)(2,1)} %copy.109.w2_ref), custom_call_target="tpu_custom_call" | custom-call | flops 5605687296 | bytes 16000000 | tf_op jit(solution)/shard_map/rows_back/pallas_call | solution.py:396
  410.6 1.6 slice.178
  412.2 0.9 fusion.12
  413.1 0.9 pad_maximum_fusion.7
  414.0 29.2 %collective-permute-start.10 = (bf16[528,768]{1,0:T(8,128)(2,1)}, bf16[528,768]{1,0:T(8,128)(2,1)}, u32[]{:S(2)}, u32[]{:S(2)}) collective-permute-start(bf16[528,768]{1,0:T(8,128)(2,1)} %pad_maximum_fusion.7), channel_id=1, source_target_pairs={{0,1},{1,0},{2,3},{3,2},{4,5},{5,4},{6,7},{7,6},{8,9},{9,8},{10,11... | collective-permute-start | bytes 2433032 | tf_op jit(solution)/shard_map/ppermute | solution.py:978
  444.6 2.7 fusion.34
  447.3 2.7 bitcast_convert_fusion.1
  450.0 6.0 %copy.111 = f32[1536,768]{0,1:T(8,128)} copy(f32[1536,768]{1,0:T(8,128)} %bitcast_convert_fusion.1) | data formatting | bytes 9437184 | tf_op jit(solution)/shard_map/convert_element_type | solution.py:1042
  456.1 3.3 pad_maximum_fusion.4.others_ref
  459.5 1.7 pad_maximum_fusion.3.mine_ref
  461.2 2.7 bitcast_convert_fusion
  463.9 1.3 convert_element_type.72
  466.6 2.3 copy-done.1
  468.8 1.2 multiply_reduce_fusion.2
  470.7 2.6 multiply_reduce_fusion
  474.6 76.5 %sum_chunks.1 = (bf16[12,256,384]{2,1,0:T(8,128)(2,1)}, f32[8,768]{1,0:T(8,128)}) custom-call(bf16[12,256,384]{2,1,0:T(8,128)(2,1)} %pad_maximum_fusion.3.mine_ref, bf16[12,256,384]{2,1,0:T(8,128)(2,1)} %pad_maximum_fusion.4.others_ref, f32[8,768]{1,0:T(8,128)} %concatenate.111.small_ref, f32[8,768]{1,0:T(8,128)} %concatenate.112.small2_ref), custom_call_target="tpu_custom_call" | custom-call | flops 40000000000 | bytes 40000000 | tf_op jit(solution)/shard_map/sum_chunks/pallas_call | solution.py:872
  551.1 1.1 slice.163
  552.3 1.8 slice_convert_fusion
  554.7 0.9 slice_bitcast_fusion.1
  555.6 3.7 reshape.594
  559.3 6.3 %copy.110 = f32[768,3,3,128]{0,3,2,1:T(8,128)} copy(f32[768,3,3,128]{3,1,0,2:T(4,128)} %bitcast.73) | data formatting | bytes 7077888 | tf_op jit(solution)/shard_map/convert_element_type | solution.py:1110
  565.6 5.3 copy.112
  571.6 2.1 maximum_convert_fusion
  573.7 4.4 fusion.7
  578.1 1.1 copy.122
  (166 shorter events, 20.4 us)
Async XLA Ops:
  4.4 4.7 copy-start.6
  4.4 4.4 copy-start.38
  4.4 4.4 copy-start
  4.5 4.7 copy-start.39
  5.8 26.8 %collective-permute-start = (bf16[528,768]{1,0:T(8,128)(2,1)}, bf16[528,768]{1,0:T(8,128)(2,1)}, u32[]{:S(2)}, u32[]{:S(2)}) collective-permute-start(bf16[528,768]{1,0:T(8,128)(2,1)} %copy.95), channel_id=1, source_target_pairs={{0,1},{1,0},{2,3},{3,2},{4,5},{5,4},{6,7},{7,6},{8,9},{9,8},{10,11... | collective-permute-start | bytes 2433032 | tf_op jit(solution)/shard_map/ppermute | solution.py:978
  8.8 22.5 %collective-permute-start.9 = (bf16[1536]{0:T(1024)(128)(2,1)S(1)}, bf16[1536]{0:T(1024)(128)(2,1)}, u32[]{:S(2)}, u32[]{:S(2)}) collective-permute-start(bf16[1536]{0:T(1024)(128)(2,1)S(1)} %copy-done.38), channel_id=1, source_target_pairs={{0,1},{1,0},{2,3},{3,2},{4,5},{5,4},{6,7},{7,6},{8,9},{9,8},{10,11... | collective-permute-start | bytes 9224 | tf_op jit(solution)/shard_map/ppermute | solution.py:978
  9.1 4.9 copy-start.9
  14.0 3.4 copy-start.19
  15.1 9.4 %copy-start.12 = (bf16[1,512,768]{2,1,0:T(8,128)(2,1)S(1)}, bf16[1,512,768]{2,1,0:T(8,128)(2,1)}, u32[]{:S(2)}) copy-start(bf16[1,512,768]{2,1,0:T(8,128)(2,1)} %get-tuple-element.171) | copy-start | bytes 2359300
  15.1 10.6 %copy-start.35 = (f32[768]{0:T(1024)S(1)}, f32[768]{0:T(1024)}, u32[]{:S(2)}) copy-start(f32[768]{0:T(1024)} %param.24) | copy-start | bytes 9220
  15.1 11.1 %copy-start.36 = (f32[768]{0:T(1024)S(1)}, f32[768]{0:T(1024)}, u32[]{:S(2)}) copy-start(f32[768]{0:T(1024)} %param.25) | copy-start | bytes 9220
  15.1 11.7 %copy-start.37 = (f32[768]{0:T(1024)S(1)}, f32[768]{0:T(1024)}, u32[]{:S(2)}) copy-start(f32[768]{0:T(1024)} %param.29) | copy-start | bytes 9220
  15.1 12.3 %copy-start.11 = (bf16[768,3,384]{2,0,1:T(8,128)(2,1)S(1)}, bf16[768,3,384]{2,0,1:T(8,128)(2,1)}, u32[]{:S(2)}) copy-start(bf16[768,3,384]{2,0,1:T(8,128)(2,1)} %param.22) | copy-start | bytes 5308420
  30.7 6.1 %copy-start.7 = (bf16[1,512,768]{1,2,0:T(8,128)(2,1)S(1)}, bf16[1,512,768]{1,2,0:T(8,128)(2,1)}, u32[]{:S(2)}) copy-start(bf16[1,512,768]{1,2,0:T(8,128)(2,1)} %copy-done.6) | copy-start | bytes 2359300
  40.7 1.2 copy-start.16
  40.7 6.0 %copy-start.20 = (f32[768]{0:T(1024)S(1)}, f32[768]{0:T(1024)}, u32[]{:S(2)}) copy-start(f32[768]{0:T(1024)} %param.20) | copy-start | bytes 9220
  40.7 5.9 %copy-start.30 = (f32[768]{0:T(1024)S(1)}, f32[768]{0:T(1024)}, u32[]{:S(2)}) copy-start(f32[768]{0:T(1024)} %param.21) | copy-start | bytes 9220
  41.9 22.7 %collective-permute-start.1 = (bf16[1152,384]{1,0:T(8,128)(2,1)S(1)}, bf16[1152,384]{1,0:T(8,128)(2,1)}, u32[]{:S(2)}, u32[]{:S(2)}) collective-permute-start(bf16[1152,384]{1,0:T(8,128)(2,1)S(1)} %copy-done.16), channel_id=1, source_target_pairs={{0,1},{1,0},{2,3},{3,2},{4,5},{5,4},{6,7},{7,6},{8,9},{9,8},{10,11... | collective-permute-start | bytes 2654216 | tf_op jit(solution)/shard_map/ppermute | solution.py:978
  44.6 75.4 %collective-permute-start.5 = (bf16[384,1536]{1,0:T(8,128)(2,1)}, bf16[384,1536]{1,0:T(8,128)(2,1)}, u32[]{:S(2)}, u32[]{:S(2)}) collective-permute-start(bf16[384,1536]{1,0:T(8,128)(2,1)} %constant_dynamic-slice_fusion.1), channel_id=1, source_target_pairs={{0,1},{1,0},{2,3},{3,2},{4,5},{5,4},{6,7},{7,6},{8,9},{9,8},{10,11... | collective-permute-start | bytes 3538952 | tf_op jit(solution)/shard_map/ppermute | solution.py:978
  44.7 75.8 %collective-permute-start.7 = (bf16[768,768]{1,0:T(8,128)(2,1)}, bf16[768,768]{1,0:T(8,128)(2,1)}, u32[]{:S(2)}, u32[]{:S(2)}) collective-permute-start(bf16[768,768]{1,0:T(8,128)(2,1)} %constant_dynamic-slice_fusion), channel_id=1, source_target_pairs={{0,1},{1,0},{2,3},{3,2},{4,5},{5,4},{6,7},{7,6},{8,9},{9,8},{10,11... | collective-permute-start | bytes 3538952 | tf_op jit(solution)/shard_map/ppermute | solution.py:978
  53.5 66.5 %collective-permute-start.3 = (bf16[192,768]{1,0:T(8,128)(2,1)}, bf16[192,768]{1,0:T(8,128)(2,1)}, u32[]{:S(2)}, u32[]{:S(2)}) collective-permute-start(bf16[192,768]{1,0:T(8,128)(2,1)} %constant_dynamic-slice_fusion.2), channel_id=1, source_target_pairs={{0,1},{1,0},{2,3},{3,2},{4,5},{5,4},{6,7},{7,6},{8,9},{9,8},{10,11... | collective-permute-start | bytes 884744 | tf_op jit(solution)/shard_map/ppermute | solution.py:978
  64.5 56.0 %collective-permute-start.2 = (bf16[1152,384]{1,0:T(8,128)(2,1)}, bf16[1152,384]{1,0:T(8,128)(2,1)}, u32[]{:S(2)}, u32[]{:S(2)}) collective-permute-start(bf16[1152,384]{1,0:T(8,128)(2,1)} %collective-permute-done.1), channel_id=1, source_target_pairs={{0,2},{2,0},{4,6},{6,4},{8,10},{10,8},{12,14},{14,12},{16,18},{18,... | collective-permute-start | bytes 2654216 | tf_op jit(solution)/shard_map/ppermute | solution.py:981
  120.0 49.0 %collective-permute-start.4 = (bf16[192,768]{1,0:T(8,128)(2,1)}, bf16[192,768]{1,0:T(8,128)(2,1)}, u32[]{:S(2)}, u32[]{:S(2)}) collective-permute-start(bf16[192,768]{1,0:T(8,128)(2,1)} %collective-permute-done.3), channel_id=1, source_target_pairs={{0,2},{2,0},{4,6},{6,4},{8,10},{10,8},{12,14},{14,12},{16,18},{18,... | collective-permute-start | bytes 884744 | tf_op jit(solution)/shard_map/ppermute | solution.py:981
  120.0 49.0 %collective-permute-start.6 = (bf16[384,1536]{1,0:T(8,128)(2,1)}, bf16[384,1536]{1,0:T(8,128)(2,1)S(1)}, u32[]{:S(2)}, u32[]{:S(2)}) collective-permute-start(bf16[384,1536]{1,0:T(8,128)(2,1)} %collective-permute-done.5), channel_id=1, source_target_pairs={{0,2},{2,0},{4,6},{6,4},{8,10},{10,8},{12,14},{14,12},{16,18},{18,... | collective-permute-start | bytes 3538952 | tf_op jit(solution)/shard_map/ppermute | solution.py:981
  120.5 48.5 %collective-permute-start.8 = (bf16[768,768]{1,0:T(8,128)(2,1)}, bf16[768,768]{1,0:T(8,128)(2,1)}, u32[]{:S(2)}, u32[]{:S(2)}) collective-permute-start(bf16[768,768]{1,0:T(8,128)(2,1)} %collective-permute-done.7), channel_id=1, source_target_pairs={{0,2},{2,0},{4,6},{6,4},{8,10},{10,8},{12,14},{14,12},{16,18},{18,... | collective-permute-start | bytes 3538952 | tf_op jit(solution)/shard_map/ppermute | solution.py:981
  168.9 2.4 copy-start.8
  173.7 2.0 copy-start.10
  410.6 32.6 %copy-start.33 = (f32[12,1,256]{2,1,0:T(1,128)S(1)}, f32[12,1,256]{2,1,0:T(1,128)}, u32[]{:S(2)}) copy-start(f32[12,1,256]{2,1,0:T(1,128)} %get-tuple-element.95) | copy-start | bytes 36868
  410.6 33.3 %copy-start.34 = (f32[8,768]{1,0:T(8,128)S(1)}, f32[8,768]{1,0:T(8,128)}, u32[]{:S(2)}) copy-start(f32[8,768]{1,0:T(8,128)} %get-tuple-element.96) | copy-start | bytes 73732
  410.6 33.9 %copy-start.18 = (bf16[384,768]{1,0:T(8,128)(2,1)S(1)}, bf16[384,768]{1,0:T(8,128)(2,1)}, u32[]{:S(2)}) copy-start(bf16[384,768]{1,0:T(8,128)(2,1)} %get-tuple-element.94) | copy-start | bytes 1769476
  410.6 33.9 %copy-start.17 = (bf16[384,768]{1,0:T(8,128)(2,1)S(1)}, bf16[384,768]{1,0:T(8,128)(2,1)}, u32[]{:S(2)}) copy-start(bf16[384,768]{1,0:T(8,128)(2,1)} %get-tuple-element.92) | copy-start | bytes 1769476
  414.0 49.8 %collective-permute-start.10 = (bf16[528,768]{1,0:T(8,128)(2,1)}, bf16[528,768]{1,0:T(8,128)(2,1)}, u32[]{:S(2)}, u32[]{:S(2)}) collective-permute-start(bf16[528,768]{1,0:T(8,128)(2,1)} %pad_maximum_fusion.7), channel_id=1, source_target_pairs={{0,1},{1,0},{2,3},{3,2},{4,5},{5,4},{6,7},{7,6},{8,9},{9,8},{10,11... | collective-permute-start | bytes 2433032 | tf_op jit(solution)/shard_map/ppermute | solution.py:978
  456.1 3.4 copy-start.13
  459.5 6.4 %slice-start = ((s8[4866048]{0:T(1024)(128)(4,1)}), s8[4194304]{0:T(1024)(128)(4,1)S(1)}, s32[]{:S(2)}) async-start(s8[4866048]{0:T(1024)(128)(4,1)} %bitcast.86), calls=%async_computation | async-start | bytes 8388608
  461.1 4.7 slice-start.1
  466.3 4.4 copy-start.3
  466.3 4.4 copy-start.5
  466.3 2.5 copy-start.1
  466.3 2.5 copy-start.21
  466.3 2.5 copy-start.23
  470.0 3.3 copy-start.24
  470.6 2.7 copy-start.26
  470.6 3.3 copy-start.27
  552.3 1.8 copy-start.28
  565.6 5.9 %copy-start.32 = (f32[1,4,2,128]{3,2,1,0:T(2,128)S(1)}, f32[1,4,2,128]{3,2,1,0:T(2,128)}, u32[]{:S(2)}) copy-start(f32[1,4,2,128]{3,2,1,0:T(2,128)} %get-tuple-element.195) | copy-start | bytes 12292
  565.6 5.9 %copy-start.25 = (f32[2,512]{1,0:T(2,128)S(1)}, f32[2,512]{1,0:T(2,128)}, u32[]{:S(2)}) copy-start(f32[2,512]{1,0:T(2,128)} %copy-done.24) | copy-start | bytes 12292
  565.6 6.0 %copy-start.31 = (f32[2,512]{1,0:T(2,128)S(1)}, f32[2,512]{1,0:T(2,128)}, u32[]{:S(2)}) copy-start(f32[2,512]{1,0:T(2,128)} %get-tuple-element.137) | copy-start | bytes 12292
  565.6 6.0 %copy-start.15 = (bf16[384,384]{1,0:T(8,128)(2,1)S(1)}, bf16[384,384]{1,0:T(8,128)(2,1)}, u32[]{:S(2)}) copy-start(bf16[384,384]{1,0:T(8,128)(2,1)} %get-tuple-element.177) | copy-start | bytes 884740
  565.6 8.0 %copy-start.4 = (f32[512,768]{1,0:T(8,128)S(1)}, f32[512,768]{1,0:T(8,128)}, u32[]{:S(2)}) copy-start(f32[512,768]{1,0:T(8,128)} %copy-done.3) | copy-start | bytes 4718596
  565.6 8.0 %copy-start.22 = (f32[768]{0:T(1024)S(1)}, f32[768]{0:T(1024)}, u32[]{:S(2)}) copy-start(f32[768]{0:T(1024)} %param.20) | copy-start | bytes 9220
  565.6 8.0 %copy-start.29 = (f32[1,4,2,128]{3,1,2,0:T(4,128)S(1)}, f32[1,4,2,128]{3,1,2,0:T(4,128)}, u32[]{:S(2)}) copy-start(f32[1,4,2,128]{3,1,2,0:T(4,128)} %copy.116) | copy-start | bytes 12292
  570.9 2.8 copy-start.2
  573.7 4.4 copy-start.14

commit v4 on v3

--- a/solution.py
+++ b/solution.py
@@ -21,6 +21,8 @@
 WINDOW = TILE + 2 * EDGE
 KEY_TILE = 256
 LANES = 128
+HIDDEN_TILE = 256
+ROW_TILE = 256
 
 epsilon = 1e-05
 neg_large = -1e30
@@ -34,13 +36,6 @@
 
 def dot(left, right, dims=NN):
     return lax.dot_general(left, right, dims, preferred_element_type=f32)
-
-
-def layer_norm(values, norm_gain, norm_bias):
-    average = jnp.mean(values, axis=-1, keepdims=True)
-    centred = values - average
-    variance = jnp.mean(centred * centred, axis=-1, keepdims=True)
-    return centred * lax.rsqrt(variance + epsilon) * norm_gain + norm_bias
 
 
 def low_lanes(shape):
@@ -58,28 +53,31 @@
     return values * cosine + swapped * sine
 
 
-def project_kernel(rows_ref, w_ref, cos_ref, sin_ref, q_ref, k_ref, v_ref):
-    rows = rows_ref[...]
-    cosine, sine = cos_ref[...], sin_ref[...]
+def project_rows(rows, w_ref, cosine, sine, q_ref, k_ref, v_ref, at):
     for part, out_ref in ((0, q_ref), (1, k_ref)):
         field = dot(rows, w_ref[part])
         for pair in range(field.shape[1] // LANES):
             cols = slice(pair * LANES, (pair + 1) * LANES)
-            out_ref[:, cols] = turn(field[:, cols], cosine, sine).astype(bf16)
-    v_ref[...] = dot(rows, w_ref[2]).astype(bf16)
+            out_ref[at, cols] = turn(field[:, cols], cosine, sine).astype(bf16)
+    v_ref[at, :] = dot(rows, w_ref[2]).astype(bf16)
+
+
+def project_kernel(rows_ref, w_ref, cos_ref, sin_ref, q_ref, k_ref, v_ref):
+    at = slice(0, rows_ref.shape[0])
+    project_rows(rows_ref[...], w_ref, cos_ref[...], sin_ref[...], q_ref, k_ref, v_ref, at)
 
 
 def project(rows, weights, cosine, sine):
     count, width = rows.shape
     cols = weights.shape[2]
-    step = count // 9
+    step = count // 3
     row_spec = pl.BlockSpec((step, width), lambda i: (i, 0))
     table_spec = pl.BlockSpec((step, LANES), lambda i: (i, 0))
     out_spec = pl.BlockSpec((step, cols), lambda i: (i, 0))
     shape = jax.ShapeDtypeStruct((count, cols), bf16)
     return pl.pallas_call(
         project_kernel,
-        grid=(9,),
+        grid=(3,),
         in_specs=[
             row_spec,
             pl.BlockSpec(weights.shape, lambda i: (0, 0, 0)),
@@ -95,6 +93,77 @@
             transcendentals=0,
         ),
     )(rows, weights, cosine, sine)
+
+
+def normal(values):
+    average = jnp.mean(values, axis=-1, keepdims=True)
+    centred = values - average
+    variance = jnp.mean(centred * centred, axis=-1, keepdims=True)
+    scale = lax.rsqrt(variance + epsilon)
+    return centred * scale, scale
+
+
+def enter_kernel(
+    tokens_ref,
+    context_ref,
+    gain_ref,
+    shift_ref,
+    w_ref,
+    cos_ref,
+    sin_ref,
+    rows_ref,
+    rows_t_ref,
+    q_ref,
+    k_ref,
+    v_ref,
+):
+    def norm(values):
+        return (normal(values.astype(f32))[0] * gain_ref[...] + shift_ref[...]).astype(bf16)
+
+    def blocks(i, _):
+        source = pl.ds(pl.multiple_of(i * TILE, TILE), TILE)
+        rows_ref[source, :] = norm(context_ref[source, :])
+        at = pl.ds(pl.multiple_of(CLEAN_OWN + i * TILE, TILE), TILE)
+        rows_ref[at, :] = norm(tokens_ref[1, source, :])
+        at = pl.ds(pl.multiple_of(NOISY_OWN + i * TILE, EDGE), TILE)
+        rows_ref[at, :] = norm(tokens_ref[0, source, :])
+        return 0
+
+    lax.fori_loop(0, TILES, blocks, 0)
+    rows_ref[2 * HALF : NOISY_BASE, :] = rows_ref[:EDGE, :]
+    edge = norm(context_ref[HALF:, :])
+    rows_ref[NOISY_BASE:NOISY_OWN, :] = edge
+    rows_ref[NOISY_OWN + HALF :, :] = edge
+    step = KEY_ROWS // 3
+
+    def fields(i, _):
+        at = pl.ds(pl.multiple_of(i * step, EDGE), step)
+        project_rows(
+            rows_ref[at, :], w_ref, cos_ref[at, :], sin_ref[at, :], q_ref, k_ref, v_ref, at
+        )
+        return 0
+
+    lax.fori_loop(0, 3, fields, 0)
+    for c in range(rows_t_ref.shape[0] // LANES):
+        cols = slice(c * LANES, (c + 1) * LANES)
+        rows_t_ref[cols, :] = rows_ref[:, cols].T
+
+
+def enter(tokens, context, gain, shift, weights, cosine, sine):
+    width, cols = weights.shape[1:]
+    vmem = pl.BlockSpec(memory_space=pltpu.VMEM)
+    shape = jax.ShapeDtypeStruct
+    field = shape((KEY_ROWS, cols), bf16)
+    return pl.pallas_call(
+        enter_kernel,
+        in_specs=[vmem] * 7,
+        out_specs=[vmem] * 5,
+        out_shape=[shape((KEY_ROWS, width), bf16), shape((width, KEY_ROWS), bf16)] + [field] * 3,
+        name="enter",
+        cost_estimate=pl.CostEstimate(
+            flops=10**10, bytes_accessed=16 * 10**6, transcendentals=0
+        ),
+    )(tokens, context, gain, shift, weights, cosine, sine)
 
 
 def split_heads(rows):
@@ -220,10 +289,11 @@
     grad_ref,
     dk_ref,
     dv_ref,
+    fields_ref,
 ):
     dk_ref[...] = jnp.zeros_like(dk_ref)
     dv_ref[...] = jnp.zeros_like(dv_ref)
-    out_ref[0, :, :LANES] = jnp.zeros((KEY_ROWS, LANES), bf16)
+    fields_ref[:, :LANES] = jnp.zeros((KEY_ROWS, LANES), bf16)
 
     def one_tile(t, _):
         clean_at = pl.multiple_of(CLEAN_OWN + t * TILE, TILE)
@@ -290,7 +360,7 @@
         d_query = jnp.concatenate(d_query, axis=0).T
         for at, part in ((noisy_at, d_query[:TILE]), (clean_at, d_query[TILE:])):
             turned = turn(part, cos_ref[pl.ds(at, TILE), :], -sin_ref[pl.ds(at, TILE), :])
-            out_ref[0, pl.ds(at, TILE), :LANES] = turned.astype(bf16)
+            fields_ref[pl.ds(at, TILE), :LANES] = turned.astype(bf16)
         return 0
 
     lax.fori_loop(0, TILES, one_tile, 0)
@@ -298,20 +368,24 @@
 
     def finish(i, _):
         rows = pl.ds(pl.multiple_of(i * step, EDGE), step)
-        out_ref[0, rows, LANES : 2 * LANES] = turn(
+        fields_ref[rows, LANES : 2 * LANES] = turn(
             dk_ref[rows, :], cos_ref[rows, :], -sin_ref[rows, :]
         ).astype(bf16)
-        out_ref[0, rows, 2 * LANES :] = dv_ref[rows, :].astype(bf16)
+        fields_ref[rows, 2 * LANES :] = dv_ref[rows, :].astype(bf16)
+        for c in range(3):
+            out_ref[c, rows, :] = fields_ref[rows, c * LANES : (c + 1) * LANES]
         return 0
 
     lax.fori_loop(0, 9, finish, 0)
 
     def weight_rows(i, _):
-        rows = pl.ds(pl.multiple_of(i * LANES, LANES), LANES)
-        grad_ref[0, rows, :] = dot(rows_ref[rows, :], out_ref[0]).astype(bf16)
+        rows = pl.ds(pl.multiple_of(i * ROW_TILE, LANES), ROW_TILE)
+        grad = dot(rows_ref[rows, :], fields_ref[...]).astype(bf16)
+        for c in range(3):
+            grad_ref[c, rows, :] = grad[:, c * LANES : (c + 1) * LANES]
         return 0
 
-    lax.fori_loop(0, rows_ref.shape[0] // LANES, weight_rows, 0)
+    lax.fori_loop(0, rows_ref.shape[0] // ROW_TILE, weight_rows, 0)
 
 
 def attend_backward(
@@ -350,14 +424,15 @@
                 whole2(rows_t),
             ],
             out_specs=[
-                pl.BlockSpec((1, count, 3 * LANES), lambda p, s: (p, 0, 0)),
-                pl.BlockSpec((1, width, 3 * LANES), lambda p, s: (p, 0, 0)),
+                pl.BlockSpec((3, count, LANES), lambda p, s: (0, 0, p)),
+                pl.BlockSpec((3, width, LANES), lambda p, s: (0, 0, p)),
             ],
-            scratch_shapes=[pltpu.VMEM((count, LANES), f32)] * 2,
+            scratch_shapes=[pltpu.VMEM((count, LANES), f32)] * 2
+            + [pltpu.VMEM((count, 3 * LANES), bf16)],
         ),
         out_shape=[
-            jax.ShapeDtypeStruct((pairs, count, 3 * LANES), bf16),
-            jax.ShapeDtypeStruct((pairs, width, 3 * LANES), bf16),
+            jax.ShapeDtypeStruct((3, count, cols), bf16),
+            jax.ShapeDtypeStruct((3, width, cols), bf16),
         ],
         name="attend_backward",
         cost_estimate=pl.CostEstimate(
@@ -377,35 +452,6 @@
         sine,
         rows_t,
     )
-
-
-def rows_back_kernel(grads_ref, grads2_ref, w_ref, w2_ref, out_ref):
-    total = 0.0
-    for grads, weights in ((grads_ref, w_ref), (grads2_ref, w2_ref)):
-        for pair in range(grads.shape[0]):
-            total = total + dot(grads[pair], weights[pair], NT)
-    out_ref[...] = total
-
-
-def rows_back(grads, grads2, weights, weights2):
-    pairs, count, cols = grads.shape
-    step = count // 9
-    width = weights.shape[1]
-    grad_spec = pl.BlockSpec((pairs, step, cols), lambda i: (0, i, 0))
-    w_spec = pl.BlockSpec(weights.shape, lambda i: (0, 0, 0))
-    return pl.pallas_call(
-        rows_back_kernel,
-        grid=(9,),
-        in_specs=[grad_spec, grad_spec, w_spec, w_spec],
-        out_specs=pl.BlockSpec((step, width), lambda i: (i, 0)),
-        out_shape=jax.ShapeDtypeStruct((count, width), f32),
-        name="rows_back",
-        cost_estimate=pl.CostEstimate(
-            flops=4 * pairs * count * cols * width,
-            bytes_accessed=16 * 10**6,
-            transcendentals=0,
-        ),
-    )(grads, grads2, weights, weights2)
 
 
 PIECES = 16
@@ -525,15 +571,18 @@
         self.b_out[k] = (mine + self.a_in[k, 0].astype(f32)).astype(bf16)
         self.copy_b(k).start()
 
-    def stage_c(self, k, grads):
+    def stage_c(self, k, grads, crossed=True):
         self.copy_a(k, 1, grads).wait()
-        self.copy_b(k).wait()
+        if crossed:
+            self.copy_b(k).wait()
 
         def total(which):
             inner = which * self.quarter
             rows = self.rows_at(inner, self.quarter)
             mine = grads[k, self.rows_at(self.core * self.half + inner, self.quarter), :]
-            got = self.a_in[k, 1, rows, :].astype(f32) + self.b_in[k, rows, :].astype(f32)
+            got = self.a_in[k, 1, rows, :].astype(f32)
+            if crossed:
+                got = got + self.b_in[k, rows, :].astype(f32)
             return mine.astype(f32) + got
 
         self.c_out[k] = total(1 - self.x).astype(bf16)
@@ -594,16 +643,7 @@
         action(step)
 
 
-HIDDEN_TILE = 256
-ROW_TILE = 256
-
-
-def normal(values):
-    average = jnp.mean(values, axis=-1, keepdims=True)
-    centred = values - average
-    variance = jnp.mean(centred * centred, axis=-1, keepdims=True)
-    scale = lax.rsqrt(variance + epsilon)
-    return centred * scale, scale
+SPLIT = 4
 
 
 def middle_kernel(exchange, tiles, *refs):
@@ -618,8 +658,12 @@
         shift_ref,
         bdown_ref,
         bup_ref,
-        up_hbm,
-        down_hbm,
+        up_mine,
+        up_here,
+        up_there,
+        down_mine,
+        down_here,
+        down_there,
         out_ref,
         mid_ref,
         datt_ref,
@@ -628,6 +672,8 @@
         gout2_ref,
         gbup_ref,
         small_ref,
+        gdown_ref,
+        gup_ref,
         full_ref,
         up_buf,
         down_buf,
@@ -642,21 +688,56 @@
     ) = refs
     place, part = lax.axis_index("dp"), lax.axis_index("mp")
     ex = exchange.bind(place, part, rest)
-    count = ex.count
+    core = ex.core
+    count = tiles // 2
     rows_all = x_ref.shape[0]
     blocks = rows_all // ROW_TILE
     width = x_ref.shape[1]
-
-    def loads(i):
+    lanes = width // 2
+
+    def which(i):
+        other = jnp.logical_or(i == 0, jnp.logical_and(i % 2 == 1, i < tiles - 1))
+        mine = jnp.where(i == tiles - 1, count - 1, i // 2 - 1)
+        return other, jnp.where(other, (i + 1) // 2, mine)
+
+    def load(i, up_source, down_source, h):
         slot = i % 2
-        cols = pl.ds(pl.multiple_of(i * HIDDEN_TILE, HIDDEN_TILE), HIDDEN_TILE)
-        return (
-            pltpu.make_async_copy(up_hbm.at[:, cols], up_buf.at[slot], load_sem.at[slot, 0]),
-            pltpu.make_async_copy(down_hbm.at[cols, :], down_buf.at[slot], load_sem.at[slot, 1]),
-        )
-
-    for load in loads(0):
-        load.start()
+        sems = load_sem.at[slot]
+        if h is None:
+            return pltpu.make_async_copy(down_source, down_buf.at[slot], sems.at[2])
+        target = up_buf.at[slot, h * lanes : (h + 1) * lanes]
+        return pltpu.make_async_copy(up_source, target, sems.at[h])
+
+    def start_loads(i):
+        other, k = which(i)
+        cols = pl.ds(pl.multiple_of(k * HIDDEN_TILE, HIDDEN_TILE), HIDDEN_TILE)
+        inner = k % (count // 2)
+        rows = pl.ds(pl.multiple_of(inner * HIDDEN_TILE, HIDDEN_TILE), HIDDEN_TILE)
+
+        def put(condition, source, h):
+            @pl.when(condition)
+            def _():
+                if h is None:
+                    load(i, None, source, None).start()
+                else:
+                    load(i, source, None, h).start()
+
+        mine = jnp.logical_not(other)
+        for h in range(2):
+            put(mine, up_mine.at[h * lanes : (h + 1) * lanes, cols], h)
+            put(jnp.logical_and(other, core == h), up_here.at[:, cols], h)
+            put(jnp.logical_and(other, core != h), up_there.at[:, cols], h)
+        held = k // (count // 2) == core
+        put(mine, down_mine.at[cols, :], None)
+        put(jnp.logical_and(other, held), down_here.at[rows, :], None)
+        put(jnp.logical_and(other, jnp.logical_not(held)), down_there.at[rows, :], None)
+
+    def wait_loads(i):
+        for h in range(2):
+            load(i, up_mine.at[:lanes, :HIDDEN_TILE], None, h).wait()
+        load(i, None, down_mine.at[:HIDDEN_TILE, :], None).wait()
+
+    start_loads(0)
     ex.greet()
 
     def prologue(r, _):
@@ -672,20 +753,20 @@
     lax.fori_loop(0, blocks, prologue, 0)
 
     def tile(i):
+        other, k = which(i)
         slot = i % 2
-        for load in loads(i):
-            load.wait()
+        wait_loads(i)
 
         @pl.when(i + 1 < tiles)
         def _():
-            for load in loads(i + 1):
-                load.start()
+            start_loads(i + 1)
 
         up, down = up_buf.at[slot], down_buf.at[slot]
+        bias_at = jnp.where(other, k, count + k)
         bias_grad = jnp.zeros((1, HIDDEN_TILE), f32)
         for r in range(blocks):
             rows = slice(r * ROW_TILE, (r + 1) * ROW_TILE)
-            pre = dot(n2_ref[rows, :], up[...]) + bup_ref[i]
+            pre = dot(n2_ref[rows, :], up[...]) + bup_ref[bias_at]
             square = pre * pre
             bend = jnp.tanh(0.7978845608028654 * (pre + 0.044715 * square * pre))
             part_one = 0.5 * (1.0 + bend)
@@ -700,25 +781,59 @@
             bias_grad = bias_grad + jnp.sum(d_pre.astype(f32), axis=0, keepdims=True)
             total_ref[rows, :] += dot(act, down[...])
             dn2_ref[rows, :] += dot(d_pre, up[...], NT)
-        gbup_ref[i] = bias_grad
-        k = i % count
-        grad_ref[k, :, :width] = dot(act_ref[...].T, dy_ref[...]).astype(bf16)
-        grad_ref[k, :, width:] = dot(dpre_ref[...].T, n2_ref[...]).astype(bf16)
-
-    def steps(i, lanes):
-        at_step(i - count - 7, count, lambda k: ex.stage_h(k, full_ref))
-        at_step(i - count - 6, count, lambda k: ex.stage_g(k, full_ref))
-        at_step(i - count - 5, count, lambda k: ex.stage_f(k, full_ref))
-        at_step(i - count - 4, count, lambda k: ex.stage_e(k, full_ref))
-        at_step(i - count - 3, count, lambda k: ex.stage_d(k))
-        at_step(i - count - 2, count, lambda k: ex.stage_c(k, grad_ref))
-        at_step(i - 1, count, lambda k: ex.stage_b(k, grad_ref))
+        gbup_ref[bias_at] = bias_grad
+        grads = (
+            dot(act_ref[...].T, dy_ref[...]).astype(bf16),
+            dot(dpre_ref[...].T, n2_ref[...]).astype(bf16),
+        )
+        for c in range(SPLIT):
+            cols = slice(c % 2 * lanes, (c % 2 + 1) * lanes)
+            grad_ref[k * SPLIT + c] = grads[c // 2][:, cols]
+
+        @pl.when(other)
+        def _():
+            for c in range(SPLIT):
+                ex.start_a(k * SPLIT + c, 0, grad_ref)
+
+        @pl.when(jnp.logical_not(other))
+        def _():
+            for c in range(SPLIT):
+                ex.start_a(k * SPLIT + c, 1, grad_ref)
+
+    def group(k, when, action):
+        @pl.when(jnp.logical_and(when, jnp.logical_and(k >= 0, k < count)))
+        def _():
+            lax.fori_loop(0, SPLIT, lambda c, _: (action(k * SPLIT + c), 0)[1], 0)
+
+    def arrive(k):
+        for c in range(SPLIT):
+            ex.stage_h(k * SPLIT + c, full_ref)
+        hidden = pl.ds(pl.multiple_of(k * HIDDEN_TILE, HIDDEN_TILE), HIDDEN_TILE)
+        for c in range(2):
+            cols = slice(c * lanes, (c + 1) * lanes)
+            gdown_ref[hidden, cols] = full_ref[k * SPLIT + c]
+            gup_ref[cols, hidden] = full_ref[k * SPLIT + 2 + c].T
+
+    def steps(i):
+        even = i % 2 == 0
+        odd = jnp.logical_not(even)
+        last = (i - 9) // 2
+
+        @pl.when(jnp.logical_and(odd, jnp.logical_and(last >= 0, last < count)))
+        def _():
+            arrive(last)
+
+        group((i - 8) // 2, even, lambda k: ex.stage_g(k, full_ref))
+        group((i - 7) // 2, odd, lambda k: ex.stage_f(k, full_ref))
+        group((i - 6) // 2, even, lambda k: ex.stage_e(k, full_ref))
+        group((i - 5) // 2, odd, lambda k: ex.stage_d(k))
+        group((i - 4) // 2, even, lambda k: ex.stage_c(k, grad_ref))
+        crossing = jnp.logical_or(i == 1, jnp.logical_and(even, i >= 2))
+        group(i // 2, crossing, lambda k: ex.stage_b(k, grad_ref))
 
     def main(i, _):
         tile(i)
-        at_step(i, count, lambda k: ex.start_a(k, 0, grad_ref))
-        at_step(i - count, count, lambda k: ex.start_a(k, 1, grad_ref))
-        steps(i, None)
+        steps(i)
         return 0
 
     lax.fori_loop(0, tiles, main, 0)
@@ -741,56 +856,64 @@
         datt_ref[rows, :] = dot(d_branch, wout_ref[...], NT).astype(bf16)
         datt2_ref[rows, :] = dot(d_branch, wout2_ref[...], NT).astype(bf16)
         add = lambda values: jnp.sum(values, axis=0, keepdims=True)
-        return (sums[0] + add(d_rows * unit), sums[1] + add(d_rows), sums[2] + add(dy))
+        sums = (sums[0] + add(d_rows * unit), sums[1] + add(d_rows), sums[2] + add(dy))
+        steps(tiles + r)
+        return sums
 
     zero = jnp.zeros((1, width), f32)
     sums = lax.fori_loop(0, blocks, epilogue, (zero, zero, zero))
     for j in range(3):
         small_ref[j : j + 1, :] = sums[j]
-    gout_ref[...] = dot(att_ref[...].T, n2_ref[...]).astype(bf16)
-    gout2_ref[...] = dot(att2_ref[...].T, n2_ref[...]).astype(bf16)
+    depth = wout_ref.shape[0]
+    for source, target in ((att_ref, gout_ref), (att2_ref, gout2_ref)):
+        grad = dot(source[...].T, n2_ref[...]).astype(bf16)
+        target[:depth, :] = grad[:, :lanes]
+        target[depth:, :] = grad[:, lanes:]
 
     def drain(i, _):
-        steps(i, None)
+        steps(i)
         return 0
 
-    lax.fori_loop(tiles, tiles + count + 2, drain, 0)
-
-
-def middle(bits, x, att, att2, wout, wout2, dy, gain, shift, bdown, bup, up, down):
+    lax.fori_loop(tiles + blocks, 2 * count + 8, drain, 0)
+
+
+def middle(bits, x, att, att2, wout, wout2, dy, gain, shift, bdown, bup, ups, downs):
     rows, width = x.shape
-    hidden = up.shape[1]
-    tiles = hidden // HIDDEN_TILE
-    count = tiles // 2
-    exchange = Exchange(bits, count, HIDDEN_TILE, 2 * width)
+    hidden = ups[0].shape[1]
+    count = hidden // HIDDEN_TILE
+    tiles = 2 * count
+    exchange = Exchange(bits, count * SPLIT, HIDDEN_TILE, width // 2)
     vmem = pl.BlockSpec(memory_space=pltpu.VMEM)
     hbm = pl.BlockSpec(memory_space=pl.ANY)
     shape = jax.ShapeDtypeStruct
+    depth = wout.shape[0]
     return pl.pallas_call(
         functools.partial(middle_kernel, exchange, tiles),
-        in_specs=[vmem] * 10 + [hbm] * 2,
-        out_specs=[vmem] * 9,
+        in_specs=[vmem] * 10 + [hbm] * 6,
+        out_specs=[vmem] * 10,
         out_shape=[
             shape((rows, width), bf16),
             shape((rows, width), f32),
             shape(att.shape, bf16),
             shape(att2.shape, bf16),
-            shape(wout.shape, bf16),
-            shape(wout2.shape, bf16),
+            shape((2 * depth, width // 2), bf16),
+            shape((2 * depth, width // 2), bf16),
             shape((tiles, 1, HIDDEN_TILE), f32),
             shape((8, width), f32),
-            shape((count, HIDDEN_TILE, 2 * width), bf16),
+            shape((hidden, width), bf16),
+            shape((width, hidden), bf16),
         ],
         scratch_shapes=[
+            pltpu.VMEM((count * SPLIT, HIDDEN_TILE, width // 2), bf16),
             pltpu.VMEM((2, width, HIDDEN_TILE), bf16),
             pltpu.VMEM((2, HIDDEN_TILE, width), bf16),
-            pltpu.SemaphoreType.DMA((2, 2)),
+            pltpu.SemaphoreType.DMA((2, 3)),
             pltpu.VMEM((rows, width), bf16),
             pltpu.VMEM((rows, width), f32),
             pltpu.VMEM((rows, width), f32),
             pltpu.VMEM((rows, HIDDEN_TILE), bf16),
             pltpu.VMEM((rows, HIDDEN_TILE), bf16),
-            pltpu.VMEM((count, HIDDEN_TILE, 2 * width), bf16),
+            pltpu.VMEM((count * SPLIT, HIDDEN_TILE, width // 2), bf16),
         ]
         + exchange.scratch(),
         compiler_params=pltpu.CompilerParams(
@@ -798,24 +921,140 @@
         ),
         name="middle",
         cost_estimate=pl.CostEstimate(
-            flops=40 * 10**9, bytes_accessed=40 * 10**6, transcendentals=4 * 10**6
+            flops=60 * 10**9, bytes_accessed=40 * 10**6, transcendentals=4 * 10**6
         ),
-    )(x, att, att2, wout, wout2, dy, gain, shift, bdown, bup, up, down)
-
-
-def sum_kernel(
-    exchange, mine_ref, others_ref, small_ref, small2_ref, full_ref, sums_ref, got_ref, work_ref, small_send, small_recv, *rest
-):
+    )(x, att, att2, wout, wout2, dy, gain, shift, bdown, bup, *ups, *downs)
+
+
+def leave_kernel(exchange, *refs):
+    (
+        mine_ref,
+        mine_out_ref,
+        crossed_ref,
+        crossed_out_ref,
+        d_ref,
+        d2_ref,
+        w_ref,
+        w2_ref,
+        tokens_ref,
+        gain_ref,
+        dmid_ref,
+        small_ref,
+        small2_ref,
+        full_ref,
+        back_ref,
+        sums_ref,
+        sum_buf,
+        rows_ref,
+        give_ref,
+        take_ref,
+        swap_sem,
+        got_ref,
+        work_ref,
+        small_send,
+        small_recv,
+        *rest,
+    ) = refs
     place, part = lax.axis_index("dp"), lax.axis_index("mp")
     ex = exchange.bind(place, part, rest)
     count, bits = ex.count, ex.bits
+    first = mine_ref.shape[0]
     ex.greet()
 
+    def begin(k, _):
+        total = mine_ref[k].astype(f32) + crossed_ref[k].astype(f32)
+        sum_buf[k] = total.astype(bf16)
+        ex.start_a(k, 1, sum_buf)
+        return 0
+
+    lax.fori_loop(0, first, begin, 0)
+
+    def begin_out(k, _):
+        total = mine_out_ref[k].astype(f32) + crossed_out_ref[k].astype(f32)
+        sum_buf[first + k] = total.astype(bf16)
+        ex.start_a(first + k, 1, sum_buf)
+        return 0
+
+    lax.fori_loop(0, count - first, begin_out, 0)
+
+    def back_of(rows):
+        total = 0.0
+        for grads, weights in ((d_ref, w_ref), (d2_ref, w2_ref)):
+            for c in range(3):
+                total = total + dot(grads[c, rows, :], weights[c], NT)
+        return total
+
+    for r in range(HALF // ROW_TILE):
+        rows = slice(r * ROW_TILE, (r + 1) * ROW_TILE)
+        given = back_of(rows)
+        if r == 0:
+            edges = back_of(slice(2 * HALF, NOISY_OWN))
+            give_ref[EDGE:ROW_TILE, :] = given[EDGE:].astype(bf16)
+            give_ref[:EDGE, :] = (given[:EDGE] + edges[:EDGE]).astype(bf16)
+            last = back_of(slice(NOISY_OWN + HALF, KEY_ROWS))
+            give_ref[HALF:, :] = (edges[EDGE:] + last).astype(bf16)
+        else:
+            give_ref[rows, :] = given.astype(bf16)
+    swap = pltpu.make_async_remote_copy(
+        src_ref=give_ref,
+        dst_ref=take_ref,
+        send_sem=swap_sem.at[0],
+        recv_sem=swap_sem.at[1],
+        device_id=ex.across,
+        device_id_type=MESH,
+    )
+    swap.start()
+
+    def steps(i):
+        at_step(i - 15, count, lambda k: ex.stage_h(k, full_ref))
+        at_step(i - 12, count, lambda k: ex.stage_g(k, full_ref))
+        at_step(i - 9, count, lambda k: ex.stage_f(k, full_ref))
+        at_step(i - 6, count, lambda k: ex.stage_e(k, full_ref))
+        at_step(i - 3, count, lambda k: ex.stage_d(k))
+        at_step(i, count, lambda k: ex.stage_c(k, sum_buf, False))
+
+    parts = 2 * TILES
+
+    def own_rows(b, _):
+        noisy = NOISY_OWN + b * TILE
+        clean = CLEAN_OWN + (b - TILES) * TILE
+        start = jnp.where(b < TILES, noisy, clean)
+        rows_ref[pl.ds(pl.multiple_of(b * TILE, TILE), TILE), :] = back_of(
+            pl.ds(pl.multiple_of(start, EDGE), TILE)
+        )
+        steps(2 * b)
+        steps(2 * b + 1)
+        return 0
+
+    lax.fori_loop(0, parts, own_rows, 0)
+    swap.wait()
+    rows_ref[HALF:, :] += take_ref[:HALF, :].astype(f32)
+    edge = pl.ds(pl.multiple_of((1 - part) * (HALF - EDGE), EDGE), EDGE)
+    rows_ref[edge, :] += take_ref[HALF:, :].astype(f32)
+
+    def norm_back(b, sums):
+        rows = pl.ds(pl.multiple_of(b * TILE, TILE), TILE)
+        unit, scale = normal(tokens_ref[rows, :].astype(f32))
+        d_rows = rows_ref[rows, :]
+        lean = d_rows * gain_ref[...]
+        back_ref[rows, :] = dmid_ref[rows, :] + scale * (
+            lean
+            - jnp.mean(lean, axis=-1, keepdims=True)
+            - unit * jnp.mean(lean * unit, axis=-1, keepdims=True)
+        )
+        add = lambda values: jnp.sum(values, axis=0, keepdims=True)
+        steps(2 * parts + b)
+        return (sums[0] + add(d_rows * unit), sums[1] + add(d_rows))
+
+    width = tokens_ref.shape[1]
+    zero = jnp.zeros((1, width), f32)
+    sums = lax.fori_loop(0, parts, norm_back, (zero, zero))
+    lead = small_ref.shape[0] - 2
+
     def small_copy(s):
-        source = small2_ref if s == 0 else work_ref.at[s - 1]
         device = ex.across if s == 0 else {"dp": flip(place, 1 << (s - 1))}
         return pltpu.make_async_remote_copy(
-            src_ref=source,
+            src_ref=work_ref.at[s],
             dst_ref=got_ref.at[s],
             send_sem=small_send.at[s],
             recv_sem=small_recv.at[s],
@@ -823,63 +1062,53 @@
             device_id_type=MESH,
         )
 
-    def small_step(s):
+    work_ref[0, :lead, :] = small2_ref[:lead, :]
+    for j in range(2):
+        work_ref[0, lead + j : lead + j + 1, :] = sums[j]
+    small_copy(0).start()
+    for s in range(bits + 1):
+        steps(3 * parts + s)
         small_copy(s).wait()
-        before = small_ref[...] if s == 0 else work_ref[s - 1]
-        work_ref[s] = before + got_ref[s]
+        if s == 0:
+            work_ref[1, :lead, :] = small_ref[:lead, :] + got_ref[0, :lead, :]
+            work_ref[1, lead:, :] = work_ref[0, lead:, :] + got_ref[0, lead:, :]
+        else:
+            work_ref[s + 1] = work_ref[s] + got_ref[s]
         if s < bits:
             small_copy(s + 1).start()
-        else:
-            sums_ref[...] = work_ref[s]
-
-    def begin(k, _):
-        ex.start_a(k, 0, others_ref)
+    sums_ref[...] = work_ref[bits + 1]
+
+    def drain(i, _):
+        steps(i)
         return 0
 
-    lax.fori_loop(0, count, begin, 0)
-    small_copy(0).start()
-
-    def second(k, _):
-        ex.start_a(k, 1, mine_ref)
-        return 0
-
-    lax.fori_loop(0, count, second, 0)
-
-    def cross(k, _):
-        ex.stage_b(k, others_ref)
-        return 0
-
-    lax.fori_loop(0, count, cross, 0)
-
-    def steps(i, _):
-        at_step(i - 5, count, lambda k: ex.stage_h(k, full_ref))
-        at_step(i - 4, count, lambda k: ex.stage_g(k, full_ref))
-        at_step(i - 3, count, lambda k: ex.stage_f(k, full_ref))
-        at_step(i - 2, count, lambda k: ex.stage_e(k, full_ref))
-        at_step(i - 1, count, lambda k: ex.stage_d(k))
-        at_step(i, count, lambda k: ex.stage_c(k, mine_ref))
-        for s in range(bits + 1):
-            pl.when(i == s + 1)(functools.partial(small_step, s))
-        return 0
-
-    lax.fori_loop(0, count + 6, steps, 0)
-
-
-def sum_chunks(bits, mine, others, small, small2):
-    count, rows, width = mine.shape
-    exchange = Exchange(bits, count, rows, width)
+    lax.fori_loop(3 * parts + bits + 1, 3 * parts + bits + 1 + 15, drain, 0)
+
+
+def leave(bits, mine, crossed, d_fields, weights, tokens, gain, d_mid, small, small2):
+    total = mine[0].shape[0] + mine[1].shape[0]
+    rows, cols = mine[0].shape[1:]
+    exchange = Exchange(bits, total, rows, cols)
+    count, width = tokens.shape
     vmem = pl.BlockSpec(memory_space=pltpu.VMEM)
+    shape = jax.ShapeDtypeStruct
     return pl.pallas_call(
-        functools.partial(sum_kernel, exchange),
-        in_specs=[vmem] * 4,
-        out_specs=[vmem] * 2,
+        functools.partial(leave_kernel, exchange),
+        in_specs=[vmem] * 13,
+        out_specs=[vmem] * 3,
         out_shape=[
-            jax.ShapeDtypeStruct(mine.shape, bf16),
-            jax.ShapeDtypeStruct(small.shape, f32),
+            shape((total, rows, cols), bf16),
+            shape((count, width), f32),
+            shape(small.shape, f32),
         ],
         scratch_shapes=[
+            pltpu.VMEM((total, rows, cols), bf16),
+            pltpu.VMEM((count, width), f32),
+            pltpu.VMEM((HALF + EDGE, width), bf16),
+            pltpu.VMEM((HALF + EDGE, width), bf16),
+            pltpu.SemaphoreType.DMA((2,)),
             pltpu.VMEM((bits + 1,) + small.shape, f32),
-            pltpu.VMEM((bits + 1,) + small.shape, f32),
+            pltpu.VMEM((bits + 2,) + small.shape, f32),
             pltpu.SemaphoreType.DMA((bits + 1,)),
             pltpu.SemaphoreType.DMA((bits + 1,)),
         ]
@@ -887,11 +1116,11 @@
         compiler_params=pltpu.CompilerParams(
             collective_id=1, has_side_effects=True, vmem_limit_bytes=67043328
         ),
-        name="sum_chunks",
+        name="leave",
         cost_estimate=pl.CostEstimate(
             flops=40 * 10**9, bytes_accessed=40 * 10**6, transcendentals=0
         ),
-    )(mine, others, small, small2)
+    )(*mine, *crossed, *d_fields, *weights, tokens, gain, d_mid, small, small2)
 
 
 def key_layout(seq_lengths, block_len, part):
@@ -936,20 +1165,24 @@
     return spans, clean_bounds, noisy_bounds, jnp.cos(angles), jnp.sin(angles) * sign
 
 
-def half_of(array, which):
-    size = array.shape[0] // 2
-    return lax.dynamic_slice_in_dim(array, which * size, size, 0)
-
-
-def in_order(bit, mine, theirs):
-    flip = bit == 0
+def half_of(array, which, axis=0):
+    size = array.shape[axis] // 2
+    return lax.dynamic_slice_in_dim(array, which * size, size, axis)
+
+
+def in_order(bit, mine, theirs, axis=0):
+    order = bit == 0
     return jnp.concatenate(
-        [jnp.where(flip, mine, theirs), jnp.where(flip, theirs, mine)], axis=0
+        [jnp.where(order, mine, theirs), jnp.where(order, theirs, mine)], axis=axis
     )
 
 
 def tie(first, second):
     return lax.optimization_barrier((first, second))
+
+
+def as_row(vector):
+    return vector.reshape(1, -1)
 
 
 def local(
@@ -973,6 +1206,7 @@
     part = lax.axis_index("mp")
     place = lax.axis_index("dp")
     bits = dp_size.bit_length() - 1
+    core = place & 1
 
     def across(array):
         return lax.ppermute(array, "mp", [(0, 1), (1, 0)])
@@ -984,12 +1218,11 @@
         here = across(half)
         return here, sibling(here)
 
-    core = place & 1
     edge = jnp.where(part == 0, tokens[0, HALF - EDGE :], tokens[0, :EDGE])
     context = across(jnp.concatenate([tokens[1], edge], axis=0))
     qkv_mine = w_qkv.transpose(1, 0, 2)
     halves = [
-        half_of(qkv_mine.reshape(-1, w_qkv.shape[2]), core),
+        half_of(qkv_mine, core, 1),
         half_of(w_out, core),
         half_of(w_up, core),
         half_of(w_down, core),
@@ -999,47 +1232,34 @@
     bias_other = across(b_up)
 
     spans, clean_bounds, noisy_bounds, cosine, sine = key_layout(lengths[0], block_size[0], part)
-    clean_other, edge_other = context[:HALF], context[HALF:]
-    key_tokens = jnp.concatenate(
-        [clean_other, tokens[1], clean_other[:EDGE], edge_other, tokens[0], edge_other], axis=0
-    )
-    normed1_keys = layer_norm(key_tokens.astype(f32), ln1_gain, ln1_bias).astype(bf16)
-    normed1_t = normed1_keys.T
-
-    def attention(weights):
-        query, keys, values = project(normed1_keys, weights, cosine, sine)
-        attended, lse = attend_forward(spans, clean_bounds, noisy_bounds, query, keys, values)
-        return (query, keys, values, attended, lse)
-
-    mine = attention(qkv_mine)
+    normed1, normed1_t, *fields = enter(
+        tokens, context, as_row(ln1_gain), as_row(ln1_bias), qkv_mine, cosine, sine
+    )
+    mine = [*fields, *attend_forward(spans, clean_bounds, noisy_bounds, *fields)]
     fetched[0] = tie(fetched[0], mine[3])[0]
-    qkv_other = in_order(core, *fetched[0]).reshape(qkv_mine.shape)
-    other = attention(qkv_other)
+    qkv_other = in_order(core, *fetched[0], axis=1)
+    fields = project(normed1, qkv_other, cosine, sine)
+    other = [*fields, *attend_forward(spans, clean_bounds, noisy_bounds, *fields)]
     fetched[1:] = tie(fetched[1:], other[3])[0]
-    out_other, up_other, down_other = [in_order(core, *pieces) for pieces in fetched[1:]]
-    up_all = jnp.concatenate([up_other, w_up], axis=1)
-    down_all = jnp.concatenate([down_other, w_down], axis=0)
     bias_all = jnp.concatenate([bias_other, b_up]).astype(f32).reshape(-1, 1, HIDDEN_TILE)
 
-    as_row = lambda vector: vector.reshape(1, -1)
-    out, d_mid, d_att, d_att2, grad_out, grad_out2, grad_bias, norms, full = middle(
+    x_rows = tokens.reshape(TOK_DEV, width)
+    out, d_mid, d_att, d_att2, grad_out, grad_out2, grad_bias, norms, grad_down, grad_up = middle(
         bits,
-        tokens.reshape(TOK_DEV, width),
+        x_rows,
         mine[3],
         other[3],
         w_out,
-        out_other,
+        in_order(core, *fetched[1]),
         cotangent.reshape(TOK_DEV, width),
         as_row(ln2_gain),
         as_row(ln2_bias),
         as_row(b_down),
         bias_all,
-        up_all,
-        down_all,
+        (w_up,) + fetched[2],
+        (w_down,) + fetched[3],
     )
     hidden = b_up.shape[0]
-    grad_down = full[:, :, :width].reshape(hidden, width).astype(f32)
-    grad_up = full[:, :, width:].reshape(hidden, width).T.astype(f32)
 
     d_qkv, grad_qkv = [], []
     for saved, d_attended in ((other, d_att2), (mine, d_att)):
@@ -1058,71 +1278,42 @@
             sine,
             normed1_t,
         )
+        spans = tie(spans, grad)[0]
         d_qkv.append(d_fields)
-        grad_qkv.append(grad)
-    pairs = mine[0].shape[1] // LANES
-
-    def by_pair(weights):
-        split = weights.reshape(3, width, pairs, LANES)
-        return split.transpose(2, 1, 0, 3).reshape(pairs, width, 3 * LANES)
-
-    d_normed1_keys = rows_back(d_qkv[1], d_qkv[0], by_pair(qkv_mine), by_pair(qkv_other))
-    clean_back = d_normed1_keys[:HALF]
-    clean_back = clean_back.at[:EDGE].add(d_normed1_keys[2 * HALF : 2 * HALF + EDGE])
-    edge_back = d_normed1_keys[NOISY_BASE:NOISY_OWN] + d_normed1_keys[NOISY_OWN + HALF :]
-    back = across(jnp.concatenate([clean_back, edge_back], axis=0).astype(bf16)).astype(f32)
-    at_end = jnp.concatenate([jnp.zeros((HALF - EDGE, width), f32), back[HALF:]], axis=0)
-    at_start = jnp.concatenate([back[HALF:], jnp.zeros((HALF - EDGE, width), f32)], axis=0)
-    d_normed1 = jnp.concatenate(
-        [
-            d_normed1_keys[NOISY_OWN : NOISY_OWN + HALF]
-            + jnp.where(part == 0, at_end, at_start),
-            d_normed1_keys[CLEAN_OWN : CLEAN_OWN + HALF] + back[:HALF],
-        ],
-        axis=0,
-    )
-    x_rows = tokens.astype(f32).reshape(TOK_DEV, width)
-    norm1_back = jax.vjp(layer_norm, x_rows, ln1_gain, ln1_bias)[1]
-    d_x_norm, grad_ln1_gain, grad_ln1_bias = norm1_back(d_normed1)
-    grad_tokens = (d_mid + d_x_norm).reshape(tokens.shape)
-    shared = jnp.concatenate(
-        [norms[:3], as_row(grad_ln1_gain), as_row(grad_ln1_bias), jnp.zeros((1, width), f32)],
-        axis=0,
-    )
-    bias2, bias1 = grad_bias.reshape(2, hidden // width, width)
-
-    def chunks(of_qkv, of_out):
-        lanes = 3 * LANES
-        flat = jnp.concatenate([of_out[:, :lanes], of_out[:, lanes:]], axis=0)
-        return jnp.concatenate(
-            [of_qkv.reshape(-1, ROW_TILE, lanes), flat.reshape(-1, ROW_TILE, lanes)], axis=0
-        )
-
-    full2, sums = sum_chunks(
+        grad_qkv.append(grad.reshape(-1, ROW_TILE, grad.shape[2]))
+    crossed_out = across(grad_out2)
+    crossed = across(grad_qkv[0])
+    lead = hidden // width
+    bias2, bias1 = grad_bias.reshape(2, lead, width)
+    shared = jnp.concatenate([norms[:3], jnp.zeros((2, width), f32)], axis=0)
+    full, grad_tokens, sums = leave(
         bits,
-        chunks(grad_qkv[1], grad_out),
-        chunks(grad_qkv[0], grad_out2),
+        (grad_qkv[1], grad_out.reshape(-1, ROW_TILE, grad_out.shape[1])),
+        (crossed, crossed_out.reshape(-1, ROW_TILE, grad_out.shape[1])),
+        (d_qkv[1], d_qkv[0]),
+        (qkv_mine, qkv_other),
+        x_rows,
+        as_row(ln1_gain),
+        d_mid,
         jnp.concatenate([bias1, shared], axis=0),
         jnp.concatenate([bias2, shared], axis=0),
     )
-    split = pairs * width // ROW_TILE
-    grad_qkv = full2[:split].reshape(pairs, width, 3, LANES).transpose(1, 2, 0, 3)
-    grad_qkv = grad_qkv.reshape(w_qkv.shape).astype(f32)
-    flat = full2[split:].reshape(2, w_out.shape[0], 3 * LANES)
+    split = 3 * width // ROW_TILE
+    grad_qkv = full[:split].reshape(qkv_mine.shape).transpose(1, 0, 2).astype(f32)
+    flat = full[split:].reshape(2, w_out.shape[0], width // 2)
     grad_out = jnp.concatenate([flat[0], flat[1]], axis=1).astype(f32)
-    lead = hidden // width
     return (
         out.reshape(tokens.shape),
-        grad_tokens,
+        grad_tokens.reshape(tokens.shape),
         sums[lead + 3],
         sums[lead + 4],
         grad_qkv,
         grad_out,
         sums[lead],
         sums[lead + 1],
-        grad_up,
+        grad_up.astype(f32),
         sums[:lead].reshape(hidden),
-        grad_down,
+        grad_down.astype(f32),
         sums[lead + 2],
     )
 

time: 590 us -> 490 us (0.83); the launches traced: 580 us -> 487 us
  local copies, waits for them, and re-layouts: 80.6 us -> 24.5 us
  other arithmetic: 63.6 us -> 26.2 us
  waiting for transfers between devices: 30.3 us -> 66.9 us
  starting transfers between devices: 36.9 us -> 13.7 us
  Pallas kernels: 366 us -> 354 us
    ppermute x7 -> x8, waiting for transfers between devices: 30.3 us -> 66.9 us  [across(): return lax.ppermute(array, 'mp', [(0, 1), (1, 0)])]
    ppermute x7 -> x8, starting transfers between devices: 36.3 us -> 13 us  [across(): return lax.ppermute(array, 'mp', [(0, 1), (1, 0)])]
    convert_element_type x4 -> x0, local copies, waits for them, and re-layouts: 20.4 us -> none  [the longest x2 10 us: local(): grad_qkv = grad_qkv.reshape(w_qkv.shape).astype(f32)]
    concatenate x10 -> x3, other arithmetic: 22 us -> 2.93 us  [the longest x2 2.24 us: in_order(): jnp.concatenate([jnp.where(order, mine, theirs), jnp.where(order, theirs,...]
    pallas_call x4 -> x3, Pallas kernels: 111 us -> 96.7 us  [the longest x1 77.9 us: leave(): pl.pallas_call(functools.partial(leave_kernel, exchange), in_specs=[vmem]...]
    slice x15 -> x3, local copies, waits for them, and re-layouts: 12.4 us -> 2.79 us  [the longest x1 1.66 us: local(): full[:split].reshape(qkv_mine.shape).transpose(1, 0, 2).astype(f32)]
    unnamed x92 -> x26, local copies, waits for them, and re-layouts: 12.5 us -> 4.17 us
  transfers between devices with their start and end apart: 11 -> 12, of which waited for: 2 -> 3; matrix products, arithmetic and copies ran while one was open for 12% -> 7% of each run, Pallas kernels for 12% -> 21%
where the time goes in v4:
time: 490 us; the launch traced here: 487 us
  Pallas kernels  354 us (72%)
  waiting for transfers between devices  66.9 us (14%)
  other arithmetic  26.2 us (5%)
  local copies, waits for them, and re-layouts  24.5 us (5%)
  starting transfers between devices  13.7 us (3%)
    pallas_call x1, Pallas kernels, middle(): pl.pallas_call(functools.partial(middle_kernel, exchange, tiles), in_spec...  135 us
    pallas_call x1, Pallas kernels, leave(): pl.pallas_call(functools.partial(leave_kernel, exchange), in_specs=[vmem]...  77.9 us
    pallas_call x2, Pallas kernels, attend_backward(): pl.pallas_call(backward_kernel, grid_spec=pltpu.PrefetchScalarGridSpec(nu...  75.9 us
    ppermute x8, waiting for transfers between devices, across(): return lax.ppermute(array, 'mp', [(0, 1), (1, 0)])  66.9 us
    pallas_call x2, Pallas kernels, attend_forward(): pl.pallas_call(forward_kernel, grid_spec=pltpu.PrefetchScalarGridSpec(num...  47.2 us
    ppermute x8, starting transfers between devices, across(): return lax.ppermute(array, 'mp', [(0, 1), (1, 0)])  13 us
    pallas_call x1, Pallas kernels, enter(): pl.pallas_call(enter_kernel, in_specs=[vmem] * 7, out_specs=[vmem] * 5, o...  11.4 us
  transfers between devices with their start and end apart: 12, of which 3 were waited for; matrix products, arithmetic and copies ran while one was open for 7% of the time, Pallas kernels for 21%

profile of v4, /device:TPU:0, one launch (start us, length us, event | category | flops | bytes accessed | tf_op | source)
XLA Modules:
  0.0 487.3 jit_solution(2597940332426318120)
XLA Ops:
  0.7 1.2 slice_bitcast_fusion
  1.9 0.8 select_bitcast_fusion
  2.6 0.9 pad_maximum_fusion.1
  3.6 3.0 collective-permute-start
  6.6 0.2 reduce-window.8
  7.4 1.3 dynamic-slice_bitcast_fusion
  8.8 1.4 constant_dynamic-slice_fusion
  10.1 0.1 fusion.2
  10.2 0.1 subtract_convert_fusion
  10.4 0.7 fusion.17
  11.1 0.5 maximum_bitcast_fusion
  11.6 1.3 constant_dynamic-slice_fusion.1
  12.9 12.0 %collective-permute-done.context_ref = bf16[528,768]{1,0:T(8,128)(2,1)} collective-permute-done((bf16[528,768]{1,0:T(8,128)(2,1)}, bf16[528,768]{1,0:T(8,128)(2,1)}, u32[]{:S(2)}, u32[]{:S(2)}) %collective-permute-start) | collective-permute-done | bytes 811040 | tf_op jit(solution)/shard_map/ppermute | solution.py:1212
  24.9 1.7 collective-permute-start.5
  26.7 0.3 collective-permute-start.7
  27.0 0.6 pad_add_fusion.noisy_ref
  27.6 1.3 copy.42
  28.9 0.7 reduce_min.21
  29.6 1.3 copy.38
  30.9 0.7 add_select_fusion.2
  31.6 1.8 collective-permute-start.1
  33.4 1.3 add_add_fusion.clean_ref
  34.7 4.4 fusion
  39.1 0.6 pad_add_fusion.1.span_ref
  39.7 0.7 concatenate.61
  40.4 1.3 reshape.402.gain_ref.refs_9_
  41.7 1.3 reshape.403.shift_ref
  43.0 1.3 reshape.405.refs_6_
  44.2 1.3 reshape.406.refs_7_
  45.5 1.3 reshape.407.refs_8_
  46.8 0.6 pad.7.clone
  47.3 0.7 concatenate.60
  48.0 0.6 maximum_convert_fusion.1.refs_9_
  48.6 0.3 collective-permute-start.3
  49.0 49.3 %collective-permute-done.1 = bf16[3,384,384]{2,1,0:T(8,128)(2,1)} collective-permute-done((bf16[3,384,384]{2,1,0:T(8,128)(2,1)S(1)}, bf16[3,384,384]{2,1,0:T(8,128)(2,1)}, u32[]{:S(2)}, u32[]{:S(2)}) %collective-permute-start.1) | collective-permute-done | bytes 884768 | tf_op jit(solution)/shard_map/ppermute | solution.py:1212
  98.2 0.5 collective-permute-start.6
  98.8 11.4 %enter.1 = (bf16[1584,768]{1,0:T(8,128)(2,1)}, bf16[768,1584]{1,0:T(8,128)(2,1)}, bf16[1584,384]{1,0:T(8,128)(2,1)}, bf16[1584,384]{1,0:T(8,128)(2,1)}, bf16[1584,384]{1,0:T(8,128)(2,1)}) custom-call(bf16[2,512,768]{2,1,0:T(8,128)(2,1)} %tokens_ref.1, bf16[528,768]{1,0:T(8,128)(2,1)} %collective-permute-done.context_ref, ...), custom_call_target="tpu_custom_call" | custom-call | flops 10000000000 | bytes 16000000 | tf_op jit(solution)/shard_map/enter/pallas_call | solution.py:157
  110.2 23.6 %attend_forward.2 = (bf16[1024,384]{1,0:T(8,128)(2,1)}, f32[3,4,2,256]{3,2,1,0:T(2,128)}) custom-call(s32[4,2]{1,0:T(4,128)} %pad_add_fusion.1.span_ref, s32[4,2,256]{2,1,0:T(2,128)} %add_add_fusion.clean_ref, s32[4,2,128]{2,1,0:T(2,128)} %pad_add_fusion.noisy_ref, bf16[1584,384]{1,0:T(8,128)(2,1)} %get-tuple-element.56.q_ref, ...), custom_call_target="tpu_custom_call" | custom-call | flops 1610612736 | bytes 4866048 | tf_op jit(solution)/shard_map/attend_forward/pallas_call | solution.py:253
  133.8 0.1 collective-permute-start.4
  133.9 1.3 broadcast_select_fusion.1
  135.2 1.4 pad_maximum_fusion.w_ref.refs_7_
  136.6 7.3 %project.1 = (bf16[1584,384]{1,0:T(8,128)(2,1)}, bf16[1584,384]{1,0:T(8,128)(2,1)}, bf16[1584,384]{1,0:T(8,128)(2,1)}) custom-call(bf16[1584,768]{1,0:T(8,128)(2,1)} %get-tuple-element.60.rows_ref, bf16[3,768,384]{2,1,0:T(8,128)(2,1)} %pad_maximum_fusion.w_ref.refs_7_, f32[1584,128]{1,0:T(8,128)} %get-tuple-element.122.cos_ref, ...), custom_call_target="tpu_custom_call" | custom-call | flops 2802843648 | bytes 7852032 | tf_op jit(solution)/shard_map/project/pallas_call | solution.py:78
  144.0 23.6 %attend_forward.3 = (bf16[1024,384]{1,0:T(8,128)(2,1)}, f32[3,4,2,256]{3,2,1,0:T(2,128)}) custom-call(s32[4,2]{1,0:T(4,128)} %pad_add_fusion.1.span_ref, s32[4,2,256]{2,1,0:T(2,128)} %add_add_fusion.clean_ref, s32[4,2,128]{2,1,0:T(2,128)} %pad_add_fusion.noisy_ref, bf16[1584,384]{1,0:T(8,128)(2,1)} %get-tuple-element.64.q_ref, ...), custom_call_target="tpu_custom_call" | custom-call | flops 1610612736 | bytes 4866048 | tf_op jit(solution)/shard_map/attend_forward/pallas_call | solution.py:253
  167.6 1.2 broadcast_select_fusion.3
  168.8 0.9 pad_maximum_fusion.2.refs_4_
  169.7 134.7 %middle.1 = (bf16[1024,768]{1,0:T(8,128)(2,1)}, f32[1024,768]{1,0:T(8,128)}, bf16[1024,384]{1,0:T(8,128)(2,1)}, bf16[1024,384]{1,0:T(8,128)(2,1)}, bf16[768,384]...) custom-call(bf16[1024,768]{1,0:T(8,128)(2,1)} %bitcast.43, ...), custom_call_target="tpu_custom_call" | custom-call | flops 60000002048 | bytes 40000000 | tf_op jit(solution)/shard_map/middle/pallas_call | solution.py:890
  304.4 38.0 %attend_backward.2 = (bf16[3,1584,384]{2,1,0:T(8,128)(2,1)}, bf16[3,768,384]{2,1,0:T(8,128)(2,1)}) custom-call(s32[4,2]{1,0:T(4,128)} %pad_add_fusion.1.span_ref, s32[4,2,256]{2,1,0:T(2,128)} %add_add_fusion.clean_ref, s32[4,2,128]{2,1,0:T(2,128)} %pad_add_fusion.noisy_ref, bf16[1584,384]{1,0:T(8,128)(2,1)} %get-tuple-element.64.q_ref, ...), custom_call_target="tpu_custom_call" | custom-call | flops 35999997952 | bytes 36000000 | tf_op jit(solution)/shard_map/attend_backward/pallas_call | solution.py:412
  342.4 5.8 %collective-permute-start.10 = (bf16[9,256,384]{2,1,0:T(8,128)(2,1)}, bf16[9,256,384]{2,1,0:T(8,128)(2,1)}, u32[]{:S(2)}, u32[]{:S(2)}) collective-permute-start(bf16[9,256,384]{2,1,0:T(8,128)(2,1)} %bitcast.55), channel_id=1, source_target_pairs={{0,1},{1,0},{2,3},{3,2},{4,5},{5,4},{6,7},{7,6},{8,9},{9,8},{10,11... | collective-permute-start | bytes 5308424 | tf_op jit(solution)/shard_map/ppermute | solution.py:1212
  348.2 0.1 collective-permute-start.11
  348.3 37.9 %attend_backward.3 = (bf16[3,1584,384]{2,1,0:T(8,128)(2,1)}, bf16[3,768,384]{2,1,0:T(8,128)(2,1)}) custom-call(s32[4,2]{1,0:T(4,128)} %pad_add_fusion.1.span_ref, s32[4,2,256]{2,1,0:T(2,128)} %add_add_fusion.clean_ref, s32[4,2,128]{2,1,0:T(2,128)} %pad_add_fusion.noisy_ref, bf16[1584,384]{1,0:T(8,128)(2,1)} %get-tuple-element.56.q_ref, ...), custom_call_target="tpu_custom_call" | custom-call | flops 35999997952 | bytes 36000000 | tf_op jit(solution)/shard_map/attend_backward/pallas_call | solution.py:412
  386.3 2.8 convert_element_type.49
  389.1 2.5 convert_element_type.50
  391.7 0.7 fusion.4
  392.3 5.6 %collective-permute-done.11 = bf16[768,384]{1,0:T(8,128)(2,1)} collective-permute-done((bf16[768,384]{1,0:T(8,128)(2,1)S(1)}, bf16[768,384]{1,0:T(8,128)(2,1)}, u32[]{:S(2)}, u32[]{:S(2)}) %collective-permute-start.11) | collective-permute-done | bytes 589856 | tf_op jit(solution)/shard_map/ppermute | solution.py:1212
  398.0 77.9 %leave.1 = (bf16[12,256,384]{2,1,0:T(8,128)(2,1)}, f32[1024,768]{1,0:T(8,128)}, f32[7,768]{1,0:T(8,128)}) custom-call(bf16[9,256,384]{2,1,0:T(8,128)(2,1)} %bitcast.57, bf16[3,256,384]{2,1,0:T(8,128)(2,1)} %bitcast.58, bf16[9,256,384]{2,1,0:T(8,128)(2,1)} %collective-permute-done.10.refs_2_, bf16[3,256,384]{2,1,0:T(8,128)(2,1)} %bitcast.19.refs_3_, ...), custom_call_target="tpu_custom_call" | custom-call | flops 40000000000 | bytes 40000000 | tf_op jit(solution)/shard_map/leave/pallas_call | solution.py:1095
  475.9 1.7 slice.68
  477.6 1.1 slice.69
  478.7 0.6 slice_reduce_fusion.2
  479.4 2.0 convert_bitcast_fusion
  481.4 0.6 reshape.415
  482.0 1.1 maximum_convert_fusion
  483.1 1.1 copy.48
  484.3 1.3 copy-done
  485.6 1.7 copy.49
  (48 shorter events, 0.4 us)
Async XLA Ops:
  0.6 5.9 %copy-start.9 = (s32[1,4]{1,0:T(1,128)S(1)}, s32[1,4]{1,0:T(1,128)}, u32[]{:S(2)}) copy-start(s32[1,4]{1,0:T(1,128)} %param.15) | copy-start | bytes 52
  3.6 21.4 %collective-permute-start = (bf16[528,768]{1,0:T(8,128)(2,1)}, bf16[528,768]{1,0:T(8,128)(2,1)}, u32[]{:S(2)}, u32[]{:S(2)}) collective-permute-start(bf16[528,768]{1,0:T(8,128)(2,1)} %pad_maximum_fusion.1), channel_id=1, source_target_pairs={{0,1},{1,0},{2,3},{3,2},{4,5},{5,4},{6,7},{7,6},{8,9},{9,8},{10,11... | collective-permute-start | bytes 2433032 | tf_op jit(solution)/shard_map/ppermute | solution.py:1212
  6.5 40.8 %collective-permute-start.9 = (bf16[1536]{0:T(1024)(128)(2,1)}, bf16[1536]{0:T(1024)(128)(2,1)}, u32[]{:S(2)}, u32[]{:S(2)}) collective-permute-start(bf16[1536]{0:T(1024)(128)(2,1)} %param.25), channel_id=1, source_target_pairs={{0,1},{1,0},{2,3},{3,2},{4,5},{5,4},{6,7},{7,6},{8,9},{9,8},{10,11... | collective-permute-start | bytes 9224 | tf_op jit(solution)/shard_map/ppermute | solution.py:1212
  7.4 3.6 copy-start.4
  24.9 73.3 %collective-permute-start.5 = (bf16[384,1536]{1,0:T(8,128)(2,1)S(1)}, bf16[384,1536]{1,0:T(8,128)(2,1)}, u32[]{:S(2)}, u32[]{:S(2)}) collective-permute-start(bf16[384,1536]{1,0:T(8,128)(2,1)S(1)} %constant_dynamic-slice_fusion.1), channel_id=1, source_target_pairs={{0,1},{1,0},{2,3},{3,2},{4,5},{5,4},{6,7},{7,6},{8,9},{9,8},{10,11... | collective-permute-start | bytes 3538952 | tf_op jit(solution)/shard_map/ppermute | solution.py:1212
  26.7 72.0 %collective-permute-start.7 = (bf16[768,768]{1,0:T(8,128)(2,1)S(1)}, bf16[768,768]{1,0:T(8,128)(2,1)}, u32[]{:S(2)}, u32[]{:S(2)}) collective-permute-start(bf16[768,768]{1,0:T(8,128)(2,1)S(1)} %constant_dynamic-slice_fusion), channel_id=1, source_target_pairs={{0,1},{1,0},{2,3},{3,2},{4,5},{5,4},{6,7},{7,6},{8,9},{9,8},{10,11... | collective-permute-start | bytes 3538952 | tf_op jit(solution)/shard_map/ppermute | solution.py:1212
  31.6 66.6 %collective-permute-start.1 = (bf16[3,384,384]{2,1,0:T(8,128)(2,1)S(1)}, bf16[3,384,384]{2,1,0:T(8,128)(2,1)}, u32[]{:S(2)}, u32[]{:S(2)}) collective-permute-start(bf16[3,384,384]{2,1,0:T(8,128)(2,1)S(1)} %dynamic-slice_bitcast_fusion), channel_id=1, source_target_pairs={{0,1},{1,0},{2,3},{3,2},{4,5},{5,4},{6,7},{7,6},{8,9},{9,8},{10,11... | collective-permute-start | bytes 2654216 | tf_op jit(solution)/shard_map/ppermute | solution.py:1212
  48.6 85.2 %collective-permute-start.3 = (bf16[192,768]{1,0:T(8,128)(2,1)S(1)}, bf16[192,768]{1,0:T(8,128)(2,1)}, u32[]{:S(2)}, u32[]{:S(2)}) collective-permute-start(bf16[192,768]{1,0:T(8,128)(2,1)S(1)} %constant_dynamic-slice_fusion.2), channel_id=1, source_target_pairs={{0,1},{1,0},{2,3},{3,2},{4,5},{5,4},{6,7},{7,6},{8,9},{9,8},{10,11... | collective-permute-start | bytes 884744 | tf_op jit(solution)/shard_map/ppermute | solution.py:1212
  98.2 35.7 %collective-permute-start.2 = (bf16[3,384,384]{2,1,0:T(8,128)(2,1)}, bf16[3,384,384]{2,1,0:T(8,128)(2,1)S(1)}, u32[]{:S(2)}, u32[]{:S(2)}) collective-permute-start(bf16[3,384,384]{2,1,0:T(8,128)(2,1)} %collective-permute-done.1), channel_id=1, source_target_pairs={{0,2},{2,0},{4,6},{6,4},{8,10},{10,8},{12,14},{14,12},{16,18},{18,... | collective-permute-start | bytes 2654216 | tf_op jit(solution)/shard_map/ppermute | solution.py:1215
  98.2 69.3 %collective-permute-start.6 = (bf16[384,1536]{1,0:T(8,128)(2,1)}, bf16[384,1536]{1,0:T(8,128)(2,1)S(1)}, u32[]{:S(2)}, u32[]{:S(2)}) collective-permute-start(bf16[384,1536]{1,0:T(8,128)(2,1)} %collective-permute-done.5.refs_11_), channel_id=1, source_target_pairs={{0,2},{2,0},{4,6},{6,4},{8,10},{10,8},{12,14},{14,12},{16,18},{18,... | collective-permute-start | bytes 3538952 | tf_op jit(solution)/shard_map/ppermute | solution.py:1215
  98.7 68.8 %collective-permute-start.8 = (bf16[768,768]{1,0:T(8,128)(2,1)}, bf16[768,768]{1,0:T(8,128)(2,1)}, u32[]{:S(2)}, u32[]{:S(2)}) collective-permute-start(bf16[768,768]{1,0:T(8,128)(2,1)} %collective-permute-done.7.refs_14_), channel_id=1, source_target_pairs={{0,2},{2,0},{4,6},{6,4},{8,10},{10,8},{12,14},{14,12},{16,18},{18,... | collective-permute-start | bytes 3538952 | tf_op jit(solution)/shard_map/ppermute | solution.py:1215
  133.8 33.7 %collective-permute-start.4 = (bf16[192,768]{1,0:T(8,128)(2,1)}, bf16[192,768]{1,0:T(8,128)(2,1)S(1)}, u32[]{:S(2)}, u32[]{:S(2)}) collective-permute-start(bf16[192,768]{1,0:T(8,128)(2,1)} %collective-permute-done.3), channel_id=1, source_target_pairs={{0,2},{2,0},{4,6},{6,4},{8,10},{10,8},{12,14},{14,12},{16,18},{18,... | collective-permute-start | bytes 884744 | tf_op jit(solution)/shard_map/ppermute | solution.py:1215
  167.6 2.1 copy-start.10
  304.4 43.8 %copy-start.11 = (bf16[768,384]{1,0:T(8,128)(2,1)S(1)}, bf16[768,384]{1,0:T(8,128)(2,1)}, u32[]{:S(2)}) copy-start(bf16[768,384]{1,0:T(8,128)(2,1)} %get-tuple-element.87) | copy-start | bytes 1769476
  342.4 55.6 %collective-permute-start.10 = (bf16[9,256,384]{2,1,0:T(8,128)(2,1)}, bf16[9,256,384]{2,1,0:T(8,128)(2,1)}, u32[]{:S(2)}, u32[]{:S(2)}) collective-permute-start(bf16[9,256,384]{2,1,0:T(8,128)(2,1)} %bitcast.55), channel_id=1, source_target_pairs={{0,1},{1,0},{2,3},{3,2},{4,5},{5,4},{6,7},{7,6},{8,9},{9,8},{10,11... | collective-permute-start | bytes 5308424 | tf_op jit(solution)/shard_map/ppermute | solution.py:1212
  348.2 49.8 %collective-permute-start.11 = (bf16[768,384]{1,0:T(8,128)(2,1)S(1)}, bf16[768,384]{1,0:T(8,128)(2,1)}, u32[]{:S(2)}, u32[]{:S(2)}) collective-permute-start(bf16[768,384]{1,0:T(8,128)(2,1)S(1)} %copy-done.11), channel_id=1, source_target_pairs={{0,1},{1,0},{2,3},{3,2},{4,5},{5,4},{6,7},{7,6},{8,9},{9,8},{10,11... | collective-permute-start | bytes 1769480 | tf_op jit(solution)/shard_map/ppermute | solution.py:1212
  348.3 37.9 %copy-start.7 = (f32[8,768]{1,0:T(8,128)S(1)}, f32[8,768]{1,0:T(8,128)}, u32[]{:S(2)}) copy-start(f32[8,768]{1,0:T(8,128)} %get-tuple-element.92) | copy-start | bytes 73732
  348.3 37.9 %copy-start.6 = (f32[12,1,256]{2,1,0:T(1,128)S(1)}, f32[12,1,256]{2,1,0:T(1,128)}, u32[]{:S(2)}) copy-start(f32[12,1,256]{2,1,0:T(1,128)} %get-tuple-element.91) | copy-start | bytes 36868
  348.3 38.0 %copy-start.2 = (bf16[768,1536]{1,0:T(8,128)(2,1)S(1)}, bf16[768,1536]{1,0:T(8,128)(2,1)}, u32[]{:S(2)}) copy-start(bf16[768,1536]{1,0:T(8,128)(2,1)} %get-tuple-element.96) | copy-start | bytes 7077892
  386.3 2.8 copy-start.1
  389.1 2.5 copy-start.8
  475.9 2.8 copy-start.5
  481.4 1.8 copy-start.3
  483.1 2.5 copy-start

commit v5 on v4

--- a/solution.py
+++ b/solution.py
@@ -106,8 +106,7 @@
 def enter_kernel(
     tokens_ref,
     context_ref,
-    gain_ref,
-    shift_ref,
+    vectors_ref,
     w_ref,
     cos_ref,
     sin_ref,
@@ -118,7 +117,8 @@
     v_ref,
 ):
     def norm(values):
-        return (normal(values.astype(f32))[0] * gain_ref[...] + shift_ref[...]).astype(bf16)
+        unit = normal(values.astype(f32))[0]
+        return (unit * vectors_ref[0:1, :] + vectors_ref[1:2, :]).astype(bf16)
 
     def blocks(i, _):
         source = pl.ds(pl.multiple_of(i * TILE, TILE), TILE)
@@ -149,21 +149,21 @@
         rows_t_ref[cols, :] = rows_ref[:, cols].T
 
 
-def enter(tokens, context, gain, shift, weights, cosine, sine):
+def enter(tokens, context, vectors, weights, cosine, sine):
     width, cols = weights.shape[1:]
     vmem = pl.BlockSpec(memory_space=pltpu.VMEM)
     shape = jax.ShapeDtypeStruct
     field = shape((KEY_ROWS, cols), bf16)
     return pl.pallas_call(
         enter_kernel,
-        in_specs=[vmem] * 7,
+        in_specs=[vmem] * 6,
         out_specs=[vmem] * 5,
         out_shape=[shape((KEY_ROWS, width), bf16), shape((width, KEY_ROWS), bf16)] + [field] * 3,
         name="enter",
         cost_estimate=pl.CostEstimate(
             flops=10**10, bytes_accessed=16 * 10**6, transcendentals=0
         ),
-    )(tokens, context, gain, shift, weights, cosine, sine)
+    )(tokens, context, vectors, weights, cosine, sine)
 
 
 def split_heads(rows):
@@ -654,16 +654,12 @@
         wout_ref,
         wout2_ref,
         dy_ref,
-        gain_ref,
-        shift_ref,
-        bdown_ref,
+        vectors_ref,
         bup_ref,
         up_mine,
         up_here,
-        up_there,
         down_mine,
         down_here,
-        down_there,
         out_ref,
         mid_ref,
         datt_ref,
@@ -675,6 +671,10 @@
         gdown_ref,
         gup_ref,
         full_ref,
+        up_there,
+        down_there,
+        pass_up,
+        pass_down,
         up_buf,
         down_buf,
         load_sem,
@@ -708,8 +708,40 @@
         target = up_buf.at[slot, h * lanes : (h + 1) * lanes]
         return pltpu.make_async_copy(up_source, target, sems.at[h])
 
+    def hand_up(k):
+        cols = pl.ds(pl.multiple_of(k * HIDDEN_TILE, HIDDEN_TILE), HIDDEN_TILE)
+        return pltpu.make_async_remote_copy(
+            src_ref=up_here.at[:, cols],
+            dst_ref=up_there.at[k],
+            send_sem=pass_up.at[k, 0],
+            recv_sem=pass_up.at[k, 1],
+            device_id=ex.sibling,
+            device_id_type=MESH,
+        )
+
+    def hand_down(k):
+        rows = pl.ds(pl.multiple_of(k * HIDDEN_TILE, HIDDEN_TILE), HIDDEN_TILE)
+        return pltpu.make_async_remote_copy(
+            src_ref=down_here.at[rows, :],
+            dst_ref=down_there.at[k],
+            send_sem=pass_down.at[k, 0],
+            recv_sem=pass_down.at[k, 1],
+            device_id=ex.sibling,
+            device_id_type=MESH,
+        )
+
     def start_loads(i):
         other, k = which(i)
+        held = k // (count // 2) == core
+
+        @pl.when(other)
+        def _():
+            hand_up(k).wait()
+
+        @pl.when(jnp.logical_and(other, jnp.logical_not(held)))
+        def _():
+            hand_down(k % (count // 2)).wait()
+
         cols = pl.ds(pl.multiple_of(k * HIDDEN_TILE, HIDDEN_TILE), HIDDEN_TILE)
         inner = k % (count // 2)
         rows = pl.ds(pl.multiple_of(inner * HIDDEN_TILE, HIDDEN_TILE), HIDDEN_TILE)
@@ -726,31 +758,42 @@
         for h in range(2):
             put(mine, up_mine.at[h * lanes : (h + 1) * lanes, cols], h)
             put(jnp.logical_and(other, core == h), up_here.at[:, cols], h)
-            put(jnp.logical_and(other, core != h), up_there.at[:, cols], h)
-        held = k // (count // 2) == core
+            put(jnp.logical_and(other, core != h), up_there.at[k], h)
         put(mine, down_mine.at[cols, :], None)
         put(jnp.logical_and(other, held), down_here.at[rows, :], None)
-        put(jnp.logical_and(other, jnp.logical_not(held)), down_there.at[rows, :], None)
+        put(jnp.logical_and(other, jnp.logical_not(held)), down_there.at[inner], None)
 
     def wait_loads(i):
         for h in range(2):
             load(i, up_mine.at[:lanes, :HIDDEN_TILE], None, h).wait()
         load(i, None, down_mine.at[:HIDDEN_TILE, :], None).wait()
 
-    start_loads(0)
     ex.greet()
+
+    def hand(k, _):
+        hand_up(k).start()
+
+        @pl.when(k < count // 2)
+        def _():
+            hand_down(k).start()
+
+        return 0
+
+    lax.fori_loop(0, count, hand, 0)
 
     def prologue(r, _):
         rows = pl.ds(pl.multiple_of(r * ROW_TILE, ROW_TILE), ROW_TILE)
         branch = dot(att_ref[rows, :], wout_ref[...]) + dot(att2_ref[rows, :], wout2_ref[...])
         mid = x_ref[rows, :].astype(f32) + branch
         mid_ref[rows, :] = mid
-        n2_ref[rows, :] = (normal(mid)[0] * gain_ref[...] + shift_ref[...]).astype(bf16)
-        total_ref[rows, :] = mid + bdown_ref[...]
+        unit = normal(mid)[0]
+        n2_ref[rows, :] = (unit * vectors_ref[2:3, :] + vectors_ref[3:4, :]).astype(bf16)
+        total_ref[rows, :] = mid + vectors_ref[4:5, :]
         dn2_ref[rows, :] = jnp.zeros((ROW_TILE, width), f32)
         return 0
 
     lax.fori_loop(0, blocks, prologue, 0)
+    start_loads(0)
 
     def tile(i):
         other, k = which(i)
@@ -805,24 +848,24 @@
         def _():
             lax.fori_loop(0, SPLIT, lambda c, _: (action(k * SPLIT + c), 0)[1], 0)
 
-    def arrive(k):
-        for c in range(SPLIT):
-            ex.stage_h(k * SPLIT + c, full_ref)
+    def arrive(c):
+        ex.stage_h(c, full_ref)
+        k, lane = c // SPLIT, c % SPLIT
         hidden = pl.ds(pl.multiple_of(k * HIDDEN_TILE, HIDDEN_TILE), HIDDEN_TILE)
-        for c in range(2):
-            cols = slice(c * lanes, (c + 1) * lanes)
-            gdown_ref[hidden, cols] = full_ref[k * SPLIT + c]
-            gup_ref[cols, hidden] = full_ref[k * SPLIT + 2 + c].T
+        cols = pl.ds(pl.multiple_of(lane % 2 * lanes, LANES), lanes)
+
+        @pl.when(lane < 2)
+        def _():
+            gdown_ref[hidden, cols] = full_ref[c]
+
+        @pl.when(lane >= 2)
+        def _():
+            gup_ref[cols, hidden] = full_ref[c].T
 
     def steps(i):
         even = i % 2 == 0
         odd = jnp.logical_not(even)
-        last = (i - 9) // 2
-
-        @pl.when(jnp.logical_and(odd, jnp.logical_and(last >= 0, last < count)))
-        def _():
-            arrive(last)
-
+        group((i - 9) // 2, odd, arrive)
         group((i - 8) // 2, even, lambda k: ex.stage_g(k, full_ref))
         group((i - 7) // 2, odd, lambda k: ex.stage_f(k, full_ref))
         group((i - 6) // 2, even, lambda k: ex.stage_e(k, full_ref))
@@ -831,6 +874,26 @@
         crossing = jnp.logical_or(i == 1, jnp.logical_and(even, i >= 2))
         group(i // 2, crossing, lambda k: ex.stage_b(k, grad_ref))
 
+    def tick(d):
+        total = count * SPLIT
+
+        def due(c, least, action):
+            @pl.when(jnp.logical_and(c >= least, c < total))
+            def _():
+                action(c)
+
+        done = [
+            (tiles + 1 - lag) // 2 * SPLIT if lag % 2 == 0 else (tiles - lag + 1) // 2 * SPLIT
+            for lag in (9, 8, 7, 6, 5, 4)
+        ]
+        first = done[5]
+        due(first - 10 + d, done[0], arrive)
+        due(first - 8 + d, done[1], lambda c: ex.stage_g(c, full_ref))
+        due(first - 6 + d, done[2], lambda c: ex.stage_f(c, full_ref))
+        due(first - 4 + d, done[3], lambda c: ex.stage_e(c, full_ref))
+        due(first - 2 + d, done[4], lambda c: ex.stage_d(c))
+        due(first + d, done[5], lambda c: ex.stage_c(c, grad_ref))
+
     def main(i, _):
         tile(i)
         steps(i)
@@ -844,7 +907,7 @@
         unit, scale = normal(mid_ref[rows, :])
         d_rows = dn2_ref[rows, :]
         dy = dy_ref[rows, :].astype(f32)
-        lean = d_rows * gain_ref[...]
+        lean = d_rows * vectors_ref[2:3, :]
         d_mid = dy + scale * (
             lean
             - jnp.mean(lean, axis=-1, keepdims=True)
@@ -857,7 +920,8 @@
         datt2_ref[rows, :] = dot(d_branch, wout2_ref[...], NT).astype(bf16)
         add = lambda values: jnp.sum(values, axis=0, keepdims=True)
         sums = (sums[0] + add(d_rows * unit), sums[1] + add(d_rows), sums[2] + add(dy))
-        steps(tiles + r)
+        tick(2 * r)
+        tick(2 * r + 1)
         return sums
 
     zero = jnp.zeros((1, width), f32)
@@ -870,14 +934,14 @@
         target[:depth, :] = grad[:, :lanes]
         target[depth:, :] = grad[:, lanes:]
 
-    def drain(i, _):
-        steps(i)
+    def drain(d, _):
+        tick(d)
         return 0
 
-    lax.fori_loop(tiles + blocks, 2 * count + 8, drain, 0)
-
-
-def middle(bits, x, att, att2, wout, wout2, dy, gain, shift, bdown, bup, ups, downs):
+    lax.fori_loop(2 * blocks, 2 * SPLIT + 10, drain, 0)
+
+
+def middle(bits, x, att, att2, wout, wout2, dy, vectors, bup, ups, downs):
     rows, width = x.shape
     hidden = ups[0].shape[1]
     count = hidden // HIDDEN_TILE
@@ -889,7 +953,7 @@
     depth = wout.shape[0]
     return pl.pallas_call(
         functools.partial(middle_kernel, exchange, tiles),
-        in_specs=[vmem] * 10 + [hbm] * 6,
+        in_specs=[vmem] * 8 + [hbm] * 4,
         out_specs=[vmem] * 10,
         out_shape=[
             shape((rows, width), bf16),
@@ -905,6 +969,10 @@
         ],
         scratch_shapes=[
             pltpu.VMEM((count * SPLIT, HIDDEN_TILE, width // 2), bf16),
+            pltpu.VMEM((count, width // 2, HIDDEN_TILE), bf16),
+            pltpu.VMEM((count // 2, HIDDEN_TILE, width), bf16),
+            pltpu.SemaphoreType.DMA((count, 2)),
+            pltpu.SemaphoreType.DMA((count // 2, 2)),
             pltpu.VMEM((2, width, HIDDEN_TILE), bf16),
             pltpu.VMEM((2, HIDDEN_TILE, width), bf16),
             pltpu.SemaphoreType.DMA((2, 3)),
@@ -923,7 +991,7 @@
         cost_estimate=pl.CostEstimate(
             flops=60 * 10**9, bytes_accessed=40 * 10**6, transcendentals=4 * 10**6
         ),
-    )(x, att, att2, wout, wout2, dy, gain, shift, bdown, bup, *ups, *downs)
+    )(x, att, att2, wout, wout2, dy, vectors, bup, *ups, *downs)
 
 
 def leave_kernel(exchange, *refs):
@@ -937,7 +1005,7 @@
         w_ref,
         w2_ref,
         tokens_ref,
-        gain_ref,
+        vectors_ref,
         dmid_ref,
         small_ref,
         small2_ref,
@@ -949,16 +1017,21 @@
         give_ref,
         take_ref,
         swap_sem,
-        got_ref,
-        work_ref,
-        small_send,
-        small_recv,
+        near_ref,
+        far_ref,
+        near_sem,
+        far_sem,
         *rest,
     ) = refs
     place, part = lax.axis_index("dp"), lax.axis_index("mp")
     ex = exchange.bind(place, part, rest)
     count, bits = ex.count, ex.bits
     first = mine_ref.shape[0]
+    near_id = part * 4 + place % 4
+    near = [
+        {"dp": flip(place, j % 4), "mp": part if j < 4 else 1 - part} for j in range(1, 8)
+    ]
+    ex.partners += [near[j - 1] for j in (3, 5, 6, 7)]
     ex.greet()
 
     def begin(k, _):
@@ -984,17 +1057,26 @@
                 total = total + dot(grads[c, rows, :], weights[c], NT)
         return total
 
-    for r in range(HALF // ROW_TILE):
-        rows = slice(r * ROW_TILE, (r + 1) * ROW_TILE)
-        given = back_of(rows)
-        if r == 0:
-            edges = back_of(slice(2 * HALF, NOISY_OWN))
-            give_ref[EDGE:ROW_TILE, :] = given[EDGE:].astype(bf16)
-            give_ref[:EDGE, :] = (given[:EDGE] + edges[:EDGE]).astype(bf16)
-            last = back_of(slice(NOISY_OWN + HALF, KEY_ROWS))
-            give_ref[HALF:, :] = (edges[EDGE:] + last).astype(bf16)
-        else:
-            give_ref[rows, :] = given.astype(bf16)
+    def steps(i):
+        at_step(i - 10, count, lambda k: ex.stage_h(k, full_ref))
+        at_step(i - 8, count, lambda k: ex.stage_g(k, full_ref))
+        at_step(i - 6, count, lambda k: ex.stage_f(k, full_ref))
+        at_step(i - 4, count, lambda k: ex.stage_e(k, full_ref))
+        at_step(i - 2, count, lambda k: ex.stage_d(k))
+        at_step(i, count, lambda k: ex.stage_c(k, sum_buf, False))
+
+    def many(low, high):
+        lax.fori_loop(low, high, lambda i, _: (steps(i), 0)[1], 0)
+
+    tail = back_of(slice(2 * HALF, KEY_ROWS))
+    own = NOISY_OWN - 2 * HALF
+    rows_ref[:HALF, :] = tail[own : own + HALF]
+    give_ref[HALF:, :] = (tail[EDGE:own] + tail[own + HALF :]).astype(bf16)
+    rows_ref[HALF : HALF + EDGE, :] = tail[:EDGE]
+    many(0, 3)
+    given = back_of(slice(0, HALF))
+    give_ref[EDGE:HALF, :] = given[EDGE:].astype(bf16)
+    give_ref[:EDGE, :] = (given[:EDGE] + rows_ref[HALF : HALF + EDGE, :]).astype(bf16)
     swap = pltpu.make_async_remote_copy(
         src_ref=give_ref,
         dst_ref=take_ref,
@@ -1004,88 +1086,118 @@
         device_id_type=MESH,
     )
     swap.start()
-
-    def steps(i):
-        at_step(i - 15, count, lambda k: ex.stage_h(k, full_ref))
-        at_step(i - 12, count, lambda k: ex.stage_g(k, full_ref))
-        at_step(i - 9, count, lambda k: ex.stage_f(k, full_ref))
-        at_step(i - 6, count, lambda k: ex.stage_e(k, full_ref))
-        at_step(i - 3, count, lambda k: ex.stage_d(k))
-        at_step(i, count, lambda k: ex.stage_c(k, sum_buf, False))
-
-    parts = 2 * TILES
-
-    def own_rows(b, _):
-        noisy = NOISY_OWN + b * TILE
-        clean = CLEAN_OWN + (b - TILES) * TILE
-        start = jnp.where(b < TILES, noisy, clean)
-        rows_ref[pl.ds(pl.multiple_of(b * TILE, TILE), TILE), :] = back_of(
-            pl.ds(pl.multiple_of(start, EDGE), TILE)
-        )
-        steps(2 * b)
-        steps(2 * b + 1)
-        return 0
-
-    lax.fori_loop(0, parts, own_rows, 0)
+    many(3, 6)
+    rows_ref[HALF:, :] = back_of(slice(CLEAN_OWN, CLEAN_OWN + HALF))
+    many(6, 10)
     swap.wait()
     rows_ref[HALF:, :] += take_ref[:HALF, :].astype(f32)
     edge = pl.ds(pl.multiple_of((1 - part) * (HALF - EDGE), EDGE), EDGE)
     rows_ref[edge, :] += take_ref[HALF:, :].astype(f32)
 
     def norm_back(b, sums):
-        rows = pl.ds(pl.multiple_of(b * TILE, TILE), TILE)
+        rows = pl.ds(pl.multiple_of(b * ROW_TILE, TILE), ROW_TILE)
         unit, scale = normal(tokens_ref[rows, :].astype(f32))
         d_rows = rows_ref[rows, :]
-        lean = d_rows * gain_ref[...]
+        lean = d_rows * vectors_ref[0:1, :]
         back_ref[rows, :] = dmid_ref[rows, :] + scale * (
             lean
             - jnp.mean(lean, axis=-1, keepdims=True)
             - unit * jnp.mean(lean * unit, axis=-1, keepdims=True)
         )
         add = lambda values: jnp.sum(values, axis=0, keepdims=True)
-        steps(2 * parts + b)
+        steps(10 + b)
         return (sums[0] + add(d_rows * unit), sums[1] + add(d_rows))
 
     width = tokens_ref.shape[1]
+    parts = tokens_ref.shape[0] // ROW_TILE
     zero = jnp.zeros((1, width), f32)
     sums = lax.fori_loop(0, parts, norm_back, (zero, zero))
     lead = small_ref.shape[0] - 2
-
-    def small_copy(s):
-        device = ex.across if s == 0 else {"dp": flip(place, 1 << (s - 1))}
+    bias = lead - 3
+    mine = near_ref.at[near_id]
+    mine[:lead, :] = small_ref[:lead, :]
+    for j in range(2):
+        mine[lead + j : lead + j + 1, :] = sums[j]
+    mine[lead + 2 : lead + 2 + bias, :] = small2_ref[:bias, :]
+    rest_rows = 16 - lead - 2 - bias
+    mine[16 - rest_rows :, :] = jnp.zeros((rest_rows, width), f32)
+
+    def near_copy(j):
         return pltpu.make_async_remote_copy(
-            src_ref=work_ref.at[s],
-            dst_ref=got_ref.at[s],
-            send_sem=small_send.at[s],
-            recv_sem=small_recv.at[s],
-            device_id=device,
+            src_ref=near_ref.at[near_id],
+            dst_ref=near_ref.at[near_id],
+            send_sem=near_sem.at[j, 0],
+            recv_sem=near_sem.at[j, 1],
+            device_id=near[j - 1],
             device_id_type=MESH,
         )
 
-    work_ref[0, :lead, :] = small2_ref[:lead, :]
-    for j in range(2):
-        work_ref[0, lead + j : lead + j + 1, :] = sums[j]
-    small_copy(0).start()
-    for s in range(bits + 1):
-        steps(3 * parts + s)
-        small_copy(s).wait()
-        if s == 0:
-            work_ref[1, :lead, :] = small_ref[:lead, :] + got_ref[0, :lead, :]
-            work_ref[1, lead:, :] = work_ref[0, lead:, :] + got_ref[0, lead:, :]
-        else:
-            work_ref[s + 1] = work_ref[s] + got_ref[s]
-        if s < bits:
-            small_copy(s + 1).start()
-    sums_ref[...] = work_ref[bits + 1]
-
-    def drain(i, _):
-        steps(i)
-        return 0
-
-    lax.fori_loop(3 * parts + bits + 1, 3 * parts + bits + 1 + 15, drain, 0)
-
-
-def leave(bits, mine, crossed, d_fields, weights, tokens, gain, d_mid, small, small2):
+    def near_got(j):
+        came = (part + j // 4) % 2 * 4 + flip(place % 4, j % 4)
+        return pltpu.make_async_remote_copy(
+            src_ref=near_ref.at[came],
+            dst_ref=near_ref.at[came],
+            send_sem=near_sem.at[j, 0],
+            recv_sem=near_sem.at[j, 1],
+            device_id=near[j - 1],
+            device_id_type=MESH,
+        )
+
+    for j in range(1, 8):
+        near_copy(j).start()
+    many(10 + parts, 13 + parts)
+    for j in range(1, 8):
+        near_copy(j).wait_send()
+        near_got(j).wait_recv()
+    total = near_ref[0]
+    for j in range(1, 8):
+        total = total + near_ref[j]
+    plane = near_ref[part * 4]
+    other = near_ref[(1 - part) * 4]
+    for j in range(1, 4):
+        plane = plane + near_ref[part * 4 + j]
+        other = other + near_ref[(1 - part) * 4 + j]
+    spot = far_ref.at[ex.z]
+    spot[...] = total
+    spot[:bias, :] = plane[:bias] + other[lead + 2 : lead + 2 + bias]
+
+    def far_copy(j, at):
+        return pltpu.make_async_remote_copy(
+            src_ref=far_ref.at[at],
+            dst_ref=far_ref.at[at],
+            send_sem=far_sem.at[j, 0],
+            recv_sem=far_sem.at[j, 1],
+            device_id=ex.peers[j - 1],
+            device_id_type=MESH,
+        )
+
+    for j in range(1, 4):
+        far_copy(j, ex.z).start()
+    many(13 + parts, 16 + parts)
+    for j in range(1, 4):
+        far_copy(j, ex.z).wait_send()
+        far_copy(j, flip(ex.z, j)).wait_recv()
+    total = far_ref[0]
+    for j in range(1, 4):
+        total = total + far_ref[j]
+    for i, b in enumerate(ex.extra):
+        far_ref[4 + 2 * i] = total
+        trade = pltpu.make_async_remote_copy(
+            src_ref=far_ref.at[4 + 2 * i],
+            dst_ref=far_ref.at[5 + 2 * i],
+            send_sem=far_sem.at[4 + i, 0],
+            recv_sem=far_sem.at[4 + i, 1],
+            device_id={"dp": flip(place, 1 << b)},
+            device_id_type=MESH,
+        )
+        trade.start()
+        trade.wait()
+        total = total + far_ref[5 + 2 * i]
+    sums_ref[...] = total
+    many(16 + parts, count + 10)
+
+
+def leave(bits, mine, crossed, d_fields, weights, tokens, vectors, d_mid, small, small2):
     total = mine[0].shape[0] + mine[1].shape[0]
     rows, cols = mine[0].shape[1:]
     exchange = Exchange(bits, total, rows, cols)
@@ -1099,7 +1211,7 @@
         out_shape=[
             shape((total, rows, cols), bf16),
             shape((count, width), f32),
-            shape(small.shape, f32),
+            shape((16, width), f32),
         ],
         scratch_shapes=[
             pltpu.VMEM((total, rows, cols), bf16),
@@ -1107,10 +1219,10 @@
             pltpu.VMEM((HALF + EDGE, width), bf16),
             pltpu.VMEM((HALF + EDGE, width), bf16),
             pltpu.SemaphoreType.DMA((2,)),
-            pltpu.VMEM((bits + 1,) + small.shape, f32),
-            pltpu.VMEM((bits + 2,) + small.shape, f32),
-            pltpu.SemaphoreType.DMA((bits + 1,)),
-            pltpu.SemaphoreType.DMA((bits + 1,)),
+            pltpu.VMEM((8, 16, width), f32),
+            pltpu.VMEM((4 + 2 * len(exchange.extra), 16, width), f32),
+            pltpu.SemaphoreType.DMA((8, 2)),
+            pltpu.SemaphoreType.DMA((4 + len(exchange.extra), 2)),
         ]
         + exchange.scratch(),
         compiler_params=pltpu.CompilerParams(
@@ -1120,7 +1232,7 @@
         cost_estimate=pl.CostEstimate(
             flops=40 * 10**9, bytes_accessed=40 * 10**6, transcendentals=0
         ),
-    )(*mine, *crossed, *d_fields, *weights, tokens, gain, d_mid, small, small2)
+    )(*mine, *crossed, *d_fields, *weights, tokens, vectors, d_mid, small, small2)
 
 
 def key_layout(seq_lengths, block_len, part):
@@ -1181,10 +1293,6 @@
     return lax.optimization_barrier((first, second))
 
 
-def as_row(vector):
-    return vector.reshape(1, -1)
-
-
 def local(
     dp_size,
     tokens,
@@ -1214,10 +1322,6 @@
     def sibling(array):
         return lax.ppermute(array, "dp", [(i, i ^ 1) for i in range(dp_size)])
 
-    def fetch(half):
-        here = across(half)
-        return here, sibling(here)
-
     edge = jnp.where(part == 0, tokens[0, HALF - EDGE :], tokens[0, :EDGE])
     context = across(jnp.concatenate([tokens[1], edge], axis=0))
     qkv_mine = w_qkv.transpose(1, 0, 2)
@@ -1227,20 +1331,23 @@
         half_of(w_up, core),
         half_of(w_down, core),
     ]
-    context, halves = tie(context, halves)
-    fetched = [fetch(half) for half in halves]
+    layout = key_layout(lengths[0], block_size[0], part)
+    vectors = jnp.stack([ln1_gain, ln1_bias, ln2_gain, ln2_bias, b_down])
+    context, (halves, layout, vectors) = tie(context, (halves, layout, vectors))
+    qkv_here, out_here, up_here, down_here = [across(half) for half in halves]
     bias_other = across(b_up)
 
-    spans, clean_bounds, noisy_bounds, cosine, sine = key_layout(lengths[0], block_size[0], part)
-    normed1, normed1_t, *fields = enter(
-        tokens, context, as_row(ln1_gain), as_row(ln1_bias), qkv_mine, cosine, sine
-    )
+    spans, clean_bounds, noisy_bounds, cosine, sine = layout
+    normed1, normed1_t, *fields = enter(tokens, context, vectors, qkv_mine, cosine, sine)
     mine = [*fields, *attend_forward(spans, clean_bounds, noisy_bounds, *fields)]
-    fetched[0] = tie(fetched[0], mine[3])[0]
-    qkv_other = in_order(core, *fetched[0], axis=1)
+    (qkv_here, out_here), _ = tie((qkv_here, out_here), mine[3])
+    qkv_other = in_order(core, qkv_here, sibling(qkv_here), axis=1)
+    out_there = sibling(out_here)
     fields = project(normed1, qkv_other, cosine, sine)
     other = [*fields, *attend_forward(spans, clean_bounds, noisy_bounds, *fields)]
-    fetched[1:] = tie(fetched[1:], other[3])[0]
+    (out_here, out_there, up_here, down_here, bias_other), _ = tie(
+        (out_here, out_there, up_here, down_here, bias_other), other[3]
+    )
     bias_all = jnp.concatenate([bias_other, b_up]).astype(f32).reshape(-1, 1, HIDDEN_TILE)
 
     x_rows = tokens.reshape(TOK_DEV, width)
@@ -1250,14 +1357,12 @@
         mine[3],
         other[3],
         w_out,
-        in_order(core, *fetched[1]),
+        in_order(core, out_here, out_there),
         cotangent.reshape(TOK_DEV, width),
-        as_row(ln2_gain),
-        as_row(ln2_bias),
-        as_row(b_down),
+        vectors,
         bias_all,
-        (w_up,) + fetched[2],
-        (w_down,) + fetched[3],
+        (w_up, up_here),
+        (w_down, down_here),
     )
     hidden = b_up.shape[0]
 
@@ -1293,7 +1398,7 @@
         (d_qkv[1], d_qkv[0]),
         (qkv_mine, qkv_other),
         x_rows,
-        as_row(ln1_gain),
+        vectors,
         d_mid,
         jnp.concatenate([bias1, shared], axis=0),
         jnp.concatenate([bias2, shared], axis=0),

time: 490 us -> 428 us (0.87); the launches traced: 487 us -> 431 us
  waiting for transfers between devices: 66.9 us -> 22.3 us
  Pallas kernels: 354 us -> 339 us
  starting transfers between devices: 13.7 us -> 28 us
  local copies, waits for them, and re-layouts: 24.5 us -> 16.7 us
    ppermute x8, waiting for transfers between devices: 66.9 us -> 22.3 us  [across(): return lax.ppermute(array, 'mp', [(0, 1), (1, 0)])]
    pallas_call x1, Pallas kernels: 135 us -> 112 us  [middle(): pl.pallas_call(functools.partial(middle_kernel, exchange, tiles), in_spec...]
    ppermute x8, starting transfers between devices: 13 us -> 28 us  [across(): return lax.ppermute(array, 'mp', [(0, 1), (1, 0)])]
    pallas_call x1, Pallas kernels: 77.9 us -> 85.1 us  [leave(): pl.pallas_call(functools.partial(leave_kernel, exchange), in_specs=[vmem]...]
    reshape x5 -> x0, local copies, waits for them, and re-layouts: 6.35 us -> none  [as_row(): return vector.reshape(1, -1)]
  transfers between devices with their start and end apart: 12 -> 10, of which waited for: 3 -> 3; matrix products, arithmetic and copies ran while one was open for 7% -> 5% of each run, Pallas kernels for 21% -> 24%
where the time goes in v5:
time: 428 us; the launch traced here: 431 us
  Pallas kernels  339 us (79%)
  starting transfers between devices  28 us (7%)
  other arithmetic  23.3 us (5%)
  waiting for transfers between devices  22.3 us (5%)
  local copies, waits for them, and re-layouts  16.7 us (4%)
    pallas_call x1, Pallas kernels, middle(): pl.pallas_call(functools.partial(middle_kernel, exchange, tiles), in_spec...  112 us
    pallas_call x1, Pallas kernels, leave(): pl.pallas_call(functools.partial(leave_kernel, exchange), in_specs=[vmem]...  85.1 us
    pallas_call x2, Pallas kernels, attend_backward(): pl.pallas_call(backward_kernel, grid_spec=pltpu.PrefetchScalarGridSpec(nu...  75.9 us
    pallas_call x2, Pallas kernels, attend_forward(): pl.pallas_call(forward_kernel, grid_spec=pltpu.PrefetchScalarGridSpec(num...  47.3 us
    ppermute x8, starting transfers between devices, across(): return lax.ppermute(array, 'mp', [(0, 1), (1, 0)])  28 us
    ppermute x8, waiting for transfers between devices, across(): return lax.ppermute(array, 'mp', [(0, 1), (1, 0)])  22.3 us
    pallas_call x1, Pallas kernels, enter(): pl.pallas_call(enter_kernel, in_specs=[vmem] * 6, out_specs=[vmem] * 5, o...  11.4 us
  transfers between devices with their start and end apart: 10, of which 3 were waited for; matrix products, arithmetic and copies ran while one was open for 5% of the time, Pallas kernels for 24%

profile of v5, /device:TPU:0, one launch (start us, length us, event | category | flops | bytes accessed | tf_op | source)
XLA Modules:
  0.0 430.6 jit_solution(2290564951374432895)
XLA Ops:
  0.7 1.2 slice_bitcast_fusion
  1.9 0.8 select_bitcast_fusion
  2.6 0.9 pad_maximum_fusion.1
  3.6 3.0 collective-permute-start
  6.5 0.2 reduce-window.8
  7.4 0.1 fusion.2
  7.5 0.1 subtract_convert_fusion
  7.7 0.3 fusion.17
  7.9 0.1 copy.42
  8.0 0.2 reduce_min.21
  8.2 0.1 copy.38
  8.3 1.3 dynamic-slice_bitcast_fusion
  9.6 0.0 copy-start.7
  9.6 0.0 copy-start.8
  9.6 0.0 copy-start.9
  9.6 0.0 copy-start.10
  9.6 0.0 copy-start.11
  9.7 1.4 constant_dynamic-slice_fusion
  11.0 0.7 pad_add_fusion.1.span_ref
  11.7 0.6 add_add_fusion.clean_ref
  12.3 0.6 pad_add_fusion.noisy_ref
  13.0 0.6 stack.29.vectors_ref.refs_6_.refs_9_
  13.6 1.3 constant_dynamic-slice_fusion.1
  15.0 4.4 %fusion = (f32[1584,128]{1,0:T(8,128)}, f32[1584,128]{1,0:T(8,128)}) fusion(f32[128]{0:T(128)S(1)} %get-tuple-element.139, f32[128]{0:T(128)S(1)} %get-tuple-element.140, f32[1584]{0:T(1024)S(1)} %get-tuple-element.133), kind=kLoop, calls=%fused_computation.7 | loop fusion | flops 405504 | bytes 1629376 | tf_op jit(solution)/shard_map/mul | solution.py:1277
  19.4 5.5 %collective-permute-done.context_ref = bf16[528,768]{1,0:T(8,128)(2,1)} collective-permute-done((bf16[528,768]{1,0:T(8,128)(2,1)}, bf16[528,768]{1,0:T(8,128)(2,1)}, u32[]{:S(2)}, u32[]{:S(2)}) %collective-permute-start) | collective-permute-done | bytes 811040 | tf_op jit(solution)/shard_map/ppermute | solution.py:1320
  24.9 1.7 collective-permute-start.1
  26.7 0.3 collective-permute-start.2
  26.9 11.4 %enter.1 = (bf16[1584,768]{1,0:T(8,128)(2,1)}, bf16[768,1584]{1,0:T(8,128)(2,1)}, bf16[1584,384]{1,0:T(8,128)(2,1)}, bf16[1584,384]{1,0:T(8,128)(2,1)}, bf16[1584,384]{1,0:T(8,128)(2,1)}) custom-call(bf16[2,512,768]{2,1,0:T(8,128)(2,1)} %tokens_ref.1, bf16[528,768]{1,0:T(8,128)(2,1)} %collective-permute-done.context_ref, ...), custom_call_target="tpu_custom_call" | custom-call | flops 10000000000 | bytes 16000000 | tf_op jit(solution)/shard_map/enter/pallas_call | solution.py:157
  38.3 23.7 %attend_forward.2 = (bf16[1024,384]{1,0:T(8,128)(2,1)}, f32[3,4,2,256]{3,2,1,0:T(2,128)}) custom-call(s32[4,2]{1,0:T(4,128)} %pad_add_fusion.1.span_ref, s32[4,2,256]{2,1,0:T(2,128)} %add_add_fusion.clean_ref, s32[4,2,128]{2,1,0:T(2,128)} %pad_add_fusion.noisy_ref, bf16[1584,384]{1,0:T(8,128)(2,1)} %get-tuple-element.67.q_ref, ...), custom_call_target="tpu_custom_call" | custom-call | flops 1610612736 | bytes 4866048 | tf_op jit(solution)/shard_map/attend_forward/pallas_call | solution.py:253
  62.0 0.0 collective-permute-done.2
  62.0 0.1 collective-permute-start.3
  62.1 13.0 %collective-permute-start.5 = (bf16[384,1536]{1,0:T(8,128)(2,1)S(1)}, bf16[384,1536]{1,0:T(8,128)(2,1)}, u32[]{:S(2)}, u32[]{:S(2)}) collective-permute-start(bf16[384,1536]{1,0:T(8,128)(2,1)S(1)} %constant_dynamic-slice_fusion.1), channel_id=1, source_target_pairs={{0,1},{1,0},{2,3},{3,2},{4,5},{5,4},{6,7},{7,6},{8,9},{9,8},{10,11... | collective-permute-start | bytes 3538952 | tf_op jit(solution)/shard_map/ppermute | solution.py:1320
  75.1 0.0 collective-permute-start.6
  75.1 2.0 collective-permute-start.7
  77.2 0.6 pad.7.clone
  77.7 1.3 broadcast_select_fusion.1
  79.1 1.4 pad_maximum_fusion.w_ref.refs_7_
  80.5 7.4 %project.1 = (bf16[1584,384]{1,0:T(8,128)(2,1)}, bf16[1584,384]{1,0:T(8,128)(2,1)}, bf16[1584,384]{1,0:T(8,128)(2,1)}) custom-call(bf16[1584,768]{1,0:T(8,128)(2,1)} %get-tuple-element.71.rows_ref, bf16[3,768,384]{2,1,0:T(8,128)(2,1)} %pad_maximum_fusion.w_ref.refs_7_, f32[1584,128]{1,0:T(8,128)} %get-tuple-element.65.cos_ref, ...), custom_call_target="tpu_custom_call" | custom-call | flops 2802843648 | bytes 7852032 | tf_op jit(solution)/shard_map/project/pallas_call | solution.py:78
  87.8 23.6 %attend_forward.3 = (bf16[1024,384]{1,0:T(8,128)(2,1)}, f32[3,4,2,256]{3,2,1,0:T(2,128)}) custom-call(s32[4,2]{1,0:T(4,128)} %pad_add_fusion.1.span_ref, s32[4,2,256]{2,1,0:T(2,128)} %add_add_fusion.clean_ref, s32[4,2,128]{2,1,0:T(2,128)} %pad_add_fusion.noisy_ref, bf16[1584,384]{1,0:T(8,128)(2,1)} %get-tuple-element.75.q_ref, ...), custom_call_target="tpu_custom_call" | custom-call | flops 1610612736 | bytes 4866048 | tf_op jit(solution)/shard_map/attend_forward/pallas_call | solution.py:253
  111.4 15.3 %collective-permute-done.7 = bf16[1536]{0:T(1024)(128)(2,1)S(1)} collective-permute-done((bf16[1536]{0:T(1024)(128)(2,1)S(1)}, bf16[1536]{0:T(1024)(128)(2,1)S(1)}, u32[]{:S(2)}, u32[]{:S(2)}) %collective-permute-start.7) | collective-permute-done | bytes 3104 | tf_op jit(solution)/shard_map/ppermute | solution.py:1320
  126.8 1.0 broadcast_select_fusion.3
  127.8 0.9 pad_maximum_fusion.2.refs_4_
  128.6 0.6 maximum_convert_fusion.1.refs_7_
  129.2 111.7 %middle.1 = (bf16[1024,768]{1,0:T(8,128)(2,1)}, f32[1024,768]{1,0:T(8,128)}, bf16[1024,384]{1,0:T(8,128)(2,1)}, bf16[1024,384]{1,0:T(8,128)(2,1)}, bf16[768,384]...) custom-call(bf16[1024,768]{1,0:T(8,128)(2,1)} %bitcast.43, ...), custom_call_target="tpu_custom_call" | custom-call | flops 60000002048 | bytes 40000000 | tf_op jit(solution)/shard_map/middle/pallas_call | solution.py:954
  240.9 38.0 %attend_backward.2 = (bf16[3,1584,384]{2,1,0:T(8,128)(2,1)}, bf16[3,768,384]{2,1,0:T(8,128)(2,1)}) custom-call(s32[4,2]{1,0:T(4,128)} %pad_add_fusion.1.span_ref, s32[4,2,256]{2,1,0:T(2,128)} %add_add_fusion.clean_ref, s32[4,2,128]{2,1,0:T(2,128)} %pad_add_fusion.noisy_ref, bf16[1584,384]{1,0:T(8,128)(2,1)} %get-tuple-element.75.q_ref, ...), custom_call_target="tpu_custom_call" | custom-call | flops 35999997952 | bytes 36000000 | tf_op jit(solution)/shard_map/attend_backward/pallas_call | solution.py:412
  279.0 7.9 %collective-permute-start.8 = (bf16[9,256,384]{2,1,0:T(8,128)(2,1)}, bf16[9,256,384]{2,1,0:T(8,128)(2,1)}, u32[]{:S(2)}, u32[]{:S(2)}) collective-permute-start(bf16[9,256,384]{2,1,0:T(8,128)(2,1)} %bitcast.55), channel_id=1, source_target_pairs={{0,1},{1,0},{2,3},{3,2},{4,5},{5,4},{6,7},{7,6},{8,9},{9,8},{10,11... | collective-permute-start | bytes 5308424 | tf_op jit(solution)/shard_map/ppermute | solution.py:1320
  286.9 0.1 collective-permute-start.9
  286.9 37.9 %attend_backward.3 = (bf16[3,1584,384]{2,1,0:T(8,128)(2,1)}, bf16[3,768,384]{2,1,0:T(8,128)(2,1)}) custom-call(s32[4,2]{1,0:T(4,128)} %pad_add_fusion.1.span_ref, s32[4,2,256]{2,1,0:T(2,128)} %add_add_fusion.clean_ref, s32[4,2,128]{2,1,0:T(2,128)} %pad_add_fusion.noisy_ref, bf16[1584,384]{1,0:T(8,128)(2,1)} %get-tuple-element.67.q_ref, ...), custom_call_target="tpu_custom_call" | custom-call | flops 35999997952 | bytes 36000000 | tf_op jit(solution)/shard_map/attend_backward/pallas_call | solution.py:412
  325.0 2.8 convert_element_type.49
  327.8 2.5 convert_element_type.50
  330.4 0.7 fusion.4
  331.0 1.4 collective-permute-done.9
  332.5 85.1 %leave.1 = (bf16[12,256,384]{2,1,0:T(8,128)(2,1)}, f32[1024,768]{1,0:T(8,128)}, f32[16,768]{1,0:T(8,128)}) custom-call(bf16[9,256,384]{2,1,0:T(8,128)(2,1)} %bitcast.57, bf16[3,256,384]{2,1,0:T(8,128)(2,1)} %bitcast.58, bf16[9,256,384]{2,1,0:T(8,128)(2,1)} %collective-permute-done.8.refs_2_, bf16[3,256,384]{2,1,0:T(8,128)(2,1)} %bitcast.19.refs_3_, ...), custom_call_target="tpu_custom_call" | custom-call | flops 40000000000 | bytes 40000000 | tf_op jit(solution)/shard_map/leave/pallas_call | solution.py:1207
  417.6 1.7 slice.68
  419.2 1.1 slice.69
  420.4 1.6 slice_reduce_fusion.2
  421.9 0.7 slice.74
  422.7 2.0 convert_bitcast_fusion
  424.7 0.1 slice_bitcast_fusion.2
  424.8 0.6 reshape.394
  425.4 1.1 maximum_convert_fusion
  426.5 1.1 copy.48
  427.6 1.3 copy-done
  428.9 1.7 copy.49
  (53 shorter events, 0.3 us)
Async XLA Ops:
  0.6 5.9 %copy-start.14 = (s32[1,4]{1,0:T(1,128)S(1)}, s32[1,4]{1,0:T(1,128)}, u32[]{:S(2)}) copy-start(s32[1,4]{1,0:T(1,128)} %param.15) | copy-start | bytes 52
  2.6 7.0 %copy-start.4 = (bf16[384,768]{1,0:T(8,128)(2,1)S(1)}, bf16[384,768]{1,0:T(8,128)(2,1)}, u32[]{:S(2)}) copy-start(bf16[384,768]{1,0:T(8,128)(2,1)} %refs_3_.1) | copy-start | bytes 1769476
  3.6 21.3 %collective-permute-start = (bf16[528,768]{1,0:T(8,128)(2,1)}, bf16[528,768]{1,0:T(8,128)(2,1)}, u32[]{:S(2)}, u32[]{:S(2)}) collective-permute-start(bf16[528,768]{1,0:T(8,128)(2,1)} %pad_maximum_fusion.1), channel_id=1, source_target_pairs={{0,1},{1,0},{2,3},{3,2},{4,5},{5,4},{6,7},{7,6},{8,9},{9,8},{10,11... | collective-permute-start | bytes 2433032 | tf_op jit(solution)/shard_map/ppermute | solution.py:1320
  9.6 3.4 copy-start.7
  9.6 3.4 copy-start.8
  9.6 3.4 copy-start.9
  9.6 3.4 copy-start.10
  9.6 3.4 copy-start.11
  24.9 37.1 %collective-permute-start.1 = (bf16[3,384,384]{2,1,0:T(8,128)(2,1)S(1)}, bf16[3,384,384]{2,1,0:T(8,128)(2,1)}, u32[]{:S(2)}, u32[]{:S(2)}) collective-permute-start(bf16[3,384,384]{2,1,0:T(8,128)(2,1)S(1)} %dynamic-slice_bitcast_fusion), channel_id=1, source_target_pairs={{0,1},{1,0},{2,3},{3,2},{4,5},{5,4},{6,7},{7,6},{8,9},{9,8},{10,11... | collective-permute-start | bytes 2654216 | tf_op jit(solution)/shard_map/ppermute | solution.py:1320
  26.7 35.4 %collective-permute-start.2 = (bf16[192,768]{1,0:T(8,128)(2,1)S(1)}, bf16[192,768]{1,0:T(8,128)(2,1)}, u32[]{:S(2)}, u32[]{:S(2)}) collective-permute-start(bf16[192,768]{1,0:T(8,128)(2,1)S(1)} %constant_dynamic-slice_fusion.2), channel_id=1, source_target_pairs={{0,1},{1,0},{2,3},{3,2},{4,5},{5,4},{6,7},{7,6},{8,9},{9,8},{10,11... | collective-permute-start | bytes 884744 | tf_op jit(solution)/shard_map/ppermute | solution.py:1320
  38.3 36.8 %copy-start.12 = (bf16[1536]{0:T(1024)(128)(2,1)S(1)}, bf16[1536]{0:T(1024)(128)(2,1)}, u32[]{:S(2)}) copy-start(bf16[1536]{0:T(1024)(128)(2,1)} %param.25) | copy-start | bytes 9220
  62.0 15.7 %collective-permute-start.3 = (bf16[3,384,384]{2,1,0:T(8,128)(2,1)}, bf16[3,384,384]{2,1,0:T(8,128)(2,1)S(1)}, u32[]{:S(2)}, u32[]{:S(2)}) collective-permute-start(bf16[3,384,384]{2,1,0:T(8,128)(2,1)} %collective-permute-done.1), channel_id=1, source_target_pairs={{0,2},{2,0},{4,6},{6,4},{8,10},{10,8},{12,14},{14,12},{16,18},{18,... | collective-permute-start | bytes 2654216 | tf_op jit(solution)/shard_map/ppermute | solution.py:1323
  62.1 64.6 %collective-permute-start.5 = (bf16[384,1536]{1,0:T(8,128)(2,1)S(1)}, bf16[384,1536]{1,0:T(8,128)(2,1)}, u32[]{:S(2)}, u32[]{:S(2)}) collective-permute-start(bf16[384,1536]{1,0:T(8,128)(2,1)S(1)} %constant_dynamic-slice_fusion.1), channel_id=1, source_target_pairs={{0,1},{1,0},{2,3},{3,2},{4,5},{5,4},{6,7},{7,6},{8,9},{9,8},{10,11... | collective-permute-start | bytes 3538952 | tf_op jit(solution)/shard_map/ppermute | solution.py:1320
  75.1 51.6 %collective-permute-start.6 = (bf16[768,768]{1,0:T(8,128)(2,1)S(1)}, bf16[768,768]{1,0:T(8,128)(2,1)}, u32[]{:S(2)}, u32[]{:S(2)}) collective-permute-start(bf16[768,768]{1,0:T(8,128)(2,1)S(1)} %constant_dynamic-slice_fusion), channel_id=1, source_target_pairs={{0,1},{1,0},{2,3},{3,2},{4,5},{5,4},{6,7},{7,6},{8,9},{9,8},{10,11... | collective-permute-start | bytes 3538952 | tf_op jit(solution)/shard_map/ppermute | solution.py:1320
  75.1 51.6 %collective-permute-start.7 = (bf16[1536]{0:T(1024)(128)(2,1)S(1)}, bf16[1536]{0:T(1024)(128)(2,1)S(1)}, u32[]{:S(2)}, u32[]{:S(2)}) collective-permute-start(bf16[1536]{0:T(1024)(128)(2,1)S(1)} %copy-done.12), channel_id=1, source_target_pairs={{0,1},{1,0},{2,3},{3,2},{4,5},{5,4},{6,7},{7,6},{8,9},{9,8},{10,11... | collective-permute-start | bytes 9224 | tf_op jit(solution)/shard_map/ppermute | solution.py:1320
  77.7 49.0 %collective-permute-start.4 = (bf16[192,768]{1,0:T(8,128)(2,1)}, bf16[192,768]{1,0:T(8,128)(2,1)S(1)}, u32[]{:S(2)}, u32[]{:S(2)}) collective-permute-start(bf16[192,768]{1,0:T(8,128)(2,1)} %collective-permute-done.2), channel_id=1, source_target_pairs={{0,2},{2,0},{4,6},{6,4},{8,10},{10,8},{12,14},{14,12},{16,18},{18,... | collective-permute-start | bytes 884744 | tf_op jit(solution)/shard_map/ppermute | solution.py:1323
  240.9 45.9 %copy-start.15 = (bf16[768,384]{1,0:T(8,128)(2,1)S(1)}, bf16[768,384]{1,0:T(8,128)(2,1)}, u32[]{:S(2)}) copy-start(bf16[768,384]{1,0:T(8,128)(2,1)} %get-tuple-element.97) | copy-start | bytes 1769476
  279.0 53.5 %collective-permute-start.8 = (bf16[9,256,384]{2,1,0:T(8,128)(2,1)}, bf16[9,256,384]{2,1,0:T(8,128)(2,1)}, u32[]{:S(2)}, u32[]{:S(2)}) collective-permute-start(bf16[9,256,384]{2,1,0:T(8,128)(2,1)} %bitcast.55), channel_id=1, source_target_pairs={{0,1},{1,0},{2,3},{3,2},{4,5},{5,4},{6,7},{7,6},{8,9},{9,8},{10,11... | collective-permute-start | bytes 5308424 | tf_op jit(solution)/shard_map/ppermute | solution.py:1320
  286.9 45.6 %collective-permute-start.9 = (bf16[768,384]{1,0:T(8,128)(2,1)S(1)}, bf16[768,384]{1,0:T(8,128)(2,1)}, u32[]{:S(2)}, u32[]{:S(2)}) collective-permute-start(bf16[768,384]{1,0:T(8,128)(2,1)S(1)} %copy-done.15), channel_id=1, source_target_pairs={{0,1},{1,0},{2,3},{3,2},{4,5},{5,4},{6,7},{7,6},{8,9},{9,8},{10,11... | collective-permute-start | bytes 1769480 | tf_op jit(solution)/shard_map/ppermute | solution.py:1320
  286.9 37.9 %copy-start.6 = (f32[8,768]{1,0:T(8,128)S(1)}, f32[8,768]{1,0:T(8,128)}, u32[]{:S(2)}) copy-start(f32[8,768]{1,0:T(8,128)} %get-tuple-element.102) | copy-start | bytes 73732
  286.9 37.9 %copy-start.5 = (f32[12,1,256]{2,1,0:T(1,128)S(1)}, f32[12,1,256]{2,1,0:T(1,128)}, u32[]{:S(2)}) copy-start(f32[12,1,256]{2,1,0:T(1,128)} %get-tuple-element.101) | copy-start | bytes 36868
  286.9 38.0 %copy-start.2 = (bf16[768,1536]{1,0:T(8,128)(2,1)S(1)}, bf16[768,1536]{1,0:T(8,128)(2,1)}, u32[]{:S(2)}) copy-start(bf16[768,1536]{1,0:T(8,128)(2,1)} %get-tuple-element.106) | copy-start | bytes 7077892
  325.0 2.8 copy-start.1
  327.8 2.5 copy-start.13
  424.7 1.8 copy-start.3
  426.5 2.5 copy-start
